TPU v7x, 32 devices: a whole 2x2x4 slice. The times are simulated.
32 devices in a mesh: dp: 16 (over z, y, core), pos: 2 (over x).
Axes of the slice: x: 2, y: 2, z: 4, core: 2. Of those that a mesh axis runs over, the one named last changes fastest.
Arguments:
- inputs: bfloat16 [32, 512, 512], P('dp', 'pos'), may hold values from -6 to 6
- pre_act: bfloat16 [32, 512, 512], P('dp', 'pos'), may hold values from -6 to 6
- grad_out: bfloat16 [32, 512, 512], P('dp', 'pos'), may hold values from -6 to 6
- weight: bfloat16 [512, 9, 512], P(('dp', 'pos')), may hold values from -0.09375 to 0.09375
Outputs:
- grad_input: bfloat16 [32, 512, 512], P('dp', 'pos')
- grad_weight: float32 [512, 9, 512], P(('dp', 'pos'))
All inputs are finite; a program needn't handle non-finite values.
Results may differ from a plain program's by a relative error of at most 0.005.
Values may be sent and summed in bfloat16 or wider, within the bound.
No kernel may reach another device: no remote copies, remote signals or barrier semaphores. Data moves between devices by JAX's collectives and lax.ppermute only.
A program may use at most 128 MiB of HBM per device.

v0:
```python
import functools
import math

import jax
import jax.numpy as jnp
from jax import lax
from jax.experimental import pallas as pl
from jax.experimental.pallas import tpu as pltpu
from jax.sharding import PartitionSpec as P


AXES = ("dp", "pos")
F32 = jnp.float32
BF16 = jnp.bfloat16
NT = (((1,), (1,)), ((), ()))


def gelu_slope(values):
    cdf = 0.5 * (1.0 + lax.erf(values * 0.7071067811865476))
    return cdf + values * jnp.exp(-0.5 * values * values) * 0.3989422804014327


def grad_pre_of(pre_act, grad_out):
    return (grad_out.astype(F32) * gelu_slope(pre_act.astype(F32))).astype(BF16)


class Plan:
    def __init__(self, dp, pos):
        self.dp, self.pos, self.count = dp, pos, dp * pos
        assert self.count & (self.count - 1) == 0
        dp_bits = [pos << b for b in range(dp.bit_length() - 1)]
        pos_bits = [1 << b for b in range(pos.bit_length() - 1)]
        self.core = dp_bits[0]
        self.cross = (dp_bits[1], pos_bits[0])
        rest = (dp_bits[2:] + pos_bits[1:])[:-1]
        self.groups = [rest[i : i + 2] for i in range(0, len(rest), 2)]

    def mask(self, device, stage):
        if stage == "core":
            return self.core
        parity = 1 if device & self.core else 0
        return self.cross[parity if stage == "a" else 1 - parity]

    def swap(self, block, stage):
        route = [(d, d ^ self.mask(d, stage)) for d in range(self.count)]
        return lax.ppermute(block, AXES, route)

    def group_masks(self, group):
        masks = [0]
        for bit in group:
            masks += [m | bit for m in masks]
        return masks

    def shift(self, block, mask):
        return lax.ppermute(block, AXES, [(d, d ^ mask) for d in range(self.count)])

    def complement(self, block):
        return self.shift(block, self.count - 1)

    def source(self, position, device, rows):
        shift = rows.bit_length() - 1
        slot, low = position >> shift, position & (rows - 1)
        bit = self.count.bit_length() - 2
        flag = (slot >> bit) & 1
        owner = device ^ (flag * self.core)
        parity = jnp.where((owner & self.core) != 0, 1, 0)
        first = parity * self.cross[1] + (1 - parity) * self.cross[0]
        second = parity * self.cross[0] + (1 - parity) * self.cross[1]
        owner = owner ^ (((slot >> (bit - 1)) & 1) * first)
        owner = owner ^ (((slot >> (bit - 2)) & 1) * second)
        bit -= 3
        for group in self.groups:
            for mask in reversed(group):
                owner = owner ^ (((slot >> bit) & 1) * mask)
                bit -= 1
        owner = owner ^ ((slot & 1) * (self.count - 1))
        return (owner << shift) + low


def anti_identity(size):
    row = lax.broadcasted_iota(jnp.int32, (size, size), 0)
    col = lax.broadcasted_iota(jnp.int32, (size, size), 1)
    return jnp.where(row + col == size - 1, 1.0, 0.0).astype(BF16)


def selection(plan, device, rows, width):
    position = lax.broadcasted_iota(jnp.int32, (width, 128), 0)
    lane = lax.broadcasted_iota(jnp.int32, (width, 128), 1)
    source = plan.source(position, device, rows)

    def one_hot(index):
        return jnp.concatenate(
            [jnp.where(index == lane + start, 1.0, 0.0).astype(BF16) for start in range(0, width, 128)],
            axis=1,
        )

    return one_hot(source), one_hot(width - 1 - source)


def dot(left, right, dims=(((1,), (0,)), ((), ()))):
    return lax.dot_general(left, right, dims, preferred_element_type=F32)


EDGE = 8


def window_start(strand, tap, taps):
    reach = (taps - 1) // 2
    return EDGE + reach - tap if strand == 0 else EDGE - reach + tap


def prepare_kernel(
    plan, rows, taps, device_ref, values_hbm, pre_hbm, out_grad_hbm,
    kept_ref, sent_ref, direct_ref, mirror_ref, padded_ref, windows_ref,
    values_ref, pre_ref, out_grad_ref, arrived,
):
    seqs, length, width = pre_ref.shape
    half, count = width // 2, seqs * length
    pairs = ((pre_hbm, pre_ref), (out_grad_hbm, out_grad_ref), (values_hbm, values_ref))
    copies = [pltpu.make_async_copy(far, near, arrived.at[i]) for i, (far, near) in enumerate(pairs)]
    for copy in copies:
        copy.start()
    direct_ref[...], mirror_ref[...] = selection(plan, device_ref[0], rows, width)
    for copy in copies:
        copy.wait()
    values = values_ref[...]
    for out_ref, cut in ((kept_ref, slice(0, half)), (sent_ref, slice(half, width))):
        out_ref[:, :count] = dot(direct_ref[cut, :], values, NT).astype(BF16)
        out_ref[:, count:] = dot(mirror_ref[cut, :], values, NT).astype(BF16)
    flip = anti_identity(half)
    for b in range(seqs):
        grads = grad_pre_of(pre_ref[b], out_grad_ref[b])
        for strand in range(2):
            place = strand * seqs + b
            inner = grads[:, :half].astype(F32) if strand == 0 else dot(grads[:, half:], flip)
            padded_ref[place, :EDGE, :] = jnp.zeros((EDGE, half), F32)
            padded_ref[place, EDGE + length :, :] = jnp.zeros((EDGE, half), F32)
            padded_ref[place, EDGE : EDGE + length, :] = inner
            for tap in range(taps):
                start = window_start(strand, tap, taps)
                windows_ref[place * length : (place + 1) * length, tap * half : (tap + 1) * half] = (
                    padded_ref[place, start : start + length, :].astype(BF16)
                )


def first_sums_kernel(taps, order_ref, halo_ref, _, __, out_ref, padded_ref, windows_ref):
    seqs, both, width = halo_ref.shape
    half, reach = width // 2, both // 2
    length = padded_ref.shape[1] - 2 * EDGE
    strip = 16
    flip = anti_identity(half)
    for b in range(seqs):
        for strand in range(2):
            place = strand * seqs + b
            edge = halo_ref[b]
            outer = edge[:, :half].astype(F32) if strand == 0 else dot(edge[:, half:], flip)
            padded_ref[place, EDGE - reach : EDGE, :] = outer[:reach]
            padded_ref[place, EDGE + length : EDGE + length + reach, :] = outer[reach:]
            for tap in range(taps):
                start = window_start(strand, tap, taps)
                for begin in (0, length - strip):
                    windows_ref[
                        place * length + begin : place * length + begin + strip, tap * half : (tap + 1) * half
                    ] = padded_ref[place, start + begin : start + begin + strip, :].astype(BF16)
    out_ref[...] = dot(order_ref[...], windows_ref[...]).astype(out_ref.dtype)


def sums_kernel(order_ref, windows_ref, out_ref):
    out_ref[...] = dot(order_ref[...], windows_ref[...])


def placed_sums(windows_ref, weights_ref, direct, mirror):
    count = windows_ref.shape[0] // 2
    total = None
    for strand, chosen in ((0, direct), (1, mirror)):
        sums = dot(windows_ref[strand * count : (strand + 1) * count, :], weights_ref[...], NT)
        high = sums.astype(BF16)
        low = (sums - high.astype(F32)).astype(BF16)
        both = dot(high, chosen) + dot(low, chosen)
        total = both if total is None else total + both
    return total


def own_input_kernel(direct_ref, mirror_ref, windows_ref, weights_ref, out_ref):
    half = weights_ref.shape[0]
    out_ref[...] = placed_sums(windows_ref, weights_ref, direct_ref[:half, :], mirror_ref[:half, :])


def other_input_kernel(direct_ref, mirror_ref, windows_ref, weights_ref, first_ref, out_ref):
    half = weights_ref.shape[0]
    total = placed_sums(windows_ref, weights_ref, direct_ref[half:, :], mirror_ref[half:, :])
    out_ref[...] = (first_ref[...] + total).astype(BF16)


def reversed_taps(blocks):
    rows, half = blocks[0].shape
    far = dot(jnp.concatenate(blocks, axis=0), anti_identity(half)).astype(BF16)
    far = dot(anti_identity(len(blocks) * rows), far)
    return [far[k * rows : (k + 1) * rows] for k in range(len(blocks))]


def tied_kernel(own_ref, far_ref, out_ref):
    taps, rows, width = far_ref.shape
    half = width // 2
    for place, near_ref, other_ref in ((0, own_ref, far_ref), (1, far_ref, own_ref)):
        other = reversed_taps([other_ref[k, :, half:] for k in range(taps)])
        for k in range(taps):
            out_ref[place * rows : (place + 1) * rows, k * half : (k + 1) * half] = (
                near_ref[k, :, :half].astype(F32) + other[k]
            ).astype(BF16)


def finish_kernel(own_ref, got_ref, out_ref):
    taps, rows, width = out_ref.shape
    half = width // 2
    cuts = [slice(k * half, (k + 1) * half) for k in range(taps)]
    far = own_ref[rows:, :] + got_ref[:rows, :].astype(F32)
    high = far.astype(BF16)
    low = (far - high.astype(F32)).astype(BF16)
    high, low = (reversed_taps([part[:, cut] for cut in cuts]) for part in (high, low))
    near = own_ref[:rows, :] + got_ref[rows:, :].astype(F32)
    for k, cut in enumerate(cuts):
        out_ref[k, :, :half] = near[:, cut]
        out_ref[k, :, half:] = high[k] + low[k]


ON_CHIP = pltpu.VMEM


def call(kernel, outs, args, scalars=0, flops=0, aliases=None, given=(), limit=24, off_chip=(), scratch=()):
    held = pl.BlockSpec(memory_space=ON_CHIP)
    spaces = {i: ON_CHIP for i in given} | {i: pltpu.HBM for i in off_chip}
    args = [pltpu.with_memory_space_constraint(a, spaces[i]) if i in spaces else a for i, a in enumerate(args)]
    result = pl.pallas_call(
        kernel,
        out_shape=[(ON_CHIP if stays else jax.ShapeDtypeStruct)(shape, dtype) for shape, dtype, stays in outs],
        in_specs=[pl.BlockSpec(memory_space=pltpu.SMEM)] * scalars
        + [pl.BlockSpec(memory_space=pltpu.HBM) if i in off_chip else held for i in range(scalars, len(args))],
        scratch_shapes=list(scratch),
        out_specs=[held] * len(outs),
        input_output_aliases=aliases or {},
        cost_estimate=pl.CostEstimate(
            flops=flops,
            transcendentals=0,
            bytes_accessed=sum(math.prod(out[0]) * jnp.dtype(out[1]).itemsize for out in outs)
            + sum(a.size * a.dtype.itemsize for a in args[scalars:]),
        ),
        compiler_params=pltpu.CompilerParams(vmem_limit_bytes=limit << 20),
    )(*args)
    return result if len(outs) > 1 else result[0]


def edges(block, reach):
    count, where = lax.axis_size("pos"), lax.axis_index("pos")
    top, bottom = block[:, -reach:], block[:, :reach]
    if count == 2:
        got = lax.ppermute(jnp.where(where == 0, top, bottom), "pos", [(0, 1), (1, 0)])
        none = jnp.zeros_like(got)
        low, high = jnp.where(where == 0, none, got), jnp.where(where == 0, got, none)
    else:
        forward = [(i, i + 1) for i in range(count - 1)]
        low = lax.ppermute(top, "pos", forward)
        high = lax.ppermute(bottom, "pos", [(b, a) for a, b in forward])
    return jnp.concatenate([low, high], axis=1)


def on_device(plan, inputs, pre_act, grad_out, weight):
    return both_gradients(plan, inputs, pre_act, grad_out, weight)


def both_gradients(plan, inputs, pre_act, grad_out, weight):
    seqs, length, width = inputs.shape
    rows, taps, _ = weight.shape
    half, reach = width // 2, (taps - 1) // 2
    depth, count = taps * half, seqs * length
    work = 4 * count * depth * half
    device = (lax.axis_index("dp") * plan.pos + lax.axis_index("pos")).astype(jnp.int32).reshape(1)

    by_tap = jnp.transpose(weight, (1, 0, 2))
    far_weight = plan.complement(by_tap)
    ends = jnp.concatenate(
        [grad_pre_of(pre_act[:, :reach], grad_out[:, :reach]), grad_pre_of(pre_act[:, -reach:], grad_out[:, -reach:])],
        axis=1,
    )
    halo = edges(ends, reach)
    kept_order, sent_order, direct, mirror, padded, windows = call(
        functools.partial(prepare_kernel, plan, rows, taps),
        [((half, 2 * count), BF16, True)] * 2
        + [((width, width), BF16, True)] * 2
        + [((2 * seqs, length + 2 * EDGE, half), F32, True), ((2 * count, depth), BF16, True)],
        (device, inputs.reshape(count, width), pre_act, grad_out),
        scalars=1, flops=4 * count * width * width, off_chip=(1, 2, 3),
        scratch=(
            pltpu.VMEM((count, width), BF16), pltpu.VMEM((seqs, length, width), BF16),
            pltpu.VMEM((seqs, length, width), BF16), pltpu.SemaphoreType.DMA((3,)),
        ),
    )
    sent, _, windows = call(
        functools.partial(first_sums_kernel, taps),
        [((half, depth), BF16, True), (padded.shape, F32, True), (windows.shape, BF16, True)],
        (sent_order, halo, padded, windows), flops=work, aliases={2: 1, 3: 2}, given=(0, 1, 2, 3),
    )
    received = plan.swap(sent, "core")
    kept = call(sums_kernel, [((half, depth), F32, True)], (kept_order, windows), flops=work, given=(0, 1))
    for stage in ("a", "b"):
        middle = kept.shape[0] // 2
        sent = (kept[middle:] + received[middle:].astype(F32)).astype(BF16)
        kept = kept[:middle] + received[:middle].astype(F32)
        received = plan.swap(sent, stage)
    for place, group in enumerate(plan.groups):
        if place == 0:
            kept = kept + received.astype(F32)
        masks = plan.group_masks(group)
        size = kept.shape[0] // len(masks)
        pieces = [
            plan.shift(kept[j * size : (j + 1) * size].astype(BF16), masks[j]).astype(F32)
            for j in range(1, len(masks))
        ]
        kept = functools.reduce(jnp.add, pieces, kept[:size])
    got = plan.complement(kept.astype(BF16))
    grad_weight = jnp.transpose(
        call(
            finish_kernel, [((taps, rows, width), F32, False)], (kept, got),
            flops=4 * rows * depth * half, given=(0, 1),
        ),
        (1, 0, 2),
    )

    gathered = call(
        tied_kernel, [((2 * rows, depth), BF16, True)], (by_tap, far_weight),
        flops=4 * rows * depth * half, given=(1,),
    )
    for place, group in reversed(list(enumerate(plan.groups))):
        gathered = jnp.concatenate([gathered] + [plan.shift(gathered, m) for m in plan.group_masks(group)[1:]], axis=0)
    for stage in ("b", "a"):
        gathered = jnp.concatenate([gathered, plan.swap(gathered, stage)], axis=0)
    other = plan.swap(gathered, "core")
    first = call(
        own_input_kernel, [((count, width), F32, True)], (direct, mirror, windows, gathered),
        flops=work, given=(0, 1, 2, 3),
    )
    grad_input = call(
        other_input_kernel, [((count, width), BF16, False)], (direct, mirror, windows, other, first),
        flops=work, given=(0, 1, 2, 3, 4),
    ).reshape(seqs, length, width)
    return grad_input, grad_weight


def solution(mesh):
    plan = Plan(mesh.shape["dp"], mesh.shape["pos"])
    placed = (
        P("dp", "pos", None),
        P("dp", "pos", None),
        P("dp", "pos", None),
        P(("dp", "pos"), None, None),
    )
    return jax.shard_map(
        functools.partial(on_device, plan),
        mesh=mesh,
        in_specs=placed,
        out_specs=(P("dp", "pos", None), P(("dp", "pos"), None, None)),
        check_vma=False,
    )
```

profile of v0, /device:TPU:1, one launch (start us, length us, event | category | flops | bytes accessed | tf_op | source)
XLA Modules:
  0.0 67.8 jit_solution(4210588933490342641)
XLA Ops:
  0.6 0.8 %fusion.19 = bf16[2,4,512]{2,1,0:T(4,128)(2,1)S(1)} fusion(bf16[2,256,512]{2,1,0:T(8,128)(2,1)} %pre_hbm.1, bf16[2,256,512]{2,1,0:T(8,128)(2,1)} %out_grad_hbm.1, pred[]{:T(512)S(6)} %eq.2), kind=kLoop, calls=%fused_computation.37 | loop fusion | flops 102400 | bytes 40961 | tf_op jit(solution)/shard_map/jit(_where)/select_n | solution.py:257
  1.5 2.1 %collective-permute-start = (bf16[2,4,512]{2,1,0:T(4,128)(2,1)S(1)}, bf16[2,4,512]{2,1,0:T(4,128)(2,1)S(1)}, u32[]{:S(2)}, u32[]{:S(2)}) collective-permute-start(bf16[2,4,512]{2,1,0:T(4,128)(2,1)S(1)} %fusion.19), channel_id=1, source_target_pairs={{0,1},{1,0},{2,3},{3,2},{4,5},{5,4},{6,7},{7,6},{8,9},{9,8},{10,11... | collective-permute-start | bytes 24584 | tf_op jit(solution)/shard_map/ppermute | solution.py:257
  3.5 3.1 %shard_map.59 = (bf16[256,1024]{1,0:T(8,128)(2,1)S(1)}, bf16[256,1024]{1,0:T(8,128)(2,1)S(1)}, bf16[512,512]{1,0:T(8,128)(2,1)S(1)}, bf16[512,512]{1,0:T(8,128)(...) custom-call(s32[1]{0:T(128)} %bitcast.device_ref, bf16[512,512]{1,0:T(8,128)(2,1)} %bitcast.9, ...), custom_call_target="tpu_custom_call" | custom-call | flops 536870912 | bytes 9502720 | tf_op jit(solution)/shard_map/pallas_call | solution.py:234
  6.7 0.0 collective-permute-done
  6.7 0.0 copy-start
  6.7 1.5 %shard_map.60 = (bf16[256,2304]{1,0:T(8,128)(2,1)S(1)}, f32[4,272,256]{2,1,0:T(8,128)S(1)}, bf16[1024,2304]{1,0:T(8,128)(2,1)S(1)}) custom-call(bf16[256,1024]{1,0:T(8,128)(2,1)S(1)} %get-tuple-element.12.order_ref, bf16[2,8,512]{2,1,0:T(8,128)(2,1)S(1)} %pad_maximum_fusion.3.halo_ref, ...), custom_call_target="tpu_custom_call", output_to_operand_aliasing={{1}: (2, {}), {2}: (3, {})} | custom-call | flops 1207959552 | bytes 13385728 | tf_op jit(solution)/shard_map/pallas_call | solution.py:234
  8.3 1.0 %collective-permute-start.6 = (bf16[256,2304]{1,0:T(8,128)(2,1)S(1)}, bf16[256,2304]{1,0:T(8,128)(2,1)S(1)}, u32[]{:S(2)}, u32[]{:S(2)}) collective-permute-start(bf16[256,2304]{1,0:T(8,128)(2,1)S(1)} %get-tuple-element.17), channel_id=1, source_target_pairs={{0,2},{1,3},{2,0},{3,1},{4,6},{5,7},{6,4},{7,5},{8,10},{9,11},{10,... | collective-permute-start | bytes 3538952 | tf_op jit(solution)/shard_map/ppermute | solution.py:46
  9.3 0.0 copy-done
  9.3 4.2 %collective-permute-start.1 = (bf16[9,16,512]{2,1,0:T(8,128)(2,1)S(1)}, bf16[9,16,512]{2,1,0:T(8,128)(2,1)S(1)}, u32[]{:S(2)}, u32[]{:S(2)}) collective-permute-start(bf16[9,16,512]{2,1,0:T(8,128)(2,1)S(1)} %bitcast.5), channel_id=1, source_target_pairs={{0,31},{1,30},{2,29},{3,28},{4,27},{5,26},{6,25},{7,24},{8,23},{9,... | collective-permute-start | bytes 442376 | tf_op jit(solution)/shard_map/ppermute | solution.py:55
  13.5 5.0 %collective-permute-done.1.far_ref = bf16[9,16,512]{2,1,0:T(8,128)(2,1)S(1)} collective-permute-done((bf16[9,16,512]{2,1,0:T(8,128)(2,1)S(1)}, bf16[9,16,512]{2,1,0:T(8,128)(2,1)S(1)}, u32[]{:S(2)}, u32[]{:S(2)}) %collective-permute-start.1) | collective-permute-done | bytes 147488 | tf_op jit(solution)/shard_map/ppermute | solution.py:55
  18.6 0.5 shard_map.61
  19.1 2.6 %collective-permute-start.2 = (bf16[32,2304]{1,0:T(8,128)(2,1)S(1)}, bf16[32,2304]{1,0:T(8,128)(2,1)S(1)}, u32[]{:S(2)}, u32[]{:S(2)}) collective-permute-start(bf16[32,2304]{1,0:T(8,128)(2,1)S(1)} %shard_map.61), channel_id=1, source_target_pairs={{0,8},{1,9},{2,10},{3,11},{4,12},{5,13},{6,14},{7,15},{8,0},{9,1},... | collective-permute-start | bytes 442376 | tf_op jit(solution)/shard_map/ppermute | solution.py:55
  21.7 1.4 %shard_map.64 = f32[256,2304]{1,0:T(8,128)S(1)} custom-call(bf16[256,1024]{1,0:T(8,128)(2,1)S(1)} %get-tuple-element.16.order_ref, bf16[1024,2304]{1,0:T(8,128)(2,1)S(1)} %get-tuple-element.15.windows_ref), custom_call_target="tpu_custom_call" | custom-call | flops 1207959552 | bytes 7602176 | tf_op jit(solution)/shard_map/pallas_call | solution.py:234
  23.1 2.8 %collective-permute-done.2 = bf16[32,2304]{1,0:T(8,128)(2,1)S(1)} collective-permute-done((bf16[32,2304]{1,0:T(8,128)(2,1)S(1)}, bf16[32,2304]{1,0:T(8,128)(2,1)S(1)}, u32[]{:S(2)}, u32[]{:S(2)}) %collective-permute-start.2) | collective-permute-done | bytes 147488 | tf_op jit(solution)/shard_map/ppermute | solution.py:55
  25.9 1.3 %collective-permute-start.3 = (bf16[64,2304]{1,0:T(8,128)(2,1)S(1)}, bf16[64,2304]{1,0:T(8,128)(2,1)S(1)}, u32[]{:S(2)}, u32[]{:S(2)}) collective-permute-start(bf16[64,2304]{1,0:T(8,128)(2,1)S(1)} %pad_maximum_fusion.2), channel_id=1, source_target_pairs={{0,1},{1,0},{2,6},{3,7},{4,5},{5,4},{6,2},{7,3},{8,9},{9,8},{10,14... | collective-permute-start | bytes 884744 | tf_op jit(solution)/shard_map/ppermute | solution.py:46
  27.2 0.0 collective-permute-done.6
  27.2 0.2 fusion
  27.4 0.3 collective-permute-start.7
  27.7 5.4 %collective-permute-done.3 = bf16[64,2304]{1,0:T(8,128)(2,1)S(1)} collective-permute-done((bf16[64,2304]{1,0:T(8,128)(2,1)S(1)}, bf16[64,2304]{1,0:T(8,128)(2,1)S(1)}, u32[]{:S(2)}, u32[]{:S(2)}) %collective-permute-start.3) | collective-permute-done | bytes 294944 | tf_op jit(solution)/shard_map/ppermute | solution.py:46
  33.1 0.1 collective-permute-start.4
  33.2 5.8 %collective-permute-done.7 = bf16[128,2304]{1,0:T(8,128)(2,1)S(1)} collective-permute-done((bf16[128,2304]{1,0:T(8,128)(2,1)S(1)}, bf16[128,2304]{1,0:T(8,128)(2,1)S(1)}, u32[]{:S(2)}, u32[]{:S(2)}) %collective-permute-start.7) | collective-permute-done | bytes 589856 | tf_op jit(solution)/shard_map/ppermute | solution.py:46
  39.0 0.1 fusion.1
  39.0 0.7 collective-permute-start.8
  39.7 9.0 %collective-permute-done.4 = bf16[128,2304]{1,0:T(8,128)(2,1)S(1)} collective-permute-done((bf16[128,2304]{1,0:T(8,128)(2,1)S(1)}, bf16[128,2304]{1,0:T(8,128)(2,1)S(1)}, u32[]{:S(2)}, u32[]{:S(2)}) %collective-permute-start.4) | collective-permute-done | bytes 589856 | tf_op jit(solution)/shard_map/ppermute | solution.py:46
  48.7 0.1 pad_maximum_fusion.weights_ref
  48.8 0.6 collective-permute-start.5
  49.4 0.0 collective-permute-done.8
  49.4 0.1 fusion.2
  49.5 1.8 %collective-permute-start.9 = (bf16[32,2304]{1,0:T(8,128)(2,1)S(1)}, bf16[32,2304]{1,0:T(8,128)(2,1)S(1)}, u32[]{:S(2)}, u32[]{:S(2)}) collective-permute-start(bf16[32,2304]{1,0:T(8,128)(2,1)S(1)} %slice.87), channel_id=1, source_target_pairs={{0,8},{1,9},{2,10},{3,11},{4,12},{5,13},{6,14},{7,15},{8,0},{9,1},... | collective-permute-start | bytes 442376 | tf_op jit(solution)/shard_map/ppermute | solution.py:55
  51.3 4.2 %collective-permute-done.9 = bf16[32,2304]{1,0:T(8,128)(2,1)S(1)} collective-permute-done((bf16[32,2304]{1,0:T(8,128)(2,1)S(1)}, bf16[32,2304]{1,0:T(8,128)(2,1)S(1)}, u32[]{:S(2)}, u32[]{:S(2)}) %collective-permute-start.9) | collective-permute-done | bytes 147488 | tf_op jit(solution)/shard_map/ppermute | solution.py:55
  55.5 3.8 %collective-permute-start.10 = (bf16[32,2304]{1,0:T(8,128)(2,1)S(1)}, bf16[32,2304]{1,0:T(8,128)(2,1)S(1)}, u32[]{:S(2)}, u32[]{:S(2)}) collective-permute-start(bf16[32,2304]{1,0:T(8,128)(2,1)S(1)} %get-tuple-element.18), channel_id=1, source_target_pairs={{0,31},{1,30},{2,29},{3,28},{4,27},{5,26},{6,25},{7,24},{8,23},{9,... | collective-permute-start | bytes 442376 | tf_op jit(solution)/shard_map/ppermute | solution.py:55
  59.4 3.2 %shard_map.62.first_ref = f32[512,512]{1,0:T(8,128)S(1)} custom-call(bf16[512,512]{1,0:T(8,128)(2,1)S(1)} %get-tuple-element.10.direct_ref, bf16[512,512]{1,0:T(8,128)(2,1)S(1)} %get-tuple-element.11.mirror_ref, bf16[1024,2304]{1,0:T(8,128)(2,1)S(1)} %get-tuple-element.15.windows_ref, bf16[256,2304]{1,0:T(8,128)(2,1)S(1)} %pad_maximum_fusion.weights_ref), custom_call_target="tpu_custom_call" | custom-call | flops 1207959552 | bytes 7995392 | tf_op jit(solution)/shard_map/pallas_call | solution.py:234
  62.5 0.0 collective-permute-done.5.weights_ref
  62.5 4.0 %shard_map.63 = bf16[512,512]{1,0:T(8,128)(2,1)} custom-call(bf16[512,512]{1,0:T(8,128)(2,1)S(1)} %get-tuple-element.10.direct_ref, bf16[512,512]{1,0:T(8,128)(2,1)S(1)} %get-tuple-element.11.mirror_ref, bf16[1024,2304]{1,0:T(8,128)(2,1)S(1)} %get-tuple-element.15.windows_ref, bf16[256,2304]{1,0:T(8,128)(2,1)S(1)} %collective-permute-done.5.weights_ref, ...), custom_call_target="tpu_custom_call" | custom-call | flops 1207959552 | bytes 8519680 | tf_op jit(solution)/shard_map/pallas_call | solution.py:234
  66.5 0.0 collective-permute-done.10.got_ref
  66.5 1.3 %shard_map.65 = f32[9,16,512]{2,1,0:T(8,128)} custom-call(f32[32,2304]{1,0:T(8,128)S(1)} %get-tuple-element.19.own_ref, bf16[32,2304]{1,0:T(8,128)(2,1)S(1)} %collective-permute-done.10.got_ref), custom_call_target="tpu_custom_call" | custom-call | flops 37748736 | bytes 737280 | tf_op jit(solution)/shard_map/pallas_call | solution.py:234
  (6 shorter events, 0.1 us)
Async XLA Ops:
  1.5 5.2 %collective-permute-start = (bf16[2,4,512]{2,1,0:T(4,128)(2,1)S(1)}, bf16[2,4,512]{2,1,0:T(4,128)(2,1)S(1)}, u32[]{:S(2)}, u32[]{:S(2)}) collective-permute-start(bf16[2,4,512]{2,1,0:T(4,128)(2,1)S(1)} %fusion.19), channel_id=1, source_target_pairs={{0,1},{1,0},{2,3},{3,2},{4,5},{5,4},{6,7},{7,6},{8,9},{9,8},{10,11... | collective-permute-start | bytes 24584 | tf_op jit(solution)/shard_map/ppermute | solution.py:257
  6.7 2.6 %copy-start = (bf16[16,9,512]{2,0,1:T(8,128)(2,1)S(1)}, bf16[16,9,512]{2,0,1:T(8,128)(2,1)}, u32[]{:S(2)}) copy-start(bf16[16,9,512]{2,0,1:T(8,128)(2,1)} %param.7) | copy-start | bytes 442372
  8.3 18.9 %collective-permute-start.6 = (bf16[256,2304]{1,0:T(8,128)(2,1)S(1)}, bf16[256,2304]{1,0:T(8,128)(2,1)S(1)}, u32[]{:S(2)}, u32[]{:S(2)}) collective-permute-start(bf16[256,2304]{1,0:T(8,128)(2,1)S(1)} %get-tuple-element.17), channel_id=1, source_target_pairs={{0,2},{1,3},{2,0},{3,1},{4,6},{5,7},{6,4},{7,5},{8,10},{9,11},{10,... | collective-permute-start | bytes 3538952 | tf_op jit(solution)/shard_map/ppermute | solution.py:46
  9.3 9.2 %collective-permute-start.1 = (bf16[9,16,512]{2,1,0:T(8,128)(2,1)S(1)}, bf16[9,16,512]{2,1,0:T(8,128)(2,1)S(1)}, u32[]{:S(2)}, u32[]{:S(2)}) collective-permute-start(bf16[9,16,512]{2,1,0:T(8,128)(2,1)S(1)} %bitcast.5), channel_id=1, source_target_pairs={{0,31},{1,30},{2,29},{3,28},{4,27},{5,26},{6,25},{7,24},{8,23},{9,... | collective-permute-start | bytes 442376 | tf_op jit(solution)/shard_map/ppermute | solution.py:55
  19.1 6.8 %collective-permute-start.2 = (bf16[32,2304]{1,0:T(8,128)(2,1)S(1)}, bf16[32,2304]{1,0:T(8,128)(2,1)S(1)}, u32[]{:S(2)}, u32[]{:S(2)}) collective-permute-start(bf16[32,2304]{1,0:T(8,128)(2,1)S(1)} %shard_map.61), channel_id=1, source_target_pairs={{0,8},{1,9},{2,10},{3,11},{4,12},{5,13},{6,14},{7,15},{8,0},{9,1},... | collective-permute-start | bytes 442376 | tf_op jit(solution)/shard_map/ppermute | solution.py:55
  25.9 7.2 %collective-permute-start.3 = (bf16[64,2304]{1,0:T(8,128)(2,1)S(1)}, bf16[64,2304]{1,0:T(8,128)(2,1)S(1)}, u32[]{:S(2)}, u32[]{:S(2)}) collective-permute-start(bf16[64,2304]{1,0:T(8,128)(2,1)S(1)} %pad_maximum_fusion.2), channel_id=1, source_target_pairs={{0,1},{1,0},{2,6},{3,7},{4,5},{5,4},{6,2},{7,3},{8,9},{9,8},{10,14... | collective-permute-start | bytes 884744 | tf_op jit(solution)/shard_map/ppermute | solution.py:46
  27.4 11.6 %collective-permute-start.7 = (bf16[128,2304]{1,0:T(8,128)(2,1)S(1)}, bf16[128,2304]{1,0:T(8,128)(2,1)S(1)}, u32[]{:S(2)}, u32[]{:S(2)}) collective-permute-start(bf16[128,2304]{1,0:T(8,128)(2,1)S(1)} %get-tuple-element.20), channel_id=1, source_target_pairs={{0,4},{1,5},{2,3},{3,2},{4,0},{5,1},{6,7},{7,6},{8,12},{9,13},{10,... | collective-permute-start | bytes 1769480 | tf_op jit(solution)/shard_map/ppermute | solution.py:46
  33.1 15.6 %collective-permute-start.4 = (bf16[128,2304]{1,0:T(8,128)(2,1)S(1)}, bf16[128,2304]{1,0:T(8,128)(2,1)S(1)}, u32[]{:S(2)}, u32[]{:S(2)}) collective-permute-start(bf16[128,2304]{1,0:T(8,128)(2,1)S(1)} %pad_maximum_fusion.1), channel_id=1, source_target_pairs={{0,4},{1,5},{2,3},{3,2},{4,0},{5,1},{6,7},{7,6},{8,12},{9,13},{10,... | collective-permute-start | bytes 1769480 | tf_op jit(solution)/shard_map/ppermute | solution.py:46
  39.0 10.4 %collective-permute-start.8 = (bf16[64,2304]{1,0:T(8,128)(2,1)S(1)}, bf16[64,2304]{1,0:T(8,128)(2,1)S(1)}, u32[]{:S(2)}, u32[]{:S(2)}) collective-permute-start(bf16[64,2304]{1,0:T(8,128)(2,1)S(1)} %fusion.1), channel_id=1, source_target_pairs={{0,1},{1,0},{2,6},{3,7},{4,5},{5,4},{6,2},{7,3},{8,9},{9,8},{10,14... | collective-permute-start | bytes 884744 | tf_op jit(solution)/shard_map/ppermute | solution.py:46
  48.8 13.7 %collective-permute-start.5 = (bf16[256,2304]{1,0:T(8,128)(2,1)S(1)}, bf16[256,2304]{1,0:T(8,128)(2,1)S(1)}, u32[]{:S(2)}, u32[]{:S(2)}) collective-permute-start(bf16[256,2304]{1,0:T(8,128)(2,1)S(1)} %pad_maximum_fusion.weights_ref), channel_id=1, source_target_pairs={{0,2},{1,3},{2,0},{3,1},{4,6},{5,7},{6,4},{7,5},{8,10},{9,11},{10,... | collective-permute-start | bytes 3538952 | tf_op jit(solution)/shard_map/ppermute | solution.py:46
  49.5 6.0 %collective-permute-start.9 = (bf16[32,2304]{1,0:T(8,128)(2,1)S(1)}, bf16[32,2304]{1,0:T(8,128)(2,1)S(1)}, u32[]{:S(2)}, u32[]{:S(2)}) collective-permute-start(bf16[32,2304]{1,0:T(8,128)(2,1)S(1)} %slice.87), channel_id=1, source_target_pairs={{0,8},{1,9},{2,10},{3,11},{4,12},{5,13},{6,14},{7,15},{8,0},{9,1},... | collective-permute-start | bytes 442376 | tf_op jit(solution)/shard_map/ppermute | solution.py:55
  55.5 11.0 %collective-permute-start.10 = (bf16[32,2304]{1,0:T(8,128)(2,1)S(1)}, bf16[32,2304]{1,0:T(8,128)(2,1)S(1)}, u32[]{:S(2)}, u32[]{:S(2)}) collective-permute-start(bf16[32,2304]{1,0:T(8,128)(2,1)S(1)} %get-tuple-element.18), channel_id=1, source_target_pairs={{0,31},{1,30},{2,29},{3,28},{4,27},{5,26},{6,25},{7,24},{8,23},{9,... | collective-permute-start | bytes 442376 | tf_op jit(solution)/shard_map/ppermute | solution.py:55
where the time goes:
time: 68 us; the launch traced here: 67.8 us
  waiting for transfers between devices  32.2 us (47%)
  starting transfers between devices  18.5 us (27%)
  Pallas kernels  14.9 us (22%)
  other arithmetic  1.32 us (2%)
  between operations  0.77 us (1%)
    ppermute x6, waiting for transfers between devices, swap(): return lax.ppermute(block, AXES, route)  20.2 us
    pallas_call x7, Pallas kernels, call(): pl.pallas_call(kernel, out_shape=[(ON_CHIP if stays else jax.ShapeDtypeSt...  14.9 us
    ppermute x4, starting transfers between devices, shift(): return lax.ppermute(block, AXES, [(d, d ^ mask) for d in range(self.count)])  12.4 us
    ppermute x4, waiting for transfers between devices, shift(): return lax.ppermute(block, AXES, [(d, d ^ mask) for d in range(self.count)])  12 us
    ppermute x6, starting transfers between devices, swap(): return lax.ppermute(block, AXES, route)  3.98 us
    ppermute x1, starting transfers between devices, edges(): lax.ppermute(jnp.where(where == 0, top, bottom), 'pos', [(0, 1), (1, 0)])  2.09 us
  transfers between devices with their start and end apart: 11, of which 6 were waited for; matrix products, arithmetic and copies ran while one was open for 1% of the time, Pallas kernels for 18%

commit v1 on v0

--- a/solution.py
+++ b/solution.py
@@ -111,7 +111,7 @@
 
 def prepare_kernel(
     plan, rows, taps, device_ref, values_hbm, pre_hbm, out_grad_hbm,
-    kept_ref, sent_ref, direct_ref, mirror_ref, padded_ref, windows_ref,
+    kept_ref, sent_ref, direct_ref, padded_ref, windows_ref,
     values_ref, pre_ref, out_grad_ref, arrived,
 ):
     seqs, length, width = pre_ref.shape
@@ -120,13 +120,14 @@
     copies = [pltpu.make_async_copy(far, near, arrived.at[i]) for i, (far, near) in enumerate(pairs)]
     for copy in copies:
         copy.start()
-    direct_ref[...], mirror_ref[...] = selection(plan, device_ref[0], rows, width)
+    direct, mirror = selection(plan, device_ref[0], rows, width)
+    direct_ref[...] = direct
     for copy in copies:
         copy.wait()
     values = values_ref[...]
     for out_ref, cut in ((kept_ref, slice(0, half)), (sent_ref, slice(half, width))):
-        out_ref[:, :count] = dot(direct_ref[cut, :], values, NT).astype(BF16)
-        out_ref[:, count:] = dot(mirror_ref[cut, :], values, NT).astype(BF16)
+        out_ref[:, :count] = dot(direct[cut], values, NT).astype(BF16)
+        out_ref[:, count:] = dot(mirror[cut], values, NT).astype(BF16)
     flip = anti_identity(half)
     for b in range(seqs):
         grads = grad_pre_of(pre_ref[b], out_grad_ref[b])
@@ -169,27 +170,28 @@
     out_ref[...] = dot(order_ref[...], windows_ref[...])
 
 
-def placed_sums(windows_ref, weights_ref, direct, mirror):
+def placed_sums(group, windows_ref, direct_ref, weight_refs, begins):
     count = windows_ref.shape[0] // 2
-    total = None
-    for strand, chosen in ((0, direct), (1, mirror)):
-        sums = dot(windows_ref[strand * count : (strand + 1) * count, :], weights_ref[...], NT)
-        high = sums.astype(BF16)
-        low = (sums - high.astype(F32)).astype(BF16)
-        both = dot(high, chosen) + dot(low, chosen)
-        total = both if total is None else total + both
-    return total
-
-
-def own_input_kernel(direct_ref, mirror_ref, windows_ref, weights_ref, out_ref):
-    half = weights_ref.shape[0]
-    out_ref[...] = placed_sums(windows_ref, weights_ref, direct_ref[:half, :], mirror_ref[:half, :])
-
-
-def other_input_kernel(direct_ref, mirror_ref, windows_ref, weights_ref, first_ref, out_ref):
-    half = weights_ref.shape[0]
-    total = placed_sums(windows_ref, weights_ref, direct_ref[half:, :], mirror_ref[half:, :])
-    out_ref[...] = (first_ref[...] + total).astype(BF16)
+    weights = jnp.concatenate([ref[...] for ref in weight_refs], axis=0)
+    chosen = jnp.concatenate(
+        [direct_ref[begin : begin + ref.shape[0], :] for ref, begin in zip(weight_refs, begins)], axis=0
+    )
+    size = weights.shape[0]
+    row = lax.broadcasted_iota(jnp.int32, (size, size), 0)
+    col = lax.broadcasted_iota(jnp.int32, (size, size), 1)
+    turn = jnp.where(row == (col ^ (group - 1)), 1.0, 0.0).astype(BF16)
+    mirrored = dot(turn, weights).astype(BF16)
+    sums = dot(windows_ref[:count, :], weights, NT) + dot(windows_ref[count:, :], mirrored, NT)
+    return dot(sums.astype(BF16), chosen)
+
+
+def early_input_kernel(group, begins, direct_ref, windows_ref, own_ref, other_ref, out_ref):
+    out_ref[...] = placed_sums(group, windows_ref, direct_ref, (own_ref, other_ref), begins).astype(BF16)
+
+
+def late_input_kernel(group, begins, direct_ref, windows_ref, own_ref, other_ref, early_ref, out_ref):
+    late = placed_sums(group, windows_ref, direct_ref, (own_ref, other_ref), begins)
+    out_ref[...] = (early_ref[...].astype(F32) + late).astype(BF16)
 
 
 def reversed_taps(blocks):
@@ -283,10 +285,10 @@
         axis=1,
     )
     halo = edges(ends, reach)
-    kept_order, sent_order, direct, mirror, padded, windows = call(
+    kept_order, sent_order, direct, padded, windows = call(
         functools.partial(prepare_kernel, plan, rows, taps),
         [((half, 2 * count), BF16, True)] * 2
-        + [((width, width), BF16, True)] * 2
+        + [((width, width), BF16, True)]
         + [((2 * seqs, length + 2 * EDGE, half), F32, True), ((2 * count, depth), BF16, True)],
         (device, inputs.reshape(count, width), pre_act, grad_out),
         scalars=1, flops=4 * count * width * width, off_chip=(1, 2, 3),
@@ -332,15 +334,19 @@
     )
     for place, group in reversed(list(enumerate(plan.groups))):
         gathered = jnp.concatenate([gathered] + [plan.shift(gathered, m) for m in plan.group_masks(group)[1:]], axis=0)
-    for stage in ("b", "a"):
-        gathered = jnp.concatenate([gathered, plan.swap(gathered, stage)], axis=0)
+    gathered = jnp.concatenate([gathered, plan.swap(gathered, "b")], axis=0)
     other = plan.swap(gathered, "core")
-    first = call(
-        own_input_kernel, [((count, width), F32, True)], (direct, mirror, windows, gathered),
+    late = plan.swap(gathered, "a")
+    late_other = plan.swap(late, "core")
+    size = gathered.shape[0]
+    early = call(
+        functools.partial(early_input_kernel, 2 * rows, (0, 2 * size)),
+        [((count, width), BF16, True)], (direct, windows, gathered, other),
         flops=work, given=(0, 1, 2, 3),
     )
     grad_input = call(
-        other_input_kernel, [((count, width), BF16, False)], (direct, mirror, windows, other, first),
+        functools.partial(late_input_kernel, 2 * rows, (size, 3 * size)),
+        [((count, width), BF16, False)], (direct, windows, late, late_other, early),
         flops=work, given=(0, 1, 2, 3, 4),
     ).reshape(seqs, length, width)
     return grad_input, grad_weight

time: 68 us -> 55.2 us (0.81)
  the two profiles are of different devices: /device:TPU:1 before, /device:TPU:13 now
where the time goes in v1:
time: 55.2 us; the launch traced here: 55 us
  waiting for transfers between devices  27 us (49%)
  Pallas kernels  13.3 us (24%)
  starting transfers between devices  12.7 us (23%)
  other arithmetic  1.25 us (2%)
  between operations  0.78 us (1%)
    ppermute x4, waiting for transfers between devices, shift(): return lax.ppermute(block, AXES, [(d, d ^ mask) for d in range(self.count)])  15.9 us
    pallas_call x7, Pallas kernels, call(): pl.pallas_call(kernel, out_shape=[(ON_CHIP if stays else jax.ShapeDtypeSt...  13.3 us
    ppermute x7, waiting for transfers between devices, swap(): return lax.ppermute(block, AXES, route)  11 us
    ppermute x7, starting transfers between devices, swap(): return lax.ppermute(block, AXES, route)  8.44 us
    ppermute x4, starting transfers between devices, shift(): return lax.ppermute(block, AXES, [(d, d ^ mask) for d in range(self.count)])  3 us
    ppermute x1, starting transfers between devices, edges(): lax.ppermute(jnp.where(where == 0, top, bottom), 'pos', [(0, 1), (1, 0)])  1.28 us
  transfers between devices with their start and end apart: 12, of which 6 were waited for; matrix products, arithmetic and copies ran while one was open for 1% of the time, Pallas kernels for 19%

profile of v1, /device:TPU:13, one launch (start us, length us, event | category | flops | bytes accessed | tf_op | source)
XLA Modules:
  0.0 55.0 jit_solution(9312599695676434359)
XLA Ops:
  0.6 0.8 %fusion.19 = bf16[2,4,512]{2,1,0:T(4,128)(2,1)S(1)} fusion(bf16[2,256,512]{2,1,0:T(8,128)(2,1)} %pre_hbm.1, bf16[2,256,512]{2,1,0:T(8,128)(2,1)} %out_grad_hbm.1, pred[]{:T(512)S(6)} %eq.2), kind=kLoop, calls=%fused_computation.36 | loop fusion | flops 102400 | bytes 40961 | tf_op jit(solution)/shard_map/jit(_where)/select_n | solution.py:259
  1.5 1.3 %collective-permute-start = (bf16[2,4,512]{2,1,0:T(4,128)(2,1)S(1)}, bf16[2,4,512]{2,1,0:T(4,128)(2,1)S(1)}, u32[]{:S(2)}, u32[]{:S(2)}) collective-permute-start(bf16[2,4,512]{2,1,0:T(4,128)(2,1)S(1)} %fusion.19), channel_id=1, source_target_pairs={{0,1},{1,0},{2,3},{3,2},{4,5},{5,4},{6,7},{7,6},{8,9},{9,8},{10,11... | collective-permute-start | bytes 24584 | tf_op jit(solution)/shard_map/ppermute | solution.py:259
  2.7 3.3 %shard_map.59 = (bf16[256,1024]{1,0:T(8,128)(2,1)S(1)}, bf16[256,1024]{1,0:T(8,128)(2,1)S(1)}, bf16[512,512]{1,0:T(8,128)(2,1)S(1)}, f32[4,272,256]{2,1,0:T(8,128)S(1)}, bf16[1024,2304]{1,0:T(8,128)(2,1)S(1)}) custom-call(s32[1]{0:T(128)} %bitcast.device_ref, bf16[512,512]{1,0:T(8,128)(2,1)} %bitcast.9, bf16[2,256,512]{2,1,0:T(8,128)(2,1)} %pre_hbm.1, ...), custom_call_target="tpu_custom_call" | custom-call | flops 536870912 | bytes 8978432 | tf_op jit(solution)/shard_map/pallas_call | solution.py:236
  6.1 0.0 collective-permute-done
  6.1 0.0 copy-start
  6.1 1.6 %shard_map.60 = (bf16[256,2304]{1,0:T(8,128)(2,1)S(1)}, f32[4,272,256]{2,1,0:T(8,128)S(1)}, bf16[1024,2304]{1,0:T(8,128)(2,1)S(1)}) custom-call(bf16[256,1024]{1,0:T(8,128)(2,1)S(1)} %get-tuple-element.10.order_ref, bf16[2,8,512]{2,1,0:T(8,128)(2,1)S(1)} %pad_maximum_fusion.2.halo_ref, ...), custom_call_target="tpu_custom_call", output_to_operand_aliasing={{1}: (2, {}), {2}: (3, {})} | custom-call | flops 1207959552 | bytes 13385728 | tf_op jit(solution)/shard_map/pallas_call | solution.py:236
  7.7 1.0 %collective-permute-start.7 = (bf16[256,2304]{1,0:T(8,128)(2,1)S(1)}, bf16[256,2304]{1,0:T(8,128)(2,1)S(1)}, u32[]{:S(2)}, u32[]{:S(2)}) collective-permute-start(bf16[256,2304]{1,0:T(8,128)(2,1)S(1)} %get-tuple-element.15), channel_id=1, source_target_pairs={{0,2},{1,3},{2,0},{3,1},{4,6},{5,7},{6,4},{7,5},{8,10},{9,11},{10,... | collective-permute-start | bytes 3538952 | tf_op jit(solution)/shard_map/ppermute | solution.py:46
  8.7 0.0 copy-done
  8.7 1.2 %collective-permute-start.1 = (bf16[9,16,512]{2,1,0:T(8,128)(2,1)S(1)}, bf16[9,16,512]{2,1,0:T(8,128)(2,1)S(1)}, u32[]{:S(2)}, u32[]{:S(2)}) collective-permute-start(bf16[9,16,512]{2,1,0:T(8,128)(2,1)S(1)} %bitcast.5), channel_id=1, source_target_pairs={{0,31},{1,30},{2,29},{3,28},{4,27},{5,26},{6,25},{7,24},{8,23},{9,... | collective-permute-start | bytes 442376 | tf_op jit(solution)/shard_map/ppermute | solution.py:55
  9.9 1.4 %shard_map.64 = f32[256,2304]{1,0:T(8,128)S(1)} custom-call(bf16[256,1024]{1,0:T(8,128)(2,1)S(1)} %get-tuple-element.14.order_ref, bf16[1024,2304]{1,0:T(8,128)(2,1)S(1)} %get-tuple-element.13.windows_ref), custom_call_target="tpu_custom_call" | custom-call | flops 1207959552 | bytes 7602176 | tf_op jit(solution)/shard_map/pallas_call | solution.py:236
  11.3 0.0 collective-permute-done.7
  11.3 0.2 fusion
  11.5 1.3 %collective-permute-start.8 = (bf16[128,2304]{1,0:T(8,128)(2,1)S(1)}, bf16[128,2304]{1,0:T(8,128)(2,1)S(1)}, u32[]{:S(2)}, u32[]{:S(2)}) collective-permute-start(bf16[128,2304]{1,0:T(8,128)(2,1)S(1)} %get-tuple-element.18), channel_id=1, source_target_pairs={{0,4},{1,5},{2,3},{3,2},{4,0},{5,1},{6,7},{7,6},{8,12},{9,13},{10,... | collective-permute-start | bytes 1769480 | tf_op jit(solution)/shard_map/ppermute | solution.py:46
  12.8 6.6 %collective-permute-done.1.far_ref = bf16[9,16,512]{2,1,0:T(8,128)(2,1)S(1)} collective-permute-done((bf16[9,16,512]{2,1,0:T(8,128)(2,1)S(1)}, bf16[9,16,512]{2,1,0:T(8,128)(2,1)S(1)}, u32[]{:S(2)}, u32[]{:S(2)}) %collective-permute-start.1) | collective-permute-done | bytes 147488 | tf_op jit(solution)/shard_map/ppermute | solution.py:55
  19.3 0.5 shard_map.61
  19.9 0.1 collective-permute-start.2
  19.9 5.3 %collective-permute-done.2 = bf16[32,2304]{1,0:T(8,128)(2,1)S(1)} collective-permute-done((bf16[32,2304]{1,0:T(8,128)(2,1)S(1)}, bf16[32,2304]{1,0:T(8,128)(2,1)S(1)}, u32[]{:S(2)}, u32[]{:S(2)}) %collective-permute-start.2) | collective-permute-done | bytes 147488 | tf_op jit(solution)/shard_map/ppermute | solution.py:55
  25.3 0.3 collective-permute-start.3
  25.6 0.0 collective-permute-done.8
  25.6 0.1 fusion.1
  25.6 1.3 %collective-permute-start.9 = (bf16[64,2304]{1,0:T(8,128)(2,1)S(1)}, bf16[64,2304]{1,0:T(8,128)(2,1)S(1)}, u32[]{:S(2)}, u32[]{:S(2)}) collective-permute-start(bf16[64,2304]{1,0:T(8,128)(2,1)S(1)} %fusion.1), channel_id=1, source_target_pairs={{0,1},{1,0},{2,6},{3,7},{4,5},{5,4},{6,2},{7,3},{8,9},{9,8},{10,14... | collective-permute-start | bytes 884744 | tf_op jit(solution)/shard_map/ppermute | solution.py:46
  26.9 4.3 %collective-permute-done.3 = bf16[64,2304]{1,0:T(8,128)(2,1)S(1)} collective-permute-done((bf16[64,2304]{1,0:T(8,128)(2,1)S(1)}, bf16[64,2304]{1,0:T(8,128)(2,1)S(1)}, u32[]{:S(2)}, u32[]{:S(2)}) %collective-permute-start.3) | collective-permute-done | bytes 294944 | tf_op jit(solution)/shard_map/ppermute | solution.py:46
  31.3 0.3 collective-permute-start.4
  31.6 2.8 %collective-permute-done.9 = bf16[64,2304]{1,0:T(8,128)(2,1)S(1)} collective-permute-done((bf16[64,2304]{1,0:T(8,128)(2,1)S(1)}, bf16[64,2304]{1,0:T(8,128)(2,1)S(1)}, u32[]{:S(2)}, u32[]{:S(2)}) %collective-permute-start.9) | collective-permute-done | bytes 294944 | tf_op jit(solution)/shard_map/ppermute | solution.py:46
  34.4 0.1 fusion.2
  34.5 0.4 collective-permute-start.10
  34.8 3.3 %collective-permute-start.6 = (bf16[128,2304]{1,0:T(8,128)(2,1)S(1)}, bf16[128,2304]{1,0:T(8,128)(2,1)S(1)}, u32[]{:S(2)}, u32[]{:S(2)}) collective-permute-start(bf16[128,2304]{1,0:T(8,128)(2,1)S(1)} %pad_maximum_fusion.own_ref), channel_id=1, source_target_pairs={{0,2},{1,3},{2,0},{3,1},{4,6},{5,7},{6,4},{7,5},{8,10},{9,11},{10,... | collective-permute-start | bytes 1769480 | tf_op jit(solution)/shard_map/ppermute | solution.py:46
  38.2 3.9 %collective-permute-done.4.own_ref = bf16[128,2304]{1,0:T(8,128)(2,1)S(1)} collective-permute-done((bf16[128,2304]{1,0:T(8,128)(2,1)S(1)}, bf16[128,2304]{1,0:T(8,128)(2,1)S(1)}, u32[]{:S(2)}, u32[]{:S(2)}) %collective-permute-start.4) | collective-permute-done | bytes 589856 | tf_op jit(solution)/shard_map/ppermute | solution.py:46
  42.1 0.9 %collective-permute-start.5 = (bf16[128,2304]{1,0:T(8,128)(2,1)S(1)}, bf16[128,2304]{1,0:T(8,128)(2,1)S(1)}, u32[]{:S(2)}, u32[]{:S(2)}) collective-permute-start(bf16[128,2304]{1,0:T(8,128)(2,1)S(1)} %collective-permute-done.4.own_ref), channel_id=1, source_target_pairs={{0,2},{1,3},{2,0},{3,1},{4,6},{5,7},{6,4},{7,5},{8,10},{9,11},{10,... | collective-permute-start | bytes 1769480 | tf_op jit(solution)/shard_map/ppermute | solution.py:46
  43.0 0.0 collective-permute-done.10
  43.0 1.4 %collective-permute-start.11 = (bf16[32,2304]{1,0:T(8,128)(2,1)S(1)}, bf16[32,2304]{1,0:T(8,128)(2,1)S(1)}, u32[]{:S(2)}, u32[]{:S(2)}) collective-permute-start(bf16[32,2304]{1,0:T(8,128)(2,1)S(1)} %get-tuple-element.16), channel_id=1, source_target_pairs={{0,31},{1,30},{2,29},{3,28},{4,27},{5,26},{6,25},{7,24},{8,23},{9,... | collective-permute-start | bytes 442376 | tf_op jit(solution)/shard_map/ppermute | solution.py:55
  44.4 0.0 collective-permute-done.6.other_ref
  44.4 2.2 %shard_map.62.early_ref = bf16[512,512]{1,0:T(8,128)(2,1)S(1)} custom-call(bf16[512,512]{1,0:T(8,128)(2,1)S(1)} %get-tuple-element.9.direct_ref, bf16[1024,2304]{1,0:T(8,128)(2,1)S(1)} %get-tuple-element.13.windows_ref, bf16[128,2304]{1,0:T(8,128)(2,1)S(1)} %pad_maximum_fusion.own_ref, bf16[128,2304]{1,0:T(8,128)(2,1)S(1)} %collective-permute-done.6.other_ref), custom_call_target="tpu_custom_call" | custom-call | flops 1207959552 | bytes 6946816 | tf_op jit(solution)/shard_map/pallas_call | solution.py:236
  46.7 0.0 collective-permute-done.5.other_ref
  46.7 3.0 %shard_map.63 = bf16[512,512]{1,0:T(8,128)(2,1)} custom-call(bf16[512,512]{1,0:T(8,128)(2,1)S(1)} %get-tuple-element.9.direct_ref, bf16[1024,2304]{1,0:T(8,128)(2,1)S(1)} %get-tuple-element.13.windows_ref, bf16[128,2304]{1,0:T(8,128)(2,1)S(1)} %collective-permute-done.4.own_ref, bf16[128,2304]{1,0:T(8,128)(2,1)S(1)} %collective-permute-done.5.other_ref, ...), custom_call_target="tpu_custom_call" | custom-call | flops 1207959552 | bytes 7471104 | tf_op jit(solution)/shard_map/pallas_call | solution.py:236
  49.7 4.1 %collective-permute-done.11.got_ref = bf16[32,2304]{1,0:T(8,128)(2,1)S(1)} collective-permute-done((bf16[32,2304]{1,0:T(8,128)(2,1)S(1)}, bf16[32,2304]{1,0:T(8,128)(2,1)S(1)}, u32[]{:S(2)}, u32[]{:S(2)}) %collective-permute-start.11) | collective-permute-done | bytes 147488 | tf_op jit(solution)/shard_map/ppermute | solution.py:55
  53.7 1.2 %shard_map.65 = f32[9,16,512]{2,1,0:T(8,128)} custom-call(f32[32,2304]{1,0:T(8,128)S(1)} %get-tuple-element.17.own_ref, bf16[32,2304]{1,0:T(8,128)(2,1)S(1)} %collective-permute-done.11.got_ref), custom_call_target="tpu_custom_call" | custom-call | flops 37748736 | bytes 737280 | tf_op jit(solution)/shard_map/pallas_call | solution.py:236
  (6 shorter events, 0.1 us)
Async XLA Ops:
  1.5 4.6 %collective-permute-start = (bf16[2,4,512]{2,1,0:T(4,128)(2,1)S(1)}, bf16[2,4,512]{2,1,0:T(4,128)(2,1)S(1)}, u32[]{:S(2)}, u32[]{:S(2)}) collective-permute-start(bf16[2,4,512]{2,1,0:T(4,128)(2,1)S(1)} %fusion.19), channel_id=1, source_target_pairs={{0,1},{1,0},{2,3},{3,2},{4,5},{5,4},{6,7},{7,6},{8,9},{9,8},{10,11... | collective-permute-start | bytes 24584 | tf_op jit(solution)/shard_map/ppermute | solution.py:259
  6.1 2.6 %copy-start = (bf16[16,9,512]{2,0,1:T(8,128)(2,1)S(1)}, bf16[16,9,512]{2,0,1:T(8,128)(2,1)}, u32[]{:S(2)}) copy-start(bf16[16,9,512]{2,0,1:T(8,128)(2,1)} %param.7) | copy-start | bytes 442372
  7.7 3.6 %collective-permute-start.7 = (bf16[256,2304]{1,0:T(8,128)(2,1)S(1)}, bf16[256,2304]{1,0:T(8,128)(2,1)S(1)}, u32[]{:S(2)}, u32[]{:S(2)}) collective-permute-start(bf16[256,2304]{1,0:T(8,128)(2,1)S(1)} %get-tuple-element.15), channel_id=1, source_target_pairs={{0,2},{1,3},{2,0},{3,1},{4,6},{5,7},{6,4},{7,5},{8,10},{9,11},{10,... | collective-permute-start | bytes 3538952 | tf_op jit(solution)/shard_map/ppermute | solution.py:46
  8.7 10.6 %collective-permute-start.1 = (bf16[9,16,512]{2,1,0:T(8,128)(2,1)S(1)}, bf16[9,16,512]{2,1,0:T(8,128)(2,1)S(1)}, u32[]{:S(2)}, u32[]{:S(2)}) collective-permute-start(bf16[9,16,512]{2,1,0:T(8,128)(2,1)S(1)} %bitcast.5), channel_id=1, source_target_pairs={{0,31},{1,30},{2,29},{3,28},{4,27},{5,26},{6,25},{7,24},{8,23},{9,... | collective-permute-start | bytes 442376 | tf_op jit(solution)/shard_map/ppermute | solution.py:55
  11.5 14.1 %collective-permute-start.8 = (bf16[128,2304]{1,0:T(8,128)(2,1)S(1)}, bf16[128,2304]{1,0:T(8,128)(2,1)S(1)}, u32[]{:S(2)}, u32[]{:S(2)}) collective-permute-start(bf16[128,2304]{1,0:T(8,128)(2,1)S(1)} %get-tuple-element.18), channel_id=1, source_target_pairs={{0,4},{1,5},{2,3},{3,2},{4,0},{5,1},{6,7},{7,6},{8,12},{9,13},{10,... | collective-permute-start | bytes 1769480 | tf_op jit(solution)/shard_map/ppermute | solution.py:46
  19.9 5.4 %collective-permute-start.2 = (bf16[32,2304]{1,0:T(8,128)(2,1)S(1)}, bf16[32,2304]{1,0:T(8,128)(2,1)S(1)}, u32[]{:S(2)}, u32[]{:S(2)}) collective-permute-start(bf16[32,2304]{1,0:T(8,128)(2,1)S(1)} %shard_map.61), channel_id=1, source_target_pairs={{0,8},{1,9},{2,10},{3,11},{4,12},{5,13},{6,14},{7,15},{8,0},{9,1},... | collective-permute-start | bytes 442376 | tf_op jit(solution)/shard_map/ppermute | solution.py:55
  25.3 5.9 %collective-permute-start.3 = (bf16[64,2304]{1,0:T(8,128)(2,1)S(1)}, bf16[64,2304]{1,0:T(8,128)(2,1)S(1)}, u32[]{:S(2)}, u32[]{:S(2)}) collective-permute-start(bf16[64,2304]{1,0:T(8,128)(2,1)S(1)} %pad_maximum_fusion.1), channel_id=1, source_target_pairs={{0,1},{1,0},{2,6},{3,7},{4,5},{5,4},{6,2},{7,3},{8,9},{9,8},{10,14... | collective-permute-start | bytes 884744 | tf_op jit(solution)/shard_map/ppermute | solution.py:46
  25.6 8.7 %collective-permute-start.9 = (bf16[64,2304]{1,0:T(8,128)(2,1)S(1)}, bf16[64,2304]{1,0:T(8,128)(2,1)S(1)}, u32[]{:S(2)}, u32[]{:S(2)}) collective-permute-start(bf16[64,2304]{1,0:T(8,128)(2,1)S(1)} %fusion.1), channel_id=1, source_target_pairs={{0,1},{1,0},{2,6},{3,7},{4,5},{5,4},{6,2},{7,3},{8,9},{9,8},{10,14... | collective-permute-start | bytes 884744 | tf_op jit(solution)/shard_map/ppermute | solution.py:46
  31.3 10.8 %collective-permute-start.4 = (bf16[128,2304]{1,0:T(8,128)(2,1)S(1)}, bf16[128,2304]{1,0:T(8,128)(2,1)S(1)}, u32[]{:S(2)}, u32[]{:S(2)}) collective-permute-start(bf16[128,2304]{1,0:T(8,128)(2,1)S(1)} %pad_maximum_fusion.own_ref), channel_id=1, source_target_pairs={{0,4},{1,5},{2,3},{3,2},{4,0},{5,1},{6,7},{7,6},{8,12},{9,13},{10,... | collective-permute-start | bytes 1769480 | tf_op jit(solution)/shard_map/ppermute | solution.py:46
  34.5 8.5 %collective-permute-start.10 = (bf16[32,2304]{1,0:T(8,128)(2,1)S(1)}, bf16[32,2304]{1,0:T(8,128)(2,1)S(1)}, u32[]{:S(2)}, u32[]{:S(2)}) collective-permute-start(bf16[32,2304]{1,0:T(8,128)(2,1)S(1)} %slice.87), channel_id=1, source_target_pairs={{0,8},{1,9},{2,10},{3,11},{4,12},{5,13},{6,14},{7,15},{8,0},{9,1},... | collective-permute-start | bytes 442376 | tf_op jit(solution)/shard_map/ppermute | solution.py:55
  34.8 9.6 %collective-permute-start.6 = (bf16[128,2304]{1,0:T(8,128)(2,1)S(1)}, bf16[128,2304]{1,0:T(8,128)(2,1)S(1)}, u32[]{:S(2)}, u32[]{:S(2)}) collective-permute-start(bf16[128,2304]{1,0:T(8,128)(2,1)S(1)} %pad_maximum_fusion.own_ref), channel_id=1, source_target_pairs={{0,2},{1,3},{2,0},{3,1},{4,6},{5,7},{6,4},{7,5},{8,10},{9,11},{10,... | collective-permute-start | bytes 1769480 | tf_op jit(solution)/shard_map/ppermute | solution.py:46
  42.1 4.6 %collective-permute-start.5 = (bf16[128,2304]{1,0:T(8,128)(2,1)S(1)}, bf16[128,2304]{1,0:T(8,128)(2,1)S(1)}, u32[]{:S(2)}, u32[]{:S(2)}) collective-permute-start(bf16[128,2304]{1,0:T(8,128)(2,1)S(1)} %collective-permute-done.4.own_ref), channel_id=1, source_target_pairs={{0,2},{1,3},{2,0},{3,1},{4,6},{5,7},{6,4},{7,5},{8,10},{9,11},{10,... | collective-permute-start | bytes 1769480 | tf_op jit(solution)/shard_map/ppermute | solution.py:46
  43.0 10.7 %collective-permute-start.11 = (bf16[32,2304]{1,0:T(8,128)(2,1)S(1)}, bf16[32,2304]{1,0:T(8,128)(2,1)S(1)}, u32[]{:S(2)}, u32[]{:S(2)}) collective-permute-start(bf16[32,2304]{1,0:T(8,128)(2,1)S(1)} %get-tuple-element.16), channel_id=1, source_target_pairs={{0,31},{1,30},{2,29},{3,28},{4,27},{5,26},{6,25},{7,24},{8,23},{9,... | collective-permute-start | bytes 442376 | tf_op jit(solution)/shard_map/ppermute | solution.py:55

commit v2 on v1

--- a/solution.py
+++ b/solution.py
@@ -189,9 +189,9 @@
     out_ref[...] = placed_sums(group, windows_ref, direct_ref, (own_ref, other_ref), begins).astype(BF16)
 
 
-def late_input_kernel(group, begins, direct_ref, windows_ref, own_ref, other_ref, early_ref, out_ref):
-    late = placed_sums(group, windows_ref, direct_ref, (own_ref, other_ref), begins)
-    out_ref[...] = (early_ref[...].astype(F32) + late).astype(BF16)
+def late_input_kernel(group, begins, direct_ref, windows_ref, early_ref, *refs):
+    late = placed_sums(group, windows_ref, direct_ref, refs[:-1], begins)
+    refs[-1][...] = (early_ref[...].astype(F32) + late).astype(BF16)
 
 
 def reversed_taps(blocks):
@@ -334,20 +334,23 @@
     )
     for place, group in reversed(list(enumerate(plan.groups))):
         gathered = jnp.concatenate([gathered] + [plan.shift(gathered, m) for m in plan.group_masks(group)[1:]], axis=0)
-    gathered = jnp.concatenate([gathered, plan.swap(gathered, "b")], axis=0)
+    size = gathered.shape[0]
+    relayed = plan.swap(gathered, "b")
+    late = [plan.swap(gathered, "a")]
+    late.append(plan.swap(relayed, "a"))
+    gathered = jnp.concatenate([gathered, relayed], axis=0)
     other = plan.swap(gathered, "core")
-    late = plan.swap(gathered, "a")
-    late_other = plan.swap(late, "core")
-    size = gathered.shape[0]
+    for place in range(2):
+        late.append(plan.swap(late[place], "core"))
     early = call(
-        functools.partial(early_input_kernel, 2 * rows, (0, 2 * size)),
+        functools.partial(early_input_kernel, 2 * rows, (0, 4 * size)),
         [((count, width), BF16, True)], (direct, windows, gathered, other),
         flops=work, given=(0, 1, 2, 3),
     )
     grad_input = call(
-        functools.partial(late_input_kernel, 2 * rows, (size, 3 * size)),
-        [((count, width), BF16, False)], (direct, windows, late, late_other, early),
-        flops=work, given=(0, 1, 2, 3, 4),
+        functools.partial(late_input_kernel, 2 * rows, (2 * size, 3 * size, 6 * size, 7 * size)),
+        [((count, width), BF16, False)], (direct, windows, early, *late),
+        flops=work, given=range(7),
     ).reshape(seqs, length, width)
     return grad_input, grad_weight
 

time: 55.2 us -> 58.8 us (1.065)
  the two profiles are of different devices: /device:TPU:13 before, /device:TPU:11 now
where the time goes in v2:
time: 58.8 us; the launch traced here: 58.6 us
  starting transfers between devices  22.4 us (38%)
  waiting for transfers between devices  20.9 us (36%)
  Pallas kernels  13.3 us (23%)
  other arithmetic  1.25 us (2%)
  between operations  0.78 us (1%)
    pallas_call x7, Pallas kernels, call(): pl.pallas_call(kernel, out_shape=[(ON_CHIP if stays else jax.ShapeDtypeSt...  13.3 us
    ppermute x4, waiting for transfers between devices, shift(): return lax.ppermute(block, AXES, [(d, d ^ mask) for d in range(self.count)])  13.1 us
    ppermute x4, starting transfers between devices, shift(): return lax.ppermute(block, AXES, [(d, d ^ mask) for d in range(self.count)])  11.5 us
    ppermute x9, starting transfers between devices, swap(): return lax.ppermute(block, AXES, route)  10.6 us
    ppermute x9, waiting for transfers between devices, swap(): return lax.ppermute(block, AXES, route)  7.78 us
  transfers between devices with their start and end apart: 14, of which 5 were waited for; matrix products, arithmetic and copies ran while one was open for 1% of the time, Pallas kernels for 18%

profile of v2, /device:TPU:11, one launch (start us, length us, event | category | flops | bytes accessed | tf_op | source)
XLA Modules:
  0.0 58.6 jit_solution(11793163039486292608)
XLA Ops:
  0.6 0.8 %fusion.19 = bf16[2,4,512]{2,1,0:T(4,128)(2,1)S(1)} fusion(bf16[2,256,512]{2,1,0:T(8,128)(2,1)} %pre_hbm.1, bf16[2,256,512]{2,1,0:T(8,128)(2,1)} %out_grad_hbm.1, pred[]{:T(512)S(6)} %eq.2), kind=kLoop, calls=%fused_computation.36 | loop fusion | flops 102400 | bytes 40961 | tf_op jit(solution)/shard_map/jit(_where)/select_n | solution.py:259
  1.5 0.3 collective-permute-start
  1.8 3.3 %shard_map.59 = (bf16[256,1024]{1,0:T(8,128)(2,1)S(1)}, bf16[256,1024]{1,0:T(8,128)(2,1)S(1)}, bf16[512,512]{1,0:T(8,128)(2,1)S(1)}, f32[4,272,256]{2,1,0:T(8,128)S(1)}, bf16[1024,2304]{1,0:T(8,128)(2,1)S(1)}) custom-call(s32[1]{0:T(128)} %bitcast.device_ref, bf16[512,512]{1,0:T(8,128)(2,1)} %bitcast.9, bf16[2,256,512]{2,1,0:T(8,128)(2,1)} %pre_hbm.1, ...), custom_call_target="tpu_custom_call" | custom-call | flops 536870912 | bytes 8978432 | tf_op jit(solution)/shard_map/pallas_call | solution.py:236
  5.1 0.0 collective-permute-done
  5.2 0.0 copy-start
  5.2 1.6 %shard_map.60 = (bf16[256,2304]{1,0:T(8,128)(2,1)S(1)}, f32[4,272,256]{2,1,0:T(8,128)S(1)}, bf16[1024,2304]{1,0:T(8,128)(2,1)S(1)}) custom-call(bf16[256,1024]{1,0:T(8,128)(2,1)S(1)} %get-tuple-element.10.order_ref, bf16[2,8,512]{2,1,0:T(8,128)(2,1)S(1)} %pad_maximum_fusion.2.halo_ref, ...), custom_call_target="tpu_custom_call", output_to_operand_aliasing={{1}: (2, {}), {2}: (3, {})} | custom-call | flops 1207959552 | bytes 13385728 | tf_op jit(solution)/shard_map/pallas_call | solution.py:236
  6.7 1.0 %collective-permute-start.9 = (bf16[256,2304]{1,0:T(8,128)(2,1)S(1)}, bf16[256,2304]{1,0:T(8,128)(2,1)S(1)}, u32[]{:S(2)}, u32[]{:S(2)}) collective-permute-start(bf16[256,2304]{1,0:T(8,128)(2,1)S(1)} %get-tuple-element.15), channel_id=1, source_target_pairs={{0,2},{1,3},{2,0},{3,1},{4,6},{5,7},{6,4},{7,5},{8,10},{9,11},{10,... | collective-permute-start | bytes 3538952 | tf_op jit(solution)/shard_map/ppermute | solution.py:46
  7.8 0.0 copy-done
  7.8 3.1 %collective-permute-start.1 = (bf16[9,16,512]{2,1,0:T(8,128)(2,1)S(1)}, bf16[9,16,512]{2,1,0:T(8,128)(2,1)S(1)}, u32[]{:S(2)}, u32[]{:S(2)}) collective-permute-start(bf16[9,16,512]{2,1,0:T(8,128)(2,1)S(1)} %bitcast.5), channel_id=1, source_target_pairs={{0,31},{1,30},{2,29},{3,28},{4,27},{5,26},{6,25},{7,24},{8,23},{9,... | collective-permute-start | bytes 442376 | tf_op jit(solution)/shard_map/ppermute | solution.py:55
  10.9 1.4 %shard_map.64 = f32[256,2304]{1,0:T(8,128)S(1)} custom-call(bf16[256,1024]{1,0:T(8,128)(2,1)S(1)} %get-tuple-element.14.order_ref, bf16[1024,2304]{1,0:T(8,128)(2,1)S(1)} %get-tuple-element.13.windows_ref), custom_call_target="tpu_custom_call" | custom-call | flops 1207959552 | bytes 7602176 | tf_op jit(solution)/shard_map/pallas_call | solution.py:236
  12.3 0.0 collective-permute-done.9
  12.3 0.2 fusion
  12.5 0.3 collective-permute-start.10
  12.8 5.5 %collective-permute-done.1.far_ref = bf16[9,16,512]{2,1,0:T(8,128)(2,1)S(1)} collective-permute-done((bf16[9,16,512]{2,1,0:T(8,128)(2,1)S(1)}, bf16[9,16,512]{2,1,0:T(8,128)(2,1)S(1)}, u32[]{:S(2)}, u32[]{:S(2)}) %collective-permute-start.1) | collective-permute-done | bytes 147488 | tf_op jit(solution)/shard_map/ppermute | solution.py:55
  18.4 0.5 shard_map.61
  18.9 0.1 collective-permute-start.2
  19.0 5.3 %collective-permute-done.2 = bf16[32,2304]{1,0:T(8,128)(2,1)S(1)} collective-permute-done((bf16[32,2304]{1,0:T(8,128)(2,1)S(1)}, bf16[32,2304]{1,0:T(8,128)(2,1)S(1)}, u32[]{:S(2)}, u32[]{:S(2)}) %collective-permute-start.2) | collective-permute-done | bytes 147488 | tf_op jit(solution)/shard_map/ppermute | solution.py:55
  24.3 1.3 %collective-permute-start.3 = (bf16[64,2304]{1,0:T(8,128)(2,1)S(1)}, bf16[64,2304]{1,0:T(8,128)(2,1)S(1)}, u32[]{:S(2)}, u32[]{:S(2)}) collective-permute-start(bf16[64,2304]{1,0:T(8,128)(2,1)S(1)} %pad_maximum_fusion.1), channel_id=1, source_target_pairs={{0,1},{1,0},{2,6},{3,7},{4,5},{5,4},{6,2},{7,3},{8,9},{9,8},{10,14... | collective-permute-start | bytes 884744 | tf_op jit(solution)/shard_map/ppermute | solution.py:46
  25.6 0.0 collective-permute-done.10
  25.6 0.1 fusion.1
  25.7 0.3 collective-permute-start.11
  26.0 1.2 %collective-permute-start.5 = (bf16[64,2304]{1,0:T(8,128)(2,1)S(1)}, bf16[64,2304]{1,0:T(8,128)(2,1)S(1)}, u32[]{:S(2)}, u32[]{:S(2)}) collective-permute-start(bf16[64,2304]{1,0:T(8,128)(2,1)S(1)} %pad_maximum_fusion.1), channel_id=1, source_target_pairs={{0,4},{1,5},{2,3},{3,2},{4,0},{5,1},{6,7},{7,6},{8,12},{9,13},{10,... | collective-permute-start | bytes 884744 | tf_op jit(solution)/shard_map/ppermute | solution.py:46
  27.2 3.1 %collective-permute-done.3 = bf16[64,2304]{1,0:T(8,128)(2,1)S(1)} collective-permute-done((bf16[64,2304]{1,0:T(8,128)(2,1)S(1)}, bf16[64,2304]{1,0:T(8,128)(2,1)S(1)}, u32[]{:S(2)}, u32[]{:S(2)}) %collective-permute-start.3) | collective-permute-done | bytes 294944 | tf_op jit(solution)/shard_map/ppermute | solution.py:46
  30.3 1.2 %collective-permute-start.6 = (bf16[64,2304]{1,0:T(8,128)(2,1)S(1)}, bf16[64,2304]{1,0:T(8,128)(2,1)S(1)}, u32[]{:S(2)}, u32[]{:S(2)}) collective-permute-start(bf16[64,2304]{1,0:T(8,128)(2,1)S(1)} %collective-permute-done.3), channel_id=1, source_target_pairs={{0,4},{1,5},{2,3},{3,2},{4,0},{5,1},{6,7},{7,6},{8,12},{9,13},{10,... | collective-permute-start | bytes 884744 | tf_op jit(solution)/shard_map/ppermute | solution.py:46
  31.5 4.7 %collective-permute-done.11 = bf16[64,2304]{1,0:T(8,128)(2,1)S(1)} collective-permute-done((bf16[64,2304]{1,0:T(8,128)(2,1)S(1)}, bf16[64,2304]{1,0:T(8,128)(2,1)S(1)}, u32[]{:S(2)}, u32[]{:S(2)}) %collective-permute-start.11) | collective-permute-done | bytes 294944 | tf_op jit(solution)/shard_map/ppermute | solution.py:46
  36.2 0.1 fusion.2
  36.3 0.6 %collective-permute-start.12 = (bf16[32,2304]{1,0:T(8,128)(2,1)S(1)}, bf16[32,2304]{1,0:T(8,128)(2,1)S(1)}, u32[]{:S(2)}, u32[]{:S(2)}) collective-permute-start(bf16[32,2304]{1,0:T(8,128)(2,1)S(1)} %slice.87), channel_id=1, source_target_pairs={{0,8},{1,9},{2,10},{3,11},{4,12},{5,13},{6,14},{7,15},{8,0},{9,1},... | collective-permute-start | bytes 442376 | tf_op jit(solution)/shard_map/ppermute | solution.py:55
  37.0 4.7 %collective-permute-start.4 = (bf16[128,2304]{1,0:T(8,128)(2,1)S(1)}, bf16[128,2304]{1,0:T(8,128)(2,1)S(1)}, u32[]{:S(2)}, u32[]{:S(2)}) collective-permute-start(bf16[128,2304]{1,0:T(8,128)(2,1)S(1)} %pad_maximum_fusion.own_ref), channel_id=1, source_target_pairs={{0,2},{1,3},{2,0},{3,1},{4,6},{5,7},{6,4},{7,5},{8,10},{9,11},{10,... | collective-permute-start | bytes 1769480 | tf_op jit(solution)/shard_map/ppermute | solution.py:46
  41.6 0.0 collective-permute-done.5.refs_0_
  41.6 0.1 collective-permute-start.7
  41.7 0.0 collective-permute-done.6.refs_1_
  41.7 0.4 collective-permute-start.8
  42.2 0.0 collective-permute-done.12
  42.2 7.6 %collective-permute-start.13 = (bf16[32,2304]{1,0:T(8,128)(2,1)S(1)}, bf16[32,2304]{1,0:T(8,128)(2,1)S(1)}, u32[]{:S(2)}, u32[]{:S(2)}) collective-permute-start(bf16[32,2304]{1,0:T(8,128)(2,1)S(1)} %get-tuple-element.16), channel_id=1, source_target_pairs={{0,31},{1,30},{2,29},{3,28},{4,27},{5,26},{6,25},{7,24},{8,23},{9,... | collective-permute-start | bytes 442376 | tf_op jit(solution)/shard_map/ppermute | solution.py:55
  49.8 0.0 collective-permute-done.4.other_ref
  49.8 2.2 %shard_map.62.early_ref = bf16[512,512]{1,0:T(8,128)(2,1)S(1)} custom-call(bf16[512,512]{1,0:T(8,128)(2,1)S(1)} %get-tuple-element.9.direct_ref, bf16[1024,2304]{1,0:T(8,128)(2,1)S(1)} %get-tuple-element.13.windows_ref, bf16[128,2304]{1,0:T(8,128)(2,1)S(1)} %pad_maximum_fusion.own_ref, bf16[128,2304]{1,0:T(8,128)(2,1)S(1)} %collective-permute-done.4.other_ref), custom_call_target="tpu_custom_call" | custom-call | flops 1207959552 | bytes 6946816 | tf_op jit(solution)/shard_map/pallas_call | solution.py:236
  52.0 0.0 collective-permute-done.7.refs_2_
  52.1 0.0 collective-permute-done.8.refs_3_
  52.1 3.0 %shard_map.63 = bf16[512,512]{1,0:T(8,128)(2,1)} custom-call(bf16[512,512]{1,0:T(8,128)(2,1)S(1)} %get-tuple-element.9.direct_ref, bf16[1024,2304]{1,0:T(8,128)(2,1)S(1)} %get-tuple-element.13.windows_ref, bf16[512,512]{1,0:T(8,128)(2,1)S(1)} %shard_map.62.early_ref, bf16[64,2304]{1,0:T(8,128)(2,1)S(1)} %collective-permute-done.5.refs_0_, ...), custom_call_target="tpu_custom_call" | custom-call | flops 1207959552 | bytes 7471104 | tf_op jit(solution)/shard_map/pallas_call | solution.py:236
  55.1 2.3 %collective-permute-done.13.got_ref = bf16[32,2304]{1,0:T(8,128)(2,1)S(1)} collective-permute-done((bf16[32,2304]{1,0:T(8,128)(2,1)S(1)}, bf16[32,2304]{1,0:T(8,128)(2,1)S(1)}, u32[]{:S(2)}, u32[]{:S(2)}) %collective-permute-start.13) | collective-permute-done | bytes 147488 | tf_op jit(solution)/shard_map/ppermute | solution.py:55
  57.3 1.2 %shard_map.65 = f32[9,16,512]{2,1,0:T(8,128)} custom-call(f32[32,2304]{1,0:T(8,128)S(1)} %get-tuple-element.17.own_ref, bf16[32,2304]{1,0:T(8,128)(2,1)S(1)} %collective-permute-done.13.got_ref), custom_call_target="tpu_custom_call" | custom-call | flops 37748736 | bytes 737280 | tf_op jit(solution)/shard_map/pallas_call | solution.py:236
  (6 shorter events, 0.1 us)
Async XLA Ops:
  1.5 3.7 %collective-permute-start = (bf16[2,4,512]{2,1,0:T(4,128)(2,1)S(1)}, bf16[2,4,512]{2,1,0:T(4,128)(2,1)S(1)}, u32[]{:S(2)}, u32[]{:S(2)}) collective-permute-start(bf16[2,4,512]{2,1,0:T(4,128)(2,1)S(1)} %fusion.19), channel_id=1, source_target_pairs={{0,1},{1,0},{2,3},{3,2},{4,5},{5,4},{6,7},{7,6},{8,9},{9,8},{10,11... | collective-permute-start | bytes 24584 | tf_op jit(solution)/shard_map/ppermute | solution.py:259
  5.2 2.6 %copy-start = (bf16[16,9,512]{2,0,1:T(8,128)(2,1)S(1)}, bf16[16,9,512]{2,0,1:T(8,128)(2,1)}, u32[]{:S(2)}) copy-start(bf16[16,9,512]{2,0,1:T(8,128)(2,1)} %param.7) | copy-start | bytes 442372
  6.7 5.6 %collective-permute-start.9 = (bf16[256,2304]{1,0:T(8,128)(2,1)S(1)}, bf16[256,2304]{1,0:T(8,128)(2,1)S(1)}, u32[]{:S(2)}, u32[]{:S(2)}) collective-permute-start(bf16[256,2304]{1,0:T(8,128)(2,1)S(1)} %get-tuple-element.15), channel_id=1, source_target_pairs={{0,2},{1,3},{2,0},{3,1},{4,6},{5,7},{6,4},{7,5},{8,10},{9,11},{10,... | collective-permute-start | bytes 3538952 | tf_op jit(solution)/shard_map/ppermute | solution.py:46
  7.8 10.6 %collective-permute-start.1 = (bf16[9,16,512]{2,1,0:T(8,128)(2,1)S(1)}, bf16[9,16,512]{2,1,0:T(8,128)(2,1)S(1)}, u32[]{:S(2)}, u32[]{:S(2)}) collective-permute-start(bf16[9,16,512]{2,1,0:T(8,128)(2,1)S(1)} %bitcast.5), channel_id=1, source_target_pairs={{0,31},{1,30},{2,29},{3,28},{4,27},{5,26},{6,25},{7,24},{8,23},{9,... | collective-permute-start | bytes 442376 | tf_op jit(solution)/shard_map/ppermute | solution.py:55
  12.5 13.1 %collective-permute-start.10 = (bf16[128,2304]{1,0:T(8,128)(2,1)S(1)}, bf16[128,2304]{1,0:T(8,128)(2,1)S(1)}, u32[]{:S(2)}, u32[]{:S(2)}) collective-permute-start(bf16[128,2304]{1,0:T(8,128)(2,1)S(1)} %get-tuple-element.18), channel_id=1, source_target_pairs={{0,4},{1,5},{2,3},{3,2},{4,0},{5,1},{6,7},{7,6},{8,12},{9,13},{10,... | collective-permute-start | bytes 1769480 | tf_op jit(solution)/shard_map/ppermute | solution.py:46
  18.9 5.4 %collective-permute-start.2 = (bf16[32,2304]{1,0:T(8,128)(2,1)S(1)}, bf16[32,2304]{1,0:T(8,128)(2,1)S(1)}, u32[]{:S(2)}, u32[]{:S(2)}) collective-permute-start(bf16[32,2304]{1,0:T(8,128)(2,1)S(1)} %shard_map.61), channel_id=1, source_target_pairs={{0,8},{1,9},{2,10},{3,11},{4,12},{5,13},{6,14},{7,15},{8,0},{9,1},... | collective-permute-start | bytes 442376 | tf_op jit(solution)/shard_map/ppermute | solution.py:55
  24.3 5.9 %collective-permute-start.3 = (bf16[64,2304]{1,0:T(8,128)(2,1)S(1)}, bf16[64,2304]{1,0:T(8,128)(2,1)S(1)}, u32[]{:S(2)}, u32[]{:S(2)}) collective-permute-start(bf16[64,2304]{1,0:T(8,128)(2,1)S(1)} %pad_maximum_fusion.1), channel_id=1, source_target_pairs={{0,1},{1,0},{2,6},{3,7},{4,5},{5,4},{6,2},{7,3},{8,9},{9,8},{10,14... | collective-permute-start | bytes 884744 | tf_op jit(solution)/shard_map/ppermute | solution.py:46
  25.7 10.5 %collective-permute-start.11 = (bf16[64,2304]{1,0:T(8,128)(2,1)S(1)}, bf16[64,2304]{1,0:T(8,128)(2,1)S(1)}, u32[]{:S(2)}, u32[]{:S(2)}) collective-permute-start(bf16[64,2304]{1,0:T(8,128)(2,1)S(1)} %fusion.1), channel_id=1, source_target_pairs={{0,1},{1,0},{2,6},{3,7},{4,5},{5,4},{6,2},{7,3},{8,9},{9,8},{10,14... | collective-permute-start | bytes 884744 | tf_op jit(solution)/shard_map/ppermute | solution.py:46
  26.0 15.7 %collective-permute-start.5 = (bf16[64,2304]{1,0:T(8,128)(2,1)S(1)}, bf16[64,2304]{1,0:T(8,128)(2,1)S(1)}, u32[]{:S(2)}, u32[]{:S(2)}) collective-permute-start(bf16[64,2304]{1,0:T(8,128)(2,1)S(1)} %pad_maximum_fusion.1), channel_id=1, source_target_pairs={{0,4},{1,5},{2,3},{3,2},{4,0},{5,1},{6,7},{7,6},{8,12},{9,13},{10,... | collective-permute-start | bytes 884744 | tf_op jit(solution)/shard_map/ppermute | solution.py:46
  30.3 11.5 %collective-permute-start.6 = (bf16[64,2304]{1,0:T(8,128)(2,1)S(1)}, bf16[64,2304]{1,0:T(8,128)(2,1)S(1)}, u32[]{:S(2)}, u32[]{:S(2)}) collective-permute-start(bf16[64,2304]{1,0:T(8,128)(2,1)S(1)} %collective-permute-done.3), channel_id=1, source_target_pairs={{0,4},{1,5},{2,3},{3,2},{4,0},{5,1},{6,7},{7,6},{8,12},{9,13},{10,... | collective-permute-start | bytes 884744 | tf_op jit(solution)/shard_map/ppermute | solution.py:46
  36.3 5.9 %collective-permute-start.12 = (bf16[32,2304]{1,0:T(8,128)(2,1)S(1)}, bf16[32,2304]{1,0:T(8,128)(2,1)S(1)}, u32[]{:S(2)}, u32[]{:S(2)}) collective-permute-start(bf16[32,2304]{1,0:T(8,128)(2,1)S(1)} %slice.87), channel_id=1, source_target_pairs={{0,8},{1,9},{2,10},{3,11},{4,12},{5,13},{6,14},{7,15},{8,0},{9,1},... | collective-permute-start | bytes 442376 | tf_op jit(solution)/shard_map/ppermute | solution.py:55
  37.0 12.8 %collective-permute-start.4 = (bf16[128,2304]{1,0:T(8,128)(2,1)S(1)}, bf16[128,2304]{1,0:T(8,128)(2,1)S(1)}, u32[]{:S(2)}, u32[]{:S(2)}) collective-permute-start(bf16[128,2304]{1,0:T(8,128)(2,1)S(1)} %pad_maximum_fusion.own_ref), channel_id=1, source_target_pairs={{0,2},{1,3},{2,0},{3,1},{4,6},{5,7},{6,4},{7,5},{8,10},{9,11},{10,... | collective-permute-start | bytes 1769480 | tf_op jit(solution)/shard_map/ppermute | solution.py:46
  41.6 10.4 %collective-permute-start.7 = (bf16[64,2304]{1,0:T(8,128)(2,1)S(1)}, bf16[64,2304]{1,0:T(8,128)(2,1)S(1)}, u32[]{:S(2)}, u32[]{:S(2)}) collective-permute-start(bf16[64,2304]{1,0:T(8,128)(2,1)S(1)} %collective-permute-done.5.refs_0_), channel_id=1, source_target_pairs={{0,2},{1,3},{2,0},{3,1},{4,6},{5,7},{6,4},{7,5},{8,10},{9,11},{10,... | collective-permute-start | bytes 884744 | tf_op jit(solution)/shard_map/ppermute | solution.py:46
  41.7 10.3 %collective-permute-start.8 = (bf16[64,2304]{1,0:T(8,128)(2,1)S(1)}, bf16[64,2304]{1,0:T(8,128)(2,1)S(1)}, u32[]{:S(2)}, u32[]{:S(2)}) collective-permute-start(bf16[64,2304]{1,0:T(8,128)(2,1)S(1)} %collective-permute-done.6.refs_1_), channel_id=1, source_target_pairs={{0,2},{1,3},{2,0},{3,1},{4,6},{5,7},{6,4},{7,5},{8,10},{9,11},{10,... | collective-permute-start | bytes 884744 | tf_op jit(solution)/shard_map/ppermute | solution.py:46
  42.2 15.1 %collective-permute-start.13 = (bf16[32,2304]{1,0:T(8,128)(2,1)S(1)}, bf16[32,2304]{1,0:T(8,128)(2,1)S(1)}, u32[]{:S(2)}, u32[]{:S(2)}) collective-permute-start(bf16[32,2304]{1,0:T(8,128)(2,1)S(1)} %get-tuple-element.16), channel_id=1, source_target_pairs={{0,31},{1,30},{2,29},{3,28},{4,27},{5,26},{6,25},{7,24},{8,23},{9,... | collective-permute-start | bytes 442376 | tf_op jit(solution)/shard_map/ppermute | solution.py:55

commit v3 on v2

--- a/solution.py
+++ b/solution.py
@@ -111,25 +111,25 @@
 
 def prepare_kernel(
     plan, rows, taps, device_ref, values_hbm, pre_hbm, out_grad_hbm,
-    kept_ref, sent_ref, direct_ref, padded_ref, windows_ref,
+    first_ref, second_ref, padded_ref, windows_ref,
     values_ref, pre_ref, out_grad_ref, arrived,
 ):
     seqs, length, width = pre_ref.shape
     half, count = width // 2, seqs * length
-    pairs = ((pre_hbm, pre_ref), (out_grad_hbm, out_grad_ref), (values_hbm, values_ref))
+    pairs = []
+    for b in range(seqs):
+        pairs += [(pre_hbm.at[b], pre_ref.at[b]), (out_grad_hbm.at[b], out_grad_ref.at[b])]
+        if b == 0:
+            pairs.append((values_hbm, values_ref))
     copies = [pltpu.make_async_copy(far, near, arrived.at[i]) for i, (far, near) in enumerate(pairs)]
     for copy in copies:
         copy.start()
     direct, mirror = selection(plan, device_ref[0], rows, width)
-    direct_ref[...] = direct
-    for copy in copies:
-        copy.wait()
-    values = values_ref[...]
-    for out_ref, cut in ((kept_ref, slice(0, half)), (sent_ref, slice(half, width))):
-        out_ref[:, :count] = dot(direct[cut], values, NT).astype(BF16)
-        out_ref[:, count:] = dot(mirror[cut], values, NT).astype(BF16)
     flip = anti_identity(half)
     for b in range(seqs):
+        for copy in copies[:2]:
+            copy.wait()
+        copies = copies[2:]
         grads = grad_pre_of(pre_ref[b], out_grad_ref[b])
         for strand in range(2):
             place = strand * seqs + b
@@ -142,9 +142,19 @@
                 windows_ref[place * length : (place + 1) * length, tap * half : (tap + 1) * half] = (
                     padded_ref[place, start : start + length, :].astype(BF16)
                 )
-
-
-def first_sums_kernel(taps, order_ref, halo_ref, _, __, out_ref, padded_ref, windows_ref):
+        if b == 0:
+            copies.pop(0).wait()
+            values = values_ref[...]
+            quarter = width // 4
+            for out_ref, begins in ((first_ref, (3, 1)), (second_ref, (2, 0))):
+                for place, begin in enumerate(begins):
+                    cut = slice(begin * quarter, (begin + 1) * quarter)
+                    out = slice(place * quarter, (place + 1) * quarter)
+                    out_ref[out, :count] = dot(direct[cut], values, NT).astype(BF16)
+                    out_ref[out, count:] = dot(mirror[cut], values, NT).astype(BF16)
+
+
+def first_sums_kernel(taps, order_ref, halo_ref, _, __, sent_ref, kept_ref, padded_ref, windows_ref):
     seqs, both, width = halo_ref.shape
     half, reach = width // 2, both // 2
     length = padded_ref.shape[1] - 2 * EDGE
@@ -163,35 +173,51 @@
                     windows_ref[
                         place * length + begin : place * length + begin + strip, tap * half : (tap + 1) * half
                     ] = padded_ref[place, start + begin : start + begin + strip, :].astype(BF16)
-    out_ref[...] = dot(order_ref[...], windows_ref[...]).astype(out_ref.dtype)
-
-
-def sums_kernel(order_ref, windows_ref, out_ref):
-    out_ref[...] = dot(order_ref[...], windows_ref[...])
-
-
-def placed_sums(group, windows_ref, direct_ref, weight_refs, begins):
+    sums_kernel(order_ref, windows_ref, sent_ref, kept_ref)
+
+
+def sums_kernel(order_ref, windows_ref, sent_ref, kept_ref):
+    sums = dot(order_ref[...], windows_ref[...])
+    size = sent_ref.shape[0]
+    sent_ref[...] = sums[:size].astype(BF16)
+    kept_ref[...] = sums[size:]
+
+
+def rounded_sums(group, windows_ref, weight_refs):
     count = windows_ref.shape[0] // 2
     weights = jnp.concatenate([ref[...] for ref in weight_refs], axis=0)
-    chosen = jnp.concatenate(
-        [direct_ref[begin : begin + ref.shape[0], :] for ref, begin in zip(weight_refs, begins)], axis=0
-    )
     size = weights.shape[0]
     row = lax.broadcasted_iota(jnp.int32, (size, size), 0)
     col = lax.broadcasted_iota(jnp.int32, (size, size), 1)
     turn = jnp.where(row == (col ^ (group - 1)), 1.0, 0.0).astype(BF16)
     mirrored = dot(turn, weights).astype(BF16)
-    sums = dot(windows_ref[:count, :], weights, NT) + dot(windows_ref[count:, :], mirrored, NT)
-    return dot(sums.astype(BF16), chosen)
-
-
-def early_input_kernel(group, begins, direct_ref, windows_ref, own_ref, other_ref, out_ref):
-    out_ref[...] = placed_sums(group, windows_ref, direct_ref, (own_ref, other_ref), begins).astype(BF16)
-
-
-def late_input_kernel(group, begins, direct_ref, windows_ref, early_ref, *refs):
-    late = placed_sums(group, windows_ref, direct_ref, refs[:-1], begins)
-    refs[-1][...] = (early_ref[...].astype(F32) + late).astype(BF16)
+    return (dot(windows_ref[:count, :], weights, NT) + dot(windows_ref[count:, :], mirrored, NT)).astype(BF16)
+
+
+def chosen_rows(direct, weight_refs, begins):
+    return jnp.concatenate([direct[a : a + ref.shape[0], :] for ref, a in zip(weight_refs, begins)], axis=0)
+
+
+def early_input_kernel(plan, rows, begins, late_begins, device_ref, windows_ref, own_ref, other_ref, out_ref, late_ref):
+    refs = (own_ref, other_ref)
+    direct, _ = selection(plan, device_ref[0], rows, out_ref.shape[1])
+    out_ref[...] = dot(rounded_sums(2 * rows, windows_ref, refs), chosen_rows(direct, refs, begins)).astype(BF16)
+    size = late_ref.shape[0] // len(late_begins)
+    for place, begin in enumerate(late_begins):
+        late_ref[place * size : (place + 1) * size, :] = direct[begin : begin + size, :]
+
+
+def late_input_kernel(group, windows_ref, early_ref, chosen_ref, *refs):
+    weight_refs, (out_hbm, out_ref, stored) = refs[:-3], refs[-3:]
+    sums = rounded_sums(group, windows_ref, weight_refs)
+    half, copies = out_ref.shape[0] // 2, []
+    for place in range(2):
+        cut = slice(place * half, (place + 1) * half)
+        out_ref[cut, :] = (early_ref[cut, :].astype(F32) + dot(sums[cut], chosen_ref[...])).astype(BF16)
+        copies.append(pltpu.make_async_copy(out_ref.at[cut, :], out_hbm.at[cut, :], stored.at[place]))
+        copies[-1].start()
+    for copy in copies:
+        copy.wait()
 
 
 def reversed_taps(blocks):
@@ -239,7 +265,7 @@
         in_specs=[pl.BlockSpec(memory_space=pltpu.SMEM)] * scalars
         + [pl.BlockSpec(memory_space=pltpu.HBM) if i in off_chip else held for i in range(scalars, len(args))],
         scratch_shapes=list(scratch),
-        out_specs=[held] * len(outs),
+        out_specs=[pl.BlockSpec(memory_space=pltpu.HBM) if out[2] is None else held for out in outs],
         input_output_aliases=aliases or {},
         cost_estimate=pl.CostEstimate(
             flops=flops,
@@ -285,30 +311,31 @@
         axis=1,
     )
     halo = edges(ends, reach)
-    kept_order, sent_order, direct, padded, windows = call(
+    first_order, second_order, padded, windows = call(
         functools.partial(prepare_kernel, plan, rows, taps),
         [((half, 2 * count), BF16, True)] * 2
-        + [((width, width), BF16, True)]
         + [((2 * seqs, length + 2 * EDGE, half), F32, True), ((2 * count, depth), BF16, True)],
         (device, inputs.reshape(count, width), pre_act, grad_out),
         scalars=1, flops=4 * count * width * width, off_chip=(1, 2, 3),
         scratch=(
             pltpu.VMEM((count, width), BF16), pltpu.VMEM((seqs, length, width), BF16),
-            pltpu.VMEM((seqs, length, width), BF16), pltpu.SemaphoreType.DMA((3,)),
+            pltpu.VMEM((seqs, length, width), BF16), pltpu.SemaphoreType.DMA((2 * seqs + 1,)),
         ),
     )
-    sent, _, windows = call(
+    sums = [((half // 2, depth), BF16, True), ((half // 2, depth), F32, True)]
+    sent, kept, _, windows = call(
         functools.partial(first_sums_kernel, taps),
-        [((half, depth), BF16, True), (padded.shape, F32, True), (windows.shape, BF16, True)],
-        (sent_order, halo, padded, windows), flops=work, aliases={2: 1, 3: 2}, given=(0, 1, 2, 3),
+        sums + [(padded.shape, F32, True), (windows.shape, BF16, True)],
+        (first_order, halo, padded, windows), flops=work, aliases={2: 2, 3: 3}, given=(0, 1, 2, 3),
     )
     received = plan.swap(sent, "core")
-    kept = call(sums_kernel, [((half, depth), F32, True)], (kept_order, windows), flops=work, given=(0, 1))
-    for stage in ("a", "b"):
-        middle = kept.shape[0] // 2
-        sent = (kept[middle:] + received[middle:].astype(F32)).astype(BF16)
-        kept = kept[:middle] + received[:middle].astype(F32)
-        received = plan.swap(sent, stage)
+    second_sent, second_kept = call(sums_kernel, sums, (second_order, windows), flops=work, given=(0, 1))
+    received = plan.swap((kept + received.astype(F32)).astype(BF16), "a")
+    kept = second_kept + plan.swap(second_sent, "core").astype(F32)
+    middle = kept.shape[0] // 2
+    sent = (kept[middle:] + received[middle:].astype(F32)).astype(BF16)
+    kept = kept[:middle] + received[:middle].astype(F32)
+    received = plan.swap(sent, "b")
     for place, group in enumerate(plan.groups):
         if place == 0:
             kept = kept + received.astype(F32)
@@ -342,15 +369,17 @@
     other = plan.swap(gathered, "core")
     for place in range(2):
         late.append(plan.swap(late[place], "core"))
-    early = call(
-        functools.partial(early_input_kernel, 2 * rows, (0, 4 * size)),
-        [((count, width), BF16, True)], (direct, windows, gathered, other),
-        flops=work, given=(0, 1, 2, 3),
+    begins = (2 * size, 3 * size, 6 * size, 7 * size)
+    early, chosen = call(
+        functools.partial(early_input_kernel, plan, rows, (0, 4 * size), begins),
+        [((count, width), BF16, True), ((half, width), BF16, True)], (device, windows, gathered, other),
+        scalars=1, flops=work, given=(1, 2, 3),
     )
     grad_input = call(
-        functools.partial(late_input_kernel, 2 * rows, (2 * size, 3 * size, 6 * size, 7 * size)),
-        [((count, width), BF16, False)], (direct, windows, early, *late),
+        functools.partial(late_input_kernel, 2 * rows),
+        [((count, width), BF16, None)], (windows, early, chosen, *late),
         flops=work, given=range(7),
+        scratch=(pltpu.VMEM((count, width), BF16), pltpu.SemaphoreType.DMA((2,))),
     ).reshape(seqs, length, width)
     return grad_input, grad_weight
 

time: 58.8 us -> 59.3 us (level); the launches traced: 58.6 us -> 58.2 us
  starting transfers between devices: 22.4 us -> 17 us
  waiting for transfers between devices: 20.9 us -> 25.2 us
  Pallas kernels: 13.3 us -> 13.9 us
    ppermute x9 -> x10, waiting for transfers between devices: 7.78 us -> 18.2 us  [swap(): return lax.ppermute(block, AXES, route)]
    ppermute x4, waiting for transfers between devices: 13.1 us -> 6.98 us  [shift(): return lax.ppermute(block, AXES, [(d, d ^ mask) for d in range(self.count)])]
    ppermute x9 -> x10, starting transfers between devices: 10.6 us -> 7.42 us  [swap(): return lax.ppermute(block, AXES, route)]
    ppermute x4, starting transfers between devices: 11.5 us -> 9.28 us  [shift(): return lax.ppermute(block, AXES, [(d, d ^ mask) for d in range(self.count)])]
    pallas_call x7, Pallas kernels: 13.3 us -> 13.9 us  [call(): pl.pallas_call(kernel, out_shape=[(ON_CHIP if stays else jax.ShapeDtypeSt...]
  transfers between devices with their start and end apart: 14 -> 15, of which waited for: 5 -> 6; matrix products, arithmetic and copies ran while one was open for 1% -> 1% of each run, Pallas kernels for 18% -> 22%
where the time goes in v3:
time: 59.3 us; the launch traced here: 58.2 us
  waiting for transfers between devices  25.2 us (42%)
  starting transfers between devices  17 us (29%)
  Pallas kernels  13.9 us (23%)
  other arithmetic  1.28 us (2%)
  between operations  0.77 us (1%)
    ppermute x10, waiting for transfers between devices, swap(): return lax.ppermute(block, AXES, route)  18.2 us
    pallas_call x7, Pallas kernels, call(): pl.pallas_call(kernel, out_shape=[(ON_CHIP if stays else jax.ShapeDtypeSt...  13.9 us
    ppermute x4, starting transfers between devices, shift(): return lax.ppermute(block, AXES, [(d, d ^ mask) for d in range(self.count)])  9.28 us
    ppermute x10, starting transfers between devices, swap(): return lax.ppermute(block, AXES, route)  7.42 us
    ppermute x4, waiting for transfers between devices, shift(): return lax.ppermute(block, AXES, [(d, d ^ mask) for d in range(self.count)])  6.98 us
  transfers between devices with their start and end apart: 15, of which 6 were waited for; matrix products, arithmetic and copies ran while one was open for 1% of the time, Pallas kernels for 22%

profile of v3, /device:TPU:11, one launch (start us, length us, event | category | flops | bytes accessed | tf_op | source)
XLA Modules:
  0.0 58.2 jit_solution(11725629878175158789)
XLA Ops:
  0.6 0.8 %fusion.18 = bf16[2,4,512]{2,1,0:T(4,128)(2,1)S(1)} fusion(bf16[2,256,512]{2,1,0:T(8,128)(2,1)} %pre_hbm.1, bf16[2,256,512]{2,1,0:T(8,128)(2,1)} %out_grad_hbm.1, pred[]{:T(512)S(6)} %eq.2), kind=kLoop, calls=%fused_computation.35 | loop fusion | flops 102400 | bytes 40961 | tf_op jit(solution)/shard_map/jit(_where)/select_n | solution.py:285
  1.5 0.3 collective-permute-start
  1.8 4.0 %collective-permute-start.1 = (bf16[9,16,512]{2,1,0:T(8,128)(2,1)}, bf16[9,16,512]{2,1,0:T(8,128)(2,1)S(1)}, u32[]{:S(2)}, u32[]{:S(2)}) collective-permute-start(bf16[9,16,512]{2,1,0:T(8,128)(2,1)} %bitcast.5), channel_id=1, source_target_pairs={{0,31},{1,30},{2,29},{3,28},{4,27},{5,26},{6,25},{7,24},{8,23},{9,... | collective-permute-start | bytes 442376 | tf_op jit(solution)/shard_map/ppermute | solution.py:55
  5.8 4.0 %shard_map.59 = (bf16[256,1024]{1,0:T(8,128)(2,1)S(1)}, bf16[256,1024]{1,0:T(8,128)(2,1)S(1)}, f32[4,272,256]{2,1,0:T(8,128)S(1)}, bf16[1024,2304]{1,0:T(8,128)(2,1)S(1)}) custom-call(s32[1]{0:T(128)} %bitcast.device_ref, bf16[512,512]{1,0:T(8,128)(2,1)} %bitcast.9, bf16[2,256,512]{2,1,0:T(8,128)(2,1)} %pre_hbm.1, bf16[2,256,512]{2,1,0:T(8,128)(2,1)} %out_grad_hbm.1), custom_call_target="tpu_custom_call" | custom-call | flops 536870912 | bytes 8454144 | tf_op jit(solution)/shard_map/pallas_call | solution.py:262
  9.8 0.0 collective-permute-done
  9.9 0.0 copy-start
  9.9 1.6 %shard_map.60 = (bf16[128,2304]{1,0:T(8,128)(2,1)S(1)}, f32[128,2304]{1,0:T(8,128)S(1)}, f32[4,272,256]{2,1,0:T(8,128)S(1)}, bf16[1024,2304]{1,0:T(8,128)(2,1)S(1)}) custom-call(bf16[256,1024]{1,0:T(8,128)(2,1)S(1)} %get-tuple-element.13.order_ref, bf16[2,8,512]{2,1,0:T(8,128)(2,1)S(1)} %pad_maximum_fusion.2.halo_ref, ...), custom_call_target="tpu_custom_call", output_to_operand_aliasing={{2}: (2, {}), {3}: (3, {})} | custom-call | flops 1207959552 | bytes 13975552 | tf_op jit(solution)/shard_map/pallas_call | solution.py:262
  11.4 0.1 collective-permute-start.10
  11.5 1.9 %collective-permute-done.1.far_ref = bf16[9,16,512]{2,1,0:T(8,128)(2,1)S(1)} collective-permute-done((bf16[9,16,512]{2,1,0:T(8,128)(2,1)}, bf16[9,16,512]{2,1,0:T(8,128)(2,1)S(1)}, u32[]{:S(2)}, u32[]{:S(2)}) %collective-permute-start.1) | collective-permute-done | bytes 147488 | tf_op jit(solution)/shard_map/ppermute | solution.py:55
  13.4 0.0 copy-done
  13.4 0.5 shard_map.61
  14.0 0.4 collective-permute-start.2
  14.3 1.4 %shard_map.64 = (bf16[128,2304]{1,0:T(8,128)(2,1)S(1)}, f32[128,2304]{1,0:T(8,128)S(1)}) custom-call(bf16[256,1024]{1,0:T(8,128)(2,1)S(1)} %get-tuple-element.19.order_ref, bf16[1024,2304]{1,0:T(8,128)(2,1)S(1)} %get-tuple-element.16.windows_ref), custom_call_target="tpu_custom_call" | custom-call | flops 1207959552 | bytes 7012352 | tf_op jit(solution)/shard_map/pallas_call | solution.py:262
  15.7 0.8 %collective-permute-start.9 = (bf16[128,2304]{1,0:T(8,128)(2,1)S(1)}, bf16[128,2304]{1,0:T(8,128)(2,1)S(1)}, u32[]{:S(2)}, u32[]{:S(2)}) collective-permute-start(bf16[128,2304]{1,0:T(8,128)(2,1)S(1)} %get-tuple-element.21), channel_id=1, source_target_pairs={{0,2},{1,3},{2,0},{3,1},{4,6},{5,7},{6,4},{7,5},{8,10},{9,11},{10,... | collective-permute-start | bytes 1769480 | tf_op jit(solution)/shard_map/ppermute | solution.py:46
  16.6 2.5 %collective-permute-done.2 = bf16[32,2304]{1,0:T(8,128)(2,1)S(1)} collective-permute-done((bf16[32,2304]{1,0:T(8,128)(2,1)S(1)}, bf16[32,2304]{1,0:T(8,128)(2,1)S(1)}, u32[]{:S(2)}, u32[]{:S(2)}) %collective-permute-start.2) | collective-permute-done | bytes 147488 | tf_op jit(solution)/shard_map/ppermute | solution.py:55
  19.1 0.7 %collective-permute-start.3 = (bf16[64,2304]{1,0:T(8,128)(2,1)S(1)}, bf16[64,2304]{1,0:T(8,128)(2,1)S(1)}, u32[]{:S(2)}, u32[]{:S(2)}) collective-permute-start(bf16[64,2304]{1,0:T(8,128)(2,1)S(1)} %pad_maximum_fusion.1), channel_id=1, source_target_pairs={{0,1},{1,0},{2,6},{3,7},{4,5},{5,4},{6,2},{7,3},{8,9},{9,8},{10,14... | collective-permute-start | bytes 884744 | tf_op jit(solution)/shard_map/ppermute | solution.py:46
  19.8 0.0 collective-permute-done.10
  19.8 0.1 add_convert_fusion
  19.9 1.3 %collective-permute-start.11 = (bf16[128,2304]{1,0:T(8,128)(2,1)S(1)}, bf16[128,2304]{1,0:T(8,128)(2,1)S(1)}, u32[]{:S(2)}, u32[]{:S(2)}) collective-permute-start(bf16[128,2304]{1,0:T(8,128)(2,1)S(1)} %add_convert_fusion), channel_id=1, source_target_pairs={{0,4},{1,5},{2,3},{3,2},{4,0},{5,1},{6,7},{7,6},{8,12},{9,13},{10,... | collective-permute-start | bytes 1769480 | tf_op jit(solution)/shard_map/ppermute | solution.py:46
  21.2 0.0 collective-permute-done.9
  21.2 0.1 convert_add_fusion
  21.3 10.6 %collective-permute-done.11 = bf16[128,2304]{1,0:T(8,128)(2,1)S(1)} collective-permute-done((bf16[128,2304]{1,0:T(8,128)(2,1)S(1)}, bf16[128,2304]{1,0:T(8,128)(2,1)S(1)}, u32[]{:S(2)}, u32[]{:S(2)}) %collective-permute-start.11) | collective-permute-done | bytes 589856 | tf_op jit(solution)/shard_map/ppermute | solution.py:46
  31.9 0.1 fusion
  31.9 0.9 %collective-permute-start.12 = (bf16[64,2304]{1,0:T(8,128)(2,1)S(1)}, bf16[64,2304]{1,0:T(8,128)(2,1)S(1)}, u32[]{:S(2)}, u32[]{:S(2)}) collective-permute-start(bf16[64,2304]{1,0:T(8,128)(2,1)S(1)} %fusion), channel_id=1, source_target_pairs={{0,1},{1,0},{2,6},{3,7},{4,5},{5,4},{6,2},{7,3},{8,9},{9,8},{10,14... | collective-permute-start | bytes 884744 | tf_op jit(solution)/shard_map/ppermute | solution.py:46
  32.8 0.6 %collective-permute-start.5 = (bf16[64,2304]{1,0:T(8,128)(2,1)S(1)}, bf16[64,2304]{1,0:T(8,128)(2,1)S(1)}, u32[]{:S(2)}, u32[]{:S(2)}) collective-permute-start(bf16[64,2304]{1,0:T(8,128)(2,1)S(1)} %pad_maximum_fusion.1), channel_id=1, source_target_pairs={{0,4},{1,5},{2,3},{3,2},{4,0},{5,1},{6,7},{7,6},{8,12},{9,13},{10,... | collective-permute-start | bytes 884744 | tf_op jit(solution)/shard_map/ppermute | solution.py:46
  33.4 0.0 collective-permute-done.3
  33.4 0.9 %collective-permute-start.6 = (bf16[64,2304]{1,0:T(8,128)(2,1)S(1)}, bf16[64,2304]{1,0:T(8,128)(2,1)S(1)}, u32[]{:S(2)}, u32[]{:S(2)}) collective-permute-start(bf16[64,2304]{1,0:T(8,128)(2,1)S(1)} %collective-permute-done.3), channel_id=1, source_target_pairs={{0,4},{1,5},{2,3},{3,2},{4,0},{5,1},{6,7},{7,6},{8,12},{9,13},{10,... | collective-permute-start | bytes 884744 | tf_op jit(solution)/shard_map/ppermute | solution.py:46
  34.3 5.5 %collective-permute-done.12 = bf16[64,2304]{1,0:T(8,128)(2,1)S(1)} collective-permute-done((bf16[64,2304]{1,0:T(8,128)(2,1)S(1)}, bf16[64,2304]{1,0:T(8,128)(2,1)S(1)}, u32[]{:S(2)}, u32[]{:S(2)}) %collective-permute-start.12) | collective-permute-done | bytes 294944 | tf_op jit(solution)/shard_map/ppermute | solution.py:46
  39.8 0.1 fusion.1
  39.9 0.4 collective-permute-start.13
  40.3 1.7 %collective-permute-start.4 = (bf16[128,2304]{1,0:T(8,128)(2,1)S(1)}, bf16[128,2304]{1,0:T(8,128)(2,1)S(1)}, u32[]{:S(2)}, u32[]{:S(2)}) collective-permute-start(bf16[128,2304]{1,0:T(8,128)(2,1)S(1)} %pad_maximum_fusion.own_ref), channel_id=1, source_target_pairs={{0,2},{1,3},{2,0},{3,1},{4,6},{5,7},{6,4},{7,5},{8,10},{9,11},{10,... | collective-permute-start | bytes 1769480 | tf_op jit(solution)/shard_map/ppermute | solution.py:46
  42.0 0.0 collective-permute-done.5.refs_0_
  42.0 0.1 collective-permute-start.7
  42.1 2.1 %collective-permute-done.6.refs_1_ = bf16[64,2304]{1,0:T(8,128)(2,1)S(1)} collective-permute-done((bf16[64,2304]{1,0:T(8,128)(2,1)S(1)}, bf16[64,2304]{1,0:T(8,128)(2,1)S(1)}, u32[]{:S(2)}, u32[]{:S(2)}) %collective-permute-start.6) | collective-permute-done | bytes 294944 | tf_op jit(solution)/shard_map/ppermute | solution.py:46
  44.2 0.4 collective-permute-start.8
  44.6 0.0 collective-permute-done.13
  44.6 4.5 %collective-permute-start.14 = (bf16[32,2304]{1,0:T(8,128)(2,1)S(1)}, bf16[32,2304]{1,0:T(8,128)(2,1)S(1)}, u32[]{:S(2)}, u32[]{:S(2)}) collective-permute-start(bf16[32,2304]{1,0:T(8,128)(2,1)S(1)} %get-tuple-element.24), channel_id=1, source_target_pairs={{0,31},{1,30},{2,29},{3,28},{4,27},{5,26},{6,25},{7,24},{8,23},{9,... | collective-permute-start | bytes 442376 | tf_op jit(solution)/shard_map/ppermute | solution.py:55
  49.1 0.0 collective-permute-done.4.other_ref
  49.2 2.3 %shard_map.62 = (bf16[512,512]{1,0:T(8,128)(2,1)S(1)}, bf16[256,512]{1,0:T(8,128)(2,1)S(1)}) custom-call(s32[1]{0:T(128)} %bitcast.device_ref, bf16[1024,2304]{1,0:T(8,128)(2,1)S(1)} %get-tuple-element.16.windows_ref, bf16[128,2304]{1,0:T(8,128)(2,1)S(1)} %pad_maximum_fusion.own_ref, bf16[128,2304]{1,0:T(8,128)(2,1)S(1)} %collective-permute-done.4.other_ref), custom_call_target="tpu_custom_call" | custom-call | flops 1207959552 | bytes 6684672 | tf_op jit(solution)/shard_map/pallas_call | solution.py:262
  51.4 0.0 collective-permute-done.7.refs_2_
  51.5 0.0 collective-permute-done.8.refs_3_
  51.5 2.9 %shard_map.63 = bf16[512,512]{1,0:T(8,128)(2,1)} custom-call(bf16[1024,2304]{1,0:T(8,128)(2,1)S(1)} %get-tuple-element.16.windows_ref, bf16[512,512]{1,0:T(8,128)(2,1)S(1)} %get-tuple-element.17.early_ref, bf16[256,512]{1,0:T(8,128)(2,1)S(1)} %get-tuple-element.18.chosen_ref, bf16[64,2304]{1,0:T(8,128)(2,1)S(1)} %collective-permute-done.5.refs_0_, ...), custom_call_target="tpu_custom_call" | custom-call | flops 1207959552 | bytes 7208960 | tf_op jit(solution)/shard_map/pallas_call | solution.py:262
  54.4 2.6 %collective-permute-done.14.got_ref = bf16[32,2304]{1,0:T(8,128)(2,1)S(1)} collective-permute-done((bf16[32,2304]{1,0:T(8,128)(2,1)S(1)}, bf16[32,2304]{1,0:T(8,128)(2,1)S(1)}, u32[]{:S(2)}, u32[]{:S(2)}) %collective-permute-start.14) | collective-permute-done | bytes 147488 | tf_op jit(solution)/shard_map/ppermute | solution.py:55
  56.9 1.2 %shard_map.65 = f32[9,16,512]{2,1,0:T(8,128)} custom-call(f32[32,2304]{1,0:T(8,128)S(1)} %get-tuple-element.25.own_ref, bf16[32,2304]{1,0:T(8,128)(2,1)S(1)} %collective-permute-done.14.got_ref), custom_call_target="tpu_custom_call" | custom-call | flops 37748736 | bytes 737280 | tf_op jit(solution)/shard_map/pallas_call | solution.py:262
  (6 shorter events, 0.1 us)
Async XLA Ops:
  1.5 8.4 %collective-permute-start = (bf16[2,4,512]{2,1,0:T(4,128)(2,1)S(1)}, bf16[2,4,512]{2,1,0:T(4,128)(2,1)S(1)}, u32[]{:S(2)}, u32[]{:S(2)}) collective-permute-start(bf16[2,4,512]{2,1,0:T(4,128)(2,1)S(1)} %fusion.18), channel_id=1, source_target_pairs={{0,1},{1,0},{2,3},{3,2},{4,5},{5,4},{6,7},{7,6},{8,9},{9,8},{10,11... | collective-permute-start | bytes 24584 | tf_op jit(solution)/shard_map/ppermute | solution.py:285
  1.8 11.7 %collective-permute-start.1 = (bf16[9,16,512]{2,1,0:T(8,128)(2,1)}, bf16[9,16,512]{2,1,0:T(8,128)(2,1)S(1)}, u32[]{:S(2)}, u32[]{:S(2)}) collective-permute-start(bf16[9,16,512]{2,1,0:T(8,128)(2,1)} %bitcast.5), channel_id=1, source_target_pairs={{0,31},{1,30},{2,29},{3,28},{4,27},{5,26},{6,25},{7,24},{8,23},{9,... | collective-permute-start | bytes 442376 | tf_op jit(solution)/shard_map/ppermute | solution.py:55
  9.9 3.6 %copy-start = (bf16[16,9,512]{2,0,1:T(8,128)(2,1)S(1)}, bf16[16,9,512]{2,0,1:T(8,128)(2,1)}, u32[]{:S(2)}) copy-start(bf16[16,9,512]{2,0,1:T(8,128)(2,1)} %param.7) | copy-start | bytes 442372
  11.4 8.4 %collective-permute-start.10 = (bf16[128,2304]{1,0:T(8,128)(2,1)S(1)}, bf16[128,2304]{1,0:T(8,128)(2,1)S(1)}, u32[]{:S(2)}, u32[]{:S(2)}) collective-permute-start(bf16[128,2304]{1,0:T(8,128)(2,1)S(1)} %get-tuple-element.23), channel_id=1, source_target_pairs={{0,2},{1,3},{2,0},{3,1},{4,6},{5,7},{6,4},{7,5},{8,10},{9,11},{10,... | collective-permute-start | bytes 1769480 | tf_op jit(solution)/shard_map/ppermute | solution.py:46
  14.0 5.1 %collective-permute-start.2 = (bf16[32,2304]{1,0:T(8,128)(2,1)S(1)}, bf16[32,2304]{1,0:T(8,128)(2,1)S(1)}, u32[]{:S(2)}, u32[]{:S(2)}) collective-permute-start(bf16[32,2304]{1,0:T(8,128)(2,1)S(1)} %shard_map.61), channel_id=1, source_target_pairs={{0,8},{1,9},{2,10},{3,11},{4,12},{5,13},{6,14},{7,15},{8,0},{9,1},... | collective-permute-start | bytes 442376 | tf_op jit(solution)/shard_map/ppermute | solution.py:55
  15.7 5.5 %collective-permute-start.9 = (bf16[128,2304]{1,0:T(8,128)(2,1)S(1)}, bf16[128,2304]{1,0:T(8,128)(2,1)S(1)}, u32[]{:S(2)}, u32[]{:S(2)}) collective-permute-start(bf16[128,2304]{1,0:T(8,128)(2,1)S(1)} %get-tuple-element.21), channel_id=1, source_target_pairs={{0,2},{1,3},{2,0},{3,1},{4,6},{5,7},{6,4},{7,5},{8,10},{9,11},{10,... | collective-permute-start | bytes 1769480 | tf_op jit(solution)/shard_map/ppermute | solution.py:46
  19.1 14.3 %collective-permute-start.3 = (bf16[64,2304]{1,0:T(8,128)(2,1)S(1)}, bf16[64,2304]{1,0:T(8,128)(2,1)S(1)}, u32[]{:S(2)}, u32[]{:S(2)}) collective-permute-start(bf16[64,2304]{1,0:T(8,128)(2,1)S(1)} %pad_maximum_fusion.1), channel_id=1, source_target_pairs={{0,1},{1,0},{2,6},{3,7},{4,5},{5,4},{6,2},{7,3},{8,9},{9,8},{10,14... | collective-permute-start | bytes 884744 | tf_op jit(solution)/shard_map/ppermute | solution.py:46
  19.9 12.0 %collective-permute-start.11 = (bf16[128,2304]{1,0:T(8,128)(2,1)S(1)}, bf16[128,2304]{1,0:T(8,128)(2,1)S(1)}, u32[]{:S(2)}, u32[]{:S(2)}) collective-permute-start(bf16[128,2304]{1,0:T(8,128)(2,1)S(1)} %add_convert_fusion), channel_id=1, source_target_pairs={{0,4},{1,5},{2,3},{3,2},{4,0},{5,1},{6,7},{7,6},{8,12},{9,13},{10,... | collective-permute-start | bytes 1769480 | tf_op jit(solution)/shard_map/ppermute | solution.py:46
  31.9 7.9 %collective-permute-start.12 = (bf16[64,2304]{1,0:T(8,128)(2,1)S(1)}, bf16[64,2304]{1,0:T(8,128)(2,1)S(1)}, u32[]{:S(2)}, u32[]{:S(2)}) collective-permute-start(bf16[64,2304]{1,0:T(8,128)(2,1)S(1)} %fusion), channel_id=1, source_target_pairs={{0,1},{1,0},{2,6},{3,7},{4,5},{5,4},{6,2},{7,3},{8,9},{9,8},{10,14... | collective-permute-start | bytes 884744 | tf_op jit(solution)/shard_map/ppermute | solution.py:46
  32.8 9.2 %collective-permute-start.5 = (bf16[64,2304]{1,0:T(8,128)(2,1)S(1)}, bf16[64,2304]{1,0:T(8,128)(2,1)S(1)}, u32[]{:S(2)}, u32[]{:S(2)}) collective-permute-start(bf16[64,2304]{1,0:T(8,128)(2,1)S(1)} %pad_maximum_fusion.1), channel_id=1, source_target_pairs={{0,4},{1,5},{2,3},{3,2},{4,0},{5,1},{6,7},{7,6},{8,12},{9,13},{10,... | collective-permute-start | bytes 884744 | tf_op jit(solution)/shard_map/ppermute | solution.py:46
  33.4 10.8 %collective-permute-start.6 = (bf16[64,2304]{1,0:T(8,128)(2,1)S(1)}, bf16[64,2304]{1,0:T(8,128)(2,1)S(1)}, u32[]{:S(2)}, u32[]{:S(2)}) collective-permute-start(bf16[64,2304]{1,0:T(8,128)(2,1)S(1)} %collective-permute-done.3), channel_id=1, source_target_pairs={{0,4},{1,5},{2,3},{3,2},{4,0},{5,1},{6,7},{7,6},{8,12},{9,13},{10,... | collective-permute-start | bytes 884744 | tf_op jit(solution)/shard_map/ppermute | solution.py:46
  39.9 4.7 %collective-permute-start.13 = (bf16[32,2304]{1,0:T(8,128)(2,1)S(1)}, bf16[32,2304]{1,0:T(8,128)(2,1)S(1)}, u32[]{:S(2)}, u32[]{:S(2)}) collective-permute-start(bf16[32,2304]{1,0:T(8,128)(2,1)S(1)} %slice.61), channel_id=1, source_target_pairs={{0,8},{1,9},{2,10},{3,11},{4,12},{5,13},{6,14},{7,15},{8,0},{9,1},... | collective-permute-start | bytes 442376 | tf_op jit(solution)/shard_map/ppermute | solution.py:55
  40.3 8.9 %collective-permute-start.4 = (bf16[128,2304]{1,0:T(8,128)(2,1)S(1)}, bf16[128,2304]{1,0:T(8,128)(2,1)S(1)}, u32[]{:S(2)}, u32[]{:S(2)}) collective-permute-start(bf16[128,2304]{1,0:T(8,128)(2,1)S(1)} %pad_maximum_fusion.own_ref), channel_id=1, source_target_pairs={{0,2},{1,3},{2,0},{3,1},{4,6},{5,7},{6,4},{7,5},{8,10},{9,11},{10,... | collective-permute-start | bytes 1769480 | tf_op jit(solution)/shard_map/ppermute | solution.py:46
  42.0 9.4 %collective-permute-start.7 = (bf16[64,2304]{1,0:T(8,128)(2,1)S(1)}, bf16[64,2304]{1,0:T(8,128)(2,1)S(1)}, u32[]{:S(2)}, u32[]{:S(2)}) collective-permute-start(bf16[64,2304]{1,0:T(8,128)(2,1)S(1)} %collective-permute-done.5.refs_0_), channel_id=1, source_target_pairs={{0,2},{1,3},{2,0},{3,1},{4,6},{5,7},{6,4},{7,5},{8,10},{9,11},{10,... | collective-permute-start | bytes 884744 | tf_op jit(solution)/shard_map/ppermute | solution.py:46
  44.2 7.2 %collective-permute-start.8 = (bf16[64,2304]{1,0:T(8,128)(2,1)S(1)}, bf16[64,2304]{1,0:T(8,128)(2,1)S(1)}, u32[]{:S(2)}, u32[]{:S(2)}) collective-permute-start(bf16[64,2304]{1,0:T(8,128)(2,1)S(1)} %collective-permute-done.6.refs_1_), channel_id=1, source_target_pairs={{0,2},{1,3},{2,0},{3,1},{4,6},{5,7},{6,4},{7,5},{8,10},{9,11},{10,... | collective-permute-start | bytes 884744 | tf_op jit(solution)/shard_map/ppermute | solution.py:46
  44.6 12.3 %collective-permute-start.14 = (bf16[32,2304]{1,0:T(8,128)(2,1)S(1)}, bf16[32,2304]{1,0:T(8,128)(2,1)S(1)}, u32[]{:S(2)}, u32[]{:S(2)}) collective-permute-start(bf16[32,2304]{1,0:T(8,128)(2,1)S(1)} %get-tuple-element.24), channel_id=1, source_target_pairs={{0,31},{1,30},{2,29},{3,28},{4,27},{5,26},{6,25},{7,24},{8,23},{9,... | collective-permute-start | bytes 442376 | tf_op jit(solution)/shard_map/ppermute | solution.py:55

commit v4 on v3

--- a/solution.py
+++ b/solution.py
@@ -116,20 +116,23 @@
 ):
     seqs, length, width = pre_ref.shape
     half, count = width // 2, seqs * length
-    pairs = []
-    for b in range(seqs):
-        pairs += [(pre_hbm.at[b], pre_ref.at[b]), (out_grad_hbm.at[b], out_grad_ref.at[b])]
-        if b == 0:
-            pairs.append((values_hbm, values_ref))
+    pairs = ((pre_hbm, pre_ref), (out_grad_hbm, out_grad_ref), (values_hbm, values_ref))
     copies = [pltpu.make_async_copy(far, near, arrived.at[i]) for i, (far, near) in enumerate(pairs)]
     for copy in copies:
         copy.start()
     direct, mirror = selection(plan, device_ref[0], rows, width)
+    for copy in copies:
+        copy.wait()
+    values = values_ref[...]
+    quarter = width // 4
+    for out_ref, begins in ((first_ref, (3, 1)), (second_ref, (2, 0))):
+        for place, begin in enumerate(begins):
+            cut = slice(begin * quarter, (begin + 1) * quarter)
+            out = slice(place * quarter, (place + 1) * quarter)
+            out_ref[out, :count] = dot(direct[cut], values, NT).astype(BF16)
+            out_ref[out, count:] = dot(mirror[cut], values, NT).astype(BF16)
     flip = anti_identity(half)
     for b in range(seqs):
-        for copy in copies[:2]:
-            copy.wait()
-        copies = copies[2:]
         grads = grad_pre_of(pre_ref[b], out_grad_ref[b])
         for strand in range(2):
             place = strand * seqs + b
@@ -142,16 +145,6 @@
                 windows_ref[place * length : (place + 1) * length, tap * half : (tap + 1) * half] = (
                     padded_ref[place, start : start + length, :].astype(BF16)
                 )
-        if b == 0:
-            copies.pop(0).wait()
-            values = values_ref[...]
-            quarter = width // 4
-            for out_ref, begins in ((first_ref, (3, 1)), (second_ref, (2, 0))):
-                for place, begin in enumerate(begins):
-                    cut = slice(begin * quarter, (begin + 1) * quarter)
-                    out = slice(place * quarter, (place + 1) * quarter)
-                    out_ref[out, :count] = dot(direct[cut], values, NT).astype(BF16)
-                    out_ref[out, count:] = dot(mirror[cut], values, NT).astype(BF16)
 
 
 def first_sums_kernel(taps, order_ref, halo_ref, _, __, sent_ref, kept_ref, padded_ref, windows_ref):
@@ -319,7 +312,7 @@
         scalars=1, flops=4 * count * width * width, off_chip=(1, 2, 3),
         scratch=(
             pltpu.VMEM((count, width), BF16), pltpu.VMEM((seqs, length, width), BF16),
-            pltpu.VMEM((seqs, length, width), BF16), pltpu.SemaphoreType.DMA((2 * seqs + 1,)),
+            pltpu.VMEM((seqs, length, width), BF16), pltpu.SemaphoreType.DMA((3,)),
         ),
     )
     sums = [((half // 2, depth), BF16, True), ((half // 2, depth), F32, True)]

time: 59.3 us -> 59.2 us (level)
  no operation moved by 1% of the time
where the time goes in v4:
time: 59.2 us; the launch traced here: 58.2 us
  waiting for transfers between devices  24.9 us (42%)
  starting transfers between devices  17.2 us (29%)
  Pallas kernels  14 us (24%)
  other arithmetic  1.28 us (2%)
  between operations  0.77 us (1%)
    ppermute x10, waiting for transfers between devices, swap(): return lax.ppermute(block, AXES, route)  18.1 us
    pallas_call x7, Pallas kernels, call(): pl.pallas_call(kernel, out_shape=[(ON_CHIP if stays else jax.ShapeDtypeSt...  14 us
    ppermute x4, starting transfers between devices, shift(): return lax.ppermute(block, AXES, [(d, d ^ mask) for d in range(self.count)])  9.35 us
    ppermute x10, starting transfers between devices, swap(): return lax.ppermute(block, AXES, route)  7.5 us
    ppermute x4, waiting for transfers between devices, shift(): return lax.ppermute(block, AXES, [(d, d ^ mask) for d in range(self.count)])  6.82 us
  transfers between devices with their start and end apart: 15, of which 6 were waited for; matrix products, arithmetic and copies ran while one was open for 1% of the time, Pallas kernels for 22%

profile of v4, /device:TPU:11, one launch (start us, length us, event | category | flops | bytes accessed | tf_op | source)
XLA Modules:
  0.0 58.2 jit_solution(11185946350620115039)
XLA Ops:
  0.6 0.8 %fusion.18 = bf16[2,4,512]{2,1,0:T(4,128)(2,1)S(1)} fusion(bf16[2,256,512]{2,1,0:T(8,128)(2,1)} %pre_hbm.1, bf16[2,256,512]{2,1,0:T(8,128)(2,1)} %out_grad_hbm.1, pred[]{:T(512)S(6)} %eq.2), kind=kLoop, calls=%fused_computation.35 | loop fusion | flops 102400 | bytes 40961 | tf_op jit(solution)/shard_map/jit(_where)/select_n | solution.py:278
  1.5 0.3 collective-permute-start
  1.8 4.0 %collective-permute-start.1 = (bf16[9,16,512]{2,1,0:T(8,128)(2,1)}, bf16[9,16,512]{2,1,0:T(8,128)(2,1)S(1)}, u32[]{:S(2)}, u32[]{:S(2)}) collective-permute-start(bf16[9,16,512]{2,1,0:T(8,128)(2,1)} %bitcast.5), channel_id=1, source_target_pairs={{0,31},{1,30},{2,29},{3,28},{4,27},{5,26},{6,25},{7,24},{8,23},{9,... | collective-permute-start | bytes 442376 | tf_op jit(solution)/shard_map/ppermute | solution.py:55
  5.8 4.1 %shard_map.59 = (bf16[256,1024]{1,0:T(8,128)(2,1)S(1)}, bf16[256,1024]{1,0:T(8,128)(2,1)S(1)}, f32[4,272,256]{2,1,0:T(8,128)S(1)}, bf16[1024,2304]{1,0:T(8,128)(2,1)S(1)}) custom-call(s32[1]{0:T(128)} %bitcast.device_ref, bf16[512,512]{1,0:T(8,128)(2,1)} %bitcast.9, bf16[2,256,512]{2,1,0:T(8,128)(2,1)} %pre_hbm.1, bf16[2,256,512]{2,1,0:T(8,128)(2,1)} %out_grad_hbm.1), custom_call_target="tpu_custom_call" | custom-call | flops 536870912 | bytes 8454144 | tf_op jit(solution)/shard_map/pallas_call | solution.py:255
  9.9 0.0 collective-permute-done
  10.0 0.0 copy-start
  10.0 1.6 %shard_map.60 = (bf16[128,2304]{1,0:T(8,128)(2,1)S(1)}, f32[128,2304]{1,0:T(8,128)S(1)}, f32[4,272,256]{2,1,0:T(8,128)S(1)}, bf16[1024,2304]{1,0:T(8,128)(2,1)S(1)}) custom-call(bf16[256,1024]{1,0:T(8,128)(2,1)S(1)} %get-tuple-element.13.order_ref, bf16[2,8,512]{2,1,0:T(8,128)(2,1)S(1)} %pad_maximum_fusion.2.halo_ref, ...), custom_call_target="tpu_custom_call", output_to_operand_aliasing={{2}: (2, {}), {3}: (3, {})} | custom-call | flops 1207959552 | bytes 13975552 | tf_op jit(solution)/shard_map/pallas_call | solution.py:255
  11.5 0.1 collective-permute-start.10
  11.6 1.8 %collective-permute-done.1.far_ref = bf16[9,16,512]{2,1,0:T(8,128)(2,1)S(1)} collective-permute-done((bf16[9,16,512]{2,1,0:T(8,128)(2,1)}, bf16[9,16,512]{2,1,0:T(8,128)(2,1)S(1)}, u32[]{:S(2)}, u32[]{:S(2)}) %collective-permute-start.1) | collective-permute-done | bytes 147488 | tf_op jit(solution)/shard_map/ppermute | solution.py:55
  13.4 0.0 copy-done
  13.4 0.5 shard_map.61
  14.0 0.4 collective-permute-start.2
  14.4 1.4 %shard_map.64 = (bf16[128,2304]{1,0:T(8,128)(2,1)S(1)}, f32[128,2304]{1,0:T(8,128)S(1)}) custom-call(bf16[256,1024]{1,0:T(8,128)(2,1)S(1)} %get-tuple-element.19.order_ref, bf16[1024,2304]{1,0:T(8,128)(2,1)S(1)} %get-tuple-element.16.windows_ref), custom_call_target="tpu_custom_call" | custom-call | flops 1207959552 | bytes 7012352 | tf_op jit(solution)/shard_map/pallas_call | solution.py:255
  15.8 0.8 %collective-permute-start.9 = (bf16[128,2304]{1,0:T(8,128)(2,1)S(1)}, bf16[128,2304]{1,0:T(8,128)(2,1)S(1)}, u32[]{:S(2)}, u32[]{:S(2)}) collective-permute-start(bf16[128,2304]{1,0:T(8,128)(2,1)S(1)} %get-tuple-element.21), channel_id=1, source_target_pairs={{0,2},{1,3},{2,0},{3,1},{4,6},{5,7},{6,4},{7,5},{8,10},{9,11},{10,... | collective-permute-start | bytes 1769480 | tf_op jit(solution)/shard_map/ppermute | solution.py:46
  16.6 2.4 %collective-permute-done.2 = bf16[32,2304]{1,0:T(8,128)(2,1)S(1)} collective-permute-done((bf16[32,2304]{1,0:T(8,128)(2,1)S(1)}, bf16[32,2304]{1,0:T(8,128)(2,1)S(1)}, u32[]{:S(2)}, u32[]{:S(2)}) %collective-permute-start.2) | collective-permute-done | bytes 147488 | tf_op jit(solution)/shard_map/ppermute | solution.py:55
  19.1 0.7 %collective-permute-start.3 = (bf16[64,2304]{1,0:T(8,128)(2,1)S(1)}, bf16[64,2304]{1,0:T(8,128)(2,1)S(1)}, u32[]{:S(2)}, u32[]{:S(2)}) collective-permute-start(bf16[64,2304]{1,0:T(8,128)(2,1)S(1)} %pad_maximum_fusion.1), channel_id=1, source_target_pairs={{0,1},{1,0},{2,6},{3,7},{4,5},{5,4},{6,2},{7,3},{8,9},{9,8},{10,14... | collective-permute-start | bytes 884744 | tf_op jit(solution)/shard_map/ppermute | solution.py:46
  19.8 0.0 collective-permute-done.10
  19.8 0.1 add_convert_fusion
  19.9 1.3 %collective-permute-start.11 = (bf16[128,2304]{1,0:T(8,128)(2,1)S(1)}, bf16[128,2304]{1,0:T(8,128)(2,1)S(1)}, u32[]{:S(2)}, u32[]{:S(2)}) collective-permute-start(bf16[128,2304]{1,0:T(8,128)(2,1)S(1)} %add_convert_fusion), channel_id=1, source_target_pairs={{0,4},{1,5},{2,3},{3,2},{4,0},{5,1},{6,7},{7,6},{8,12},{9,13},{10,... | collective-permute-start | bytes 1769480 | tf_op jit(solution)/shard_map/ppermute | solution.py:46
  21.2 0.0 collective-permute-done.9
  21.2 0.1 convert_add_fusion
  21.3 10.6 %collective-permute-done.11 = bf16[128,2304]{1,0:T(8,128)(2,1)S(1)} collective-permute-done((bf16[128,2304]{1,0:T(8,128)(2,1)S(1)}, bf16[128,2304]{1,0:T(8,128)(2,1)S(1)}, u32[]{:S(2)}, u32[]{:S(2)}) %collective-permute-start.11) | collective-permute-done | bytes 589856 | tf_op jit(solution)/shard_map/ppermute | solution.py:46
  31.9 0.1 fusion
  31.9 0.9 %collective-permute-start.12 = (bf16[64,2304]{1,0:T(8,128)(2,1)S(1)}, bf16[64,2304]{1,0:T(8,128)(2,1)S(1)}, u32[]{:S(2)}, u32[]{:S(2)}) collective-permute-start(bf16[64,2304]{1,0:T(8,128)(2,1)S(1)} %fusion), channel_id=1, source_target_pairs={{0,1},{1,0},{2,6},{3,7},{4,5},{5,4},{6,2},{7,3},{8,9},{9,8},{10,14... | collective-permute-start | bytes 884744 | tf_op jit(solution)/shard_map/ppermute | solution.py:46
  32.8 0.6 %collective-permute-start.5 = (bf16[64,2304]{1,0:T(8,128)(2,1)S(1)}, bf16[64,2304]{1,0:T(8,128)(2,1)S(1)}, u32[]{:S(2)}, u32[]{:S(2)}) collective-permute-start(bf16[64,2304]{1,0:T(8,128)(2,1)S(1)} %pad_maximum_fusion.1), channel_id=1, source_target_pairs={{0,4},{1,5},{2,3},{3,2},{4,0},{5,1},{6,7},{7,6},{8,12},{9,13},{10,... | collective-permute-start | bytes 884744 | tf_op jit(solution)/shard_map/ppermute | solution.py:46
  33.4 0.0 collective-permute-done.3
  33.4 0.9 %collective-permute-start.6 = (bf16[64,2304]{1,0:T(8,128)(2,1)S(1)}, bf16[64,2304]{1,0:T(8,128)(2,1)S(1)}, u32[]{:S(2)}, u32[]{:S(2)}) collective-permute-start(bf16[64,2304]{1,0:T(8,128)(2,1)S(1)} %collective-permute-done.3), channel_id=1, source_target_pairs={{0,4},{1,5},{2,3},{3,2},{4,0},{5,1},{6,7},{7,6},{8,12},{9,13},{10,... | collective-permute-start | bytes 884744 | tf_op jit(solution)/shard_map/ppermute | solution.py:46
  34.3 5.5 %collective-permute-done.12 = bf16[64,2304]{1,0:T(8,128)(2,1)S(1)} collective-permute-done((bf16[64,2304]{1,0:T(8,128)(2,1)S(1)}, bf16[64,2304]{1,0:T(8,128)(2,1)S(1)}, u32[]{:S(2)}, u32[]{:S(2)}) %collective-permute-start.12) | collective-permute-done | bytes 294944 | tf_op jit(solution)/shard_map/ppermute | solution.py:46
  39.8 0.1 fusion.1
  39.9 0.4 collective-permute-start.13
  40.3 1.8 %collective-permute-start.4 = (bf16[128,2304]{1,0:T(8,128)(2,1)S(1)}, bf16[128,2304]{1,0:T(8,128)(2,1)S(1)}, u32[]{:S(2)}, u32[]{:S(2)}) collective-permute-start(bf16[128,2304]{1,0:T(8,128)(2,1)S(1)} %pad_maximum_fusion.own_ref), channel_id=1, source_target_pairs={{0,2},{1,3},{2,0},{3,1},{4,6},{5,7},{6,4},{7,5},{8,10},{9,11},{10,... | collective-permute-start | bytes 1769480 | tf_op jit(solution)/shard_map/ppermute | solution.py:46
  42.1 0.0 collective-permute-done.5.refs_0_
  42.1 0.1 collective-permute-start.7
  42.2 2.0 %collective-permute-done.6.refs_1_ = bf16[64,2304]{1,0:T(8,128)(2,1)S(1)} collective-permute-done((bf16[64,2304]{1,0:T(8,128)(2,1)S(1)}, bf16[64,2304]{1,0:T(8,128)(2,1)S(1)}, u32[]{:S(2)}, u32[]{:S(2)}) %collective-permute-start.6) | collective-permute-done | bytes 294944 | tf_op jit(solution)/shard_map/ppermute | solution.py:46
  44.2 0.4 collective-permute-start.8
  44.6 0.0 collective-permute-done.13
  44.6 4.5 %collective-permute-start.14 = (bf16[32,2304]{1,0:T(8,128)(2,1)S(1)}, bf16[32,2304]{1,0:T(8,128)(2,1)S(1)}, u32[]{:S(2)}, u32[]{:S(2)}) collective-permute-start(bf16[32,2304]{1,0:T(8,128)(2,1)S(1)} %get-tuple-element.24), channel_id=1, source_target_pairs={{0,31},{1,30},{2,29},{3,28},{4,27},{5,26},{6,25},{7,24},{8,23},{9,... | collective-permute-start | bytes 442376 | tf_op jit(solution)/shard_map/ppermute | solution.py:55
  49.1 0.0 collective-permute-done.4.other_ref
  49.2 2.3 %shard_map.62 = (bf16[512,512]{1,0:T(8,128)(2,1)S(1)}, bf16[256,512]{1,0:T(8,128)(2,1)S(1)}) custom-call(s32[1]{0:T(128)} %bitcast.device_ref, bf16[1024,2304]{1,0:T(8,128)(2,1)S(1)} %get-tuple-element.16.windows_ref, bf16[128,2304]{1,0:T(8,128)(2,1)S(1)} %pad_maximum_fusion.own_ref, bf16[128,2304]{1,0:T(8,128)(2,1)S(1)} %collective-permute-done.4.other_ref), custom_call_target="tpu_custom_call" | custom-call | flops 1207959552 | bytes 6684672 | tf_op jit(solution)/shard_map/pallas_call | solution.py:255
  51.4 0.0 collective-permute-done.7.refs_2_
  51.5 0.0 collective-permute-done.8.refs_3_
  51.5 2.9 %shard_map.63 = bf16[512,512]{1,0:T(8,128)(2,1)} custom-call(bf16[1024,2304]{1,0:T(8,128)(2,1)S(1)} %get-tuple-element.16.windows_ref, bf16[512,512]{1,0:T(8,128)(2,1)S(1)} %get-tuple-element.17.early_ref, bf16[256,512]{1,0:T(8,128)(2,1)S(1)} %get-tuple-element.18.chosen_ref, bf16[64,2304]{1,0:T(8,128)(2,1)S(1)} %collective-permute-done.5.refs_0_, ...), custom_call_target="tpu_custom_call" | custom-call | flops 1207959552 | bytes 7208960 | tf_op jit(solution)/shard_map/pallas_call | solution.py:255
  54.4 2.6 %collective-permute-done.14.got_ref = bf16[32,2304]{1,0:T(8,128)(2,1)S(1)} collective-permute-done((bf16[32,2304]{1,0:T(8,128)(2,1)S(1)}, bf16[32,2304]{1,0:T(8,128)(2,1)S(1)}, u32[]{:S(2)}, u32[]{:S(2)}) %collective-permute-start.14) | collective-permute-done | bytes 147488 | tf_op jit(solution)/shard_map/ppermute | solution.py:55
  56.9 1.2 %shard_map.65 = f32[9,16,512]{2,1,0:T(8,128)} custom-call(f32[32,2304]{1,0:T(8,128)S(1)} %get-tuple-element.25.own_ref, bf16[32,2304]{1,0:T(8,128)(2,1)S(1)} %collective-permute-done.14.got_ref), custom_call_target="tpu_custom_call" | custom-call | flops 37748736 | bytes 737280 | tf_op jit(solution)/shard_map/pallas_call | solution.py:255
  (6 shorter events, 0.1 us)
Async XLA Ops:
  1.5 8.4 %collective-permute-start = (bf16[2,4,512]{2,1,0:T(4,128)(2,1)S(1)}, bf16[2,4,512]{2,1,0:T(4,128)(2,1)S(1)}, u32[]{:S(2)}, u32[]{:S(2)}) collective-permute-start(bf16[2,4,512]{2,1,0:T(4,128)(2,1)S(1)} %fusion.18), channel_id=1, source_target_pairs={{0,1},{1,0},{2,3},{3,2},{4,5},{5,4},{6,7},{7,6},{8,9},{9,8},{10,11... | collective-permute-start | bytes 24584 | tf_op jit(solution)/shard_map/ppermute | solution.py:278
  1.8 11.7 %collective-permute-start.1 = (bf16[9,16,512]{2,1,0:T(8,128)(2,1)}, bf16[9,16,512]{2,1,0:T(8,128)(2,1)S(1)}, u32[]{:S(2)}, u32[]{:S(2)}) collective-permute-start(bf16[9,16,512]{2,1,0:T(8,128)(2,1)} %bitcast.5), channel_id=1, source_target_pairs={{0,31},{1,30},{2,29},{3,28},{4,27},{5,26},{6,25},{7,24},{8,23},{9,... | collective-permute-start | bytes 442376 | tf_op jit(solution)/shard_map/ppermute | solution.py:55
  10.0 3.5 %copy-start = (bf16[16,9,512]{2,0,1:T(8,128)(2,1)S(1)}, bf16[16,9,512]{2,0,1:T(8,128)(2,1)}, u32[]{:S(2)}) copy-start(bf16[16,9,512]{2,0,1:T(8,128)(2,1)} %param.7) | copy-start | bytes 442372
  11.5 8.3 %collective-permute-start.10 = (bf16[128,2304]{1,0:T(8,128)(2,1)S(1)}, bf16[128,2304]{1,0:T(8,128)(2,1)S(1)}, u32[]{:S(2)}, u32[]{:S(2)}) collective-permute-start(bf16[128,2304]{1,0:T(8,128)(2,1)S(1)} %get-tuple-element.23), channel_id=1, source_target_pairs={{0,2},{1,3},{2,0},{3,1},{4,6},{5,7},{6,4},{7,5},{8,10},{9,11},{10,... | collective-permute-start | bytes 1769480 | tf_op jit(solution)/shard_map/ppermute | solution.py:46
  14.0 5.1 %collective-permute-start.2 = (bf16[32,2304]{1,0:T(8,128)(2,1)S(1)}, bf16[32,2304]{1,0:T(8,128)(2,1)S(1)}, u32[]{:S(2)}, u32[]{:S(2)}) collective-permute-start(bf16[32,2304]{1,0:T(8,128)(2,1)S(1)} %shard_map.61), channel_id=1, source_target_pairs={{0,8},{1,9},{2,10},{3,11},{4,12},{5,13},{6,14},{7,15},{8,0},{9,1},... | collective-permute-start | bytes 442376 | tf_op jit(solution)/shard_map/ppermute | solution.py:55
  15.8 5.4 %collective-permute-start.9 = (bf16[128,2304]{1,0:T(8,128)(2,1)S(1)}, bf16[128,2304]{1,0:T(8,128)(2,1)S(1)}, u32[]{:S(2)}, u32[]{:S(2)}) collective-permute-start(bf16[128,2304]{1,0:T(8,128)(2,1)S(1)} %get-tuple-element.21), channel_id=1, source_target_pairs={{0,2},{1,3},{2,0},{3,1},{4,6},{5,7},{6,4},{7,5},{8,10},{9,11},{10,... | collective-permute-start | bytes 1769480 | tf_op jit(solution)/shard_map/ppermute | solution.py:46
  19.1 14.3 %collective-permute-start.3 = (bf16[64,2304]{1,0:T(8,128)(2,1)S(1)}, bf16[64,2304]{1,0:T(8,128)(2,1)S(1)}, u32[]{:S(2)}, u32[]{:S(2)}) collective-permute-start(bf16[64,2304]{1,0:T(8,128)(2,1)S(1)} %pad_maximum_fusion.1), channel_id=1, source_target_pairs={{0,1},{1,0},{2,6},{3,7},{4,5},{5,4},{6,2},{7,3},{8,9},{9,8},{10,14... | collective-permute-start | bytes 884744 | tf_op jit(solution)/shard_map/ppermute | solution.py:46
  19.9 12.0 %collective-permute-start.11 = (bf16[128,2304]{1,0:T(8,128)(2,1)S(1)}, bf16[128,2304]{1,0:T(8,128)(2,1)S(1)}, u32[]{:S(2)}, u32[]{:S(2)}) collective-permute-start(bf16[128,2304]{1,0:T(8,128)(2,1)S(1)} %add_convert_fusion), channel_id=1, source_target_pairs={{0,4},{1,5},{2,3},{3,2},{4,0},{5,1},{6,7},{7,6},{8,12},{9,13},{10,... | collective-permute-start | bytes 1769480 | tf_op jit(solution)/shard_map/ppermute | solution.py:46
  31.9 7.9 %collective-permute-start.12 = (bf16[64,2304]{1,0:T(8,128)(2,1)S(1)}, bf16[64,2304]{1,0:T(8,128)(2,1)S(1)}, u32[]{:S(2)}, u32[]{:S(2)}) collective-permute-start(bf16[64,2304]{1,0:T(8,128)(2,1)S(1)} %fusion), channel_id=1, source_target_pairs={{0,1},{1,0},{2,6},{3,7},{4,5},{5,4},{6,2},{7,3},{8,9},{9,8},{10,14... | collective-permute-start | bytes 884744 | tf_op jit(solution)/shard_map/ppermute | solution.py:46
  32.8 9.3 %collective-permute-start.5 = (bf16[64,2304]{1,0:T(8,128)(2,1)S(1)}, bf16[64,2304]{1,0:T(8,128)(2,1)S(1)}, u32[]{:S(2)}, u32[]{:S(2)}) collective-permute-start(bf16[64,2304]{1,0:T(8,128)(2,1)S(1)} %pad_maximum_fusion.1), channel_id=1, source_target_pairs={{0,4},{1,5},{2,3},{3,2},{4,0},{5,1},{6,7},{7,6},{8,12},{9,13},{10,... | collective-permute-start | bytes 884744 | tf_op jit(solution)/shard_map/ppermute | solution.py:46
  33.4 10.8 %collective-permute-start.6 = (bf16[64,2304]{1,0:T(8,128)(2,1)S(1)}, bf16[64,2304]{1,0:T(8,128)(2,1)S(1)}, u32[]{:S(2)}, u32[]{:S(2)}) collective-permute-start(bf16[64,2304]{1,0:T(8,128)(2,1)S(1)} %collective-permute-done.3), channel_id=1, source_target_pairs={{0,4},{1,5},{2,3},{3,2},{4,0},{5,1},{6,7},{7,6},{8,12},{9,13},{10,... | collective-permute-start | bytes 884744 | tf_op jit(solution)/shard_map/ppermute | solution.py:46
  39.9 4.7 %collective-permute-start.13 = (bf16[32,2304]{1,0:T(8,128)(2,1)S(1)}, bf16[32,2304]{1,0:T(8,128)(2,1)S(1)}, u32[]{:S(2)}, u32[]{:S(2)}) collective-permute-start(bf16[32,2304]{1,0:T(8,128)(2,1)S(1)} %slice.61), channel_id=1, source_target_pairs={{0,8},{1,9},{2,10},{3,11},{4,12},{5,13},{6,14},{7,15},{8,0},{9,1},... | collective-permute-start | bytes 442376 | tf_op jit(solution)/shard_map/ppermute | solution.py:55
  40.3 8.9 %collective-permute-start.4 = (bf16[128,2304]{1,0:T(8,128)(2,1)S(1)}, bf16[128,2304]{1,0:T(8,128)(2,1)S(1)}, u32[]{:S(2)}, u32[]{:S(2)}) collective-permute-start(bf16[128,2304]{1,0:T(8,128)(2,1)S(1)} %pad_maximum_fusion.own_ref), channel_id=1, source_target_pairs={{0,2},{1,3},{2,0},{3,1},{4,6},{5,7},{6,4},{7,5},{8,10},{9,11},{10,... | collective-permute-start | bytes 1769480 | tf_op jit(solution)/shard_map/ppermute | solution.py:46
  42.1 9.3 %collective-permute-start.7 = (bf16[64,2304]{1,0:T(8,128)(2,1)S(1)}, bf16[64,2304]{1,0:T(8,128)(2,1)S(1)}, u32[]{:S(2)}, u32[]{:S(2)}) collective-permute-start(bf16[64,2304]{1,0:T(8,128)(2,1)S(1)} %collective-permute-done.5.refs_0_), channel_id=1, source_target_pairs={{0,2},{1,3},{2,0},{3,1},{4,6},{5,7},{6,4},{7,5},{8,10},{9,11},{10,... | collective-permute-start | bytes 884744 | tf_op jit(solution)/shard_map/ppermute | solution.py:46
  44.2 7.2 %collective-permute-start.8 = (bf16[64,2304]{1,0:T(8,128)(2,1)S(1)}, bf16[64,2304]{1,0:T(8,128)(2,1)S(1)}, u32[]{:S(2)}, u32[]{:S(2)}) collective-permute-start(bf16[64,2304]{1,0:T(8,128)(2,1)S(1)} %collective-permute-done.6.refs_1_), channel_id=1, source_target_pairs={{0,2},{1,3},{2,0},{3,1},{4,6},{5,7},{6,4},{7,5},{8,10},{9,11},{10,... | collective-permute-start | bytes 884744 | tf_op jit(solution)/shard_map/ppermute | solution.py:46
  44.6 12.3 %collective-permute-start.14 = (bf16[32,2304]{1,0:T(8,128)(2,1)S(1)}, bf16[32,2304]{1,0:T(8,128)(2,1)S(1)}, u32[]{:S(2)}, u32[]{:S(2)}) collective-permute-start(bf16[32,2304]{1,0:T(8,128)(2,1)S(1)} %get-tuple-element.24), channel_id=1, source_target_pairs={{0,31},{1,30},{2,29},{3,28},{4,27},{5,26},{6,25},{7,24},{8,23},{9,... | collective-permute-start | bytes 442376 | tf_op jit(solution)/shard_map/ppermute | solution.py:55

commit v5 on v4

--- a/solution.py
+++ b/solution.py
@@ -125,12 +125,11 @@
         copy.wait()
     values = values_ref[...]
     quarter = width // 4
-    for out_ref, begins in ((first_ref, (3, 1)), (second_ref, (2, 0))):
-        for place, begin in enumerate(begins):
-            cut = slice(begin * quarter, (begin + 1) * quarter)
-            out = slice(place * quarter, (place + 1) * quarter)
-            out_ref[out, :count] = dot(direct[cut], values, NT).astype(BF16)
-            out_ref[out, count:] = dot(mirror[cut], values, NT).astype(BF16)
+    for chosen, cols in ((direct, slice(0, count)), (mirror, slice(count, 2 * count))):
+        ordered = dot(chosen, values, NT).astype(BF16)
+        for out_ref, begins in ((first_ref, (3, 1)), (second_ref, (2, 0))):
+            for place, begin in enumerate(begins):
+                out_ref[place * quarter : (place + 1) * quarter, cols] = ordered[begin * quarter : (begin + 1) * quarter]
     flip = anti_identity(half)
     for b in range(seqs):
         grads = grad_pre_of(pre_ref[b], out_grad_ref[b])

time: 59.2 us -> 59.2 us (level)
  waiting for transfers between devices: 24.9 us -> 26.4 us
  starting transfers between devices: 17.2 us -> 16.4 us
  Pallas kernels: 14 us -> 13.3 us
    ppermute x4, waiting for transfers between devices: 6.82 us -> 8.29 us  [shift(): return lax.ppermute(block, AXES, [(d, d ^ mask) for d in range(self.count)])]
    pallas_call x7, Pallas kernels: 14 us -> 13.3 us  [call(): pl.pallas_call(kernel, out_shape=[(ON_CHIP if stays else jax.ShapeDtypeSt...]
  transfers between devices with their start and end apart: 15 -> 15, of which waited for: 6 -> 6; matrix products, arithmetic and copies ran while one was open for 1% -> 1% of each run, Pallas kernels for 22% -> 21%
where the time goes in v5:
time: 59.2 us; the launch traced here: 58.2 us
  waiting for transfers between devices  26.4 us (45%)
  starting transfers between devices  16.4 us (28%)
  Pallas kernels  13.3 us (22%)
  other arithmetic  1.28 us (2%)
  between operations  0.78 us (1%)
    ppermute x10, waiting for transfers between devices, swap(): return lax.ppermute(block, AXES, route)  18.1 us
    pallas_call x7, Pallas kernels, call(): pl.pallas_call(kernel, out_shape=[(ON_CHIP if stays else jax.ShapeDtypeSt...  13.3 us
    ppermute x4, starting transfers between devices, shift(): return lax.ppermute(block, AXES, [(d, d ^ mask) for d in range(self.count)])  8.99 us
    ppermute x4, waiting for transfers between devices, shift(): return lax.ppermute(block, AXES, [(d, d ^ mask) for d in range(self.count)])  8.29 us
    ppermute x10, starting transfers between devices, swap(): return lax.ppermute(block, AXES, route)  7.14 us
  transfers between devices with their start and end apart: 15, of which 6 were waited for; matrix products, arithmetic and copies ran while one was open for 1% of the time, Pallas kernels for 21%

profile of v5, /device:TPU:11, one launch (start us, length us, event | category | flops | bytes accessed | tf_op | source)
XLA Modules:
  0.0 58.2 jit_solution(8993807189161037479)
XLA Ops:
  0.6 0.8 %fusion.18 = bf16[2,4,512]{2,1,0:T(4,128)(2,1)S(1)} fusion(bf16[2,256,512]{2,1,0:T(8,128)(2,1)} %pre_hbm.1, bf16[2,256,512]{2,1,0:T(8,128)(2,1)} %out_grad_hbm.1, pred[]{:T(512)S(6)} %eq.2), kind=kLoop, calls=%fused_computation.35 | loop fusion | flops 102400 | bytes 40961 | tf_op jit(solution)/shard_map/jit(_where)/select_n | solution.py:277
  1.5 0.3 collective-permute-start
  1.8 4.0 %collective-permute-start.1 = (bf16[9,16,512]{2,1,0:T(8,128)(2,1)}, bf16[9,16,512]{2,1,0:T(8,128)(2,1)S(1)}, u32[]{:S(2)}, u32[]{:S(2)}) collective-permute-start(bf16[9,16,512]{2,1,0:T(8,128)(2,1)} %bitcast.5), channel_id=1, source_target_pairs={{0,31},{1,30},{2,29},{3,28},{4,27},{5,26},{6,25},{7,24},{8,23},{9,... | collective-permute-start | bytes 442376 | tf_op jit(solution)/shard_map/ppermute | solution.py:55
  5.8 3.3 %shard_map.59 = (bf16[256,1024]{1,0:T(8,128)(2,1)S(1)}, bf16[256,1024]{1,0:T(8,128)(2,1)S(1)}, f32[4,272,256]{2,1,0:T(8,128)S(1)}, bf16[1024,2304]{1,0:T(8,128)(2,1)S(1)}) custom-call(s32[1]{0:T(128)} %bitcast.device_ref, bf16[512,512]{1,0:T(8,128)(2,1)} %bitcast.9, bf16[2,256,512]{2,1,0:T(8,128)(2,1)} %pre_hbm.1, bf16[2,256,512]{2,1,0:T(8,128)(2,1)} %out_grad_hbm.1), custom_call_target="tpu_custom_call" | custom-call | flops 536870912 | bytes 8454144 | tf_op jit(solution)/shard_map/pallas_call | solution.py:254
  9.1 0.0 collective-permute-done
  9.2 0.0 copy-start
  9.2 1.6 %shard_map.60 = (bf16[128,2304]{1,0:T(8,128)(2,1)S(1)}, f32[128,2304]{1,0:T(8,128)S(1)}, f32[4,272,256]{2,1,0:T(8,128)S(1)}, bf16[1024,2304]{1,0:T(8,128)(2,1)S(1)}) custom-call(bf16[256,1024]{1,0:T(8,128)(2,1)S(1)} %get-tuple-element.13.order_ref, bf16[2,8,512]{2,1,0:T(8,128)(2,1)S(1)} %pad_maximum_fusion.2.halo_ref, ...), custom_call_target="tpu_custom_call", output_to_operand_aliasing={{2}: (2, {}), {3}: (3, {})} | custom-call | flops 1207959552 | bytes 13975552 | tf_op jit(solution)/shard_map/pallas_call | solution.py:254
  10.8 0.1 collective-permute-start.10
  10.8 2.6 %collective-permute-done.1.far_ref = bf16[9,16,512]{2,1,0:T(8,128)(2,1)S(1)} collective-permute-done((bf16[9,16,512]{2,1,0:T(8,128)(2,1)}, bf16[9,16,512]{2,1,0:T(8,128)(2,1)S(1)}, u32[]{:S(2)}, u32[]{:S(2)}) %collective-permute-start.1) | collective-permute-done | bytes 147488 | tf_op jit(solution)/shard_map/ppermute | solution.py:55
  13.4 0.0 copy-done
  13.4 0.5 shard_map.61
  14.0 0.1 collective-permute-start.2
  14.1 1.4 %shard_map.64 = (bf16[128,2304]{1,0:T(8,128)(2,1)S(1)}, f32[128,2304]{1,0:T(8,128)S(1)}) custom-call(bf16[256,1024]{1,0:T(8,128)(2,1)S(1)} %get-tuple-element.19.order_ref, bf16[1024,2304]{1,0:T(8,128)(2,1)S(1)} %get-tuple-element.16.windows_ref), custom_call_target="tpu_custom_call" | custom-call | flops 1207959552 | bytes 7012352 | tf_op jit(solution)/shard_map/pallas_call | solution.py:254
  15.5 0.5 collective-permute-start.9
  15.9 3.1 %collective-permute-done.2 = bf16[32,2304]{1,0:T(8,128)(2,1)S(1)} collective-permute-done((bf16[32,2304]{1,0:T(8,128)(2,1)S(1)}, bf16[32,2304]{1,0:T(8,128)(2,1)S(1)}, u32[]{:S(2)}, u32[]{:S(2)}) %collective-permute-start.2) | collective-permute-done | bytes 147488 | tf_op jit(solution)/shard_map/ppermute | solution.py:55
  19.1 0.7 %collective-permute-start.3 = (bf16[64,2304]{1,0:T(8,128)(2,1)S(1)}, bf16[64,2304]{1,0:T(8,128)(2,1)S(1)}, u32[]{:S(2)}, u32[]{:S(2)}) collective-permute-start(bf16[64,2304]{1,0:T(8,128)(2,1)S(1)} %pad_maximum_fusion.1), channel_id=1, source_target_pairs={{0,1},{1,0},{2,6},{3,7},{4,5},{5,4},{6,2},{7,3},{8,9},{9,8},{10,14... | collective-permute-start | bytes 884744 | tf_op jit(solution)/shard_map/ppermute | solution.py:46
  19.8 0.0 collective-permute-done.10
  19.8 0.1 add_convert_fusion
  19.9 1.3 %collective-permute-start.11 = (bf16[128,2304]{1,0:T(8,128)(2,1)S(1)}, bf16[128,2304]{1,0:T(8,128)(2,1)S(1)}, u32[]{:S(2)}, u32[]{:S(2)}) collective-permute-start(bf16[128,2304]{1,0:T(8,128)(2,1)S(1)} %add_convert_fusion), channel_id=1, source_target_pairs={{0,4},{1,5},{2,3},{3,2},{4,0},{5,1},{6,7},{7,6},{8,12},{9,13},{10,... | collective-permute-start | bytes 1769480 | tf_op jit(solution)/shard_map/ppermute | solution.py:46
  21.2 0.0 collective-permute-done.9
  21.2 0.1 convert_add_fusion
  21.3 10.6 %collective-permute-done.11 = bf16[128,2304]{1,0:T(8,128)(2,1)S(1)} collective-permute-done((bf16[128,2304]{1,0:T(8,128)(2,1)S(1)}, bf16[128,2304]{1,0:T(8,128)(2,1)S(1)}, u32[]{:S(2)}, u32[]{:S(2)}) %collective-permute-start.11) | collective-permute-done | bytes 589856 | tf_op jit(solution)/shard_map/ppermute | solution.py:46
  31.9 0.1 fusion
  31.9 0.9 %collective-permute-start.12 = (bf16[64,2304]{1,0:T(8,128)(2,1)S(1)}, bf16[64,2304]{1,0:T(8,128)(2,1)S(1)}, u32[]{:S(2)}, u32[]{:S(2)}) collective-permute-start(bf16[64,2304]{1,0:T(8,128)(2,1)S(1)} %fusion), channel_id=1, source_target_pairs={{0,1},{1,0},{2,6},{3,7},{4,5},{5,4},{6,2},{7,3},{8,9},{9,8},{10,14... | collective-permute-start | bytes 884744 | tf_op jit(solution)/shard_map/ppermute | solution.py:46
  32.8 0.6 %collective-permute-start.5 = (bf16[64,2304]{1,0:T(8,128)(2,1)S(1)}, bf16[64,2304]{1,0:T(8,128)(2,1)S(1)}, u32[]{:S(2)}, u32[]{:S(2)}) collective-permute-start(bf16[64,2304]{1,0:T(8,128)(2,1)S(1)} %pad_maximum_fusion.1), channel_id=1, source_target_pairs={{0,4},{1,5},{2,3},{3,2},{4,0},{5,1},{6,7},{7,6},{8,12},{9,13},{10,... | collective-permute-start | bytes 884744 | tf_op jit(solution)/shard_map/ppermute | solution.py:46
  33.4 0.0 collective-permute-done.3
  33.4 0.9 %collective-permute-start.6 = (bf16[64,2304]{1,0:T(8,128)(2,1)S(1)}, bf16[64,2304]{1,0:T(8,128)(2,1)S(1)}, u32[]{:S(2)}, u32[]{:S(2)}) collective-permute-start(bf16[64,2304]{1,0:T(8,128)(2,1)S(1)} %collective-permute-done.3), channel_id=1, source_target_pairs={{0,4},{1,5},{2,3},{3,2},{4,0},{5,1},{6,7},{7,6},{8,12},{9,13},{10,... | collective-permute-start | bytes 884744 | tf_op jit(solution)/shard_map/ppermute | solution.py:46
  34.3 5.5 %collective-permute-done.12 = bf16[64,2304]{1,0:T(8,128)(2,1)S(1)} collective-permute-done((bf16[64,2304]{1,0:T(8,128)(2,1)S(1)}, bf16[64,2304]{1,0:T(8,128)(2,1)S(1)}, u32[]{:S(2)}, u32[]{:S(2)}) %collective-permute-start.12) | collective-permute-done | bytes 294944 | tf_op jit(solution)/shard_map/ppermute | solution.py:46
  39.8 0.1 fusion.1
  39.9 0.4 collective-permute-start.13
  40.3 1.8 %collective-permute-start.4 = (bf16[128,2304]{1,0:T(8,128)(2,1)S(1)}, bf16[128,2304]{1,0:T(8,128)(2,1)S(1)}, u32[]{:S(2)}, u32[]{:S(2)}) collective-permute-start(bf16[128,2304]{1,0:T(8,128)(2,1)S(1)} %pad_maximum_fusion.own_ref), channel_id=1, source_target_pairs={{0,2},{1,3},{2,0},{3,1},{4,6},{5,7},{6,4},{7,5},{8,10},{9,11},{10,... | collective-permute-start | bytes 1769480 | tf_op jit(solution)/shard_map/ppermute | solution.py:46
  42.1 0.0 collective-permute-done.5.refs_0_
  42.1 0.1 collective-permute-start.7
  42.2 2.0 %collective-permute-done.6.refs_1_ = bf16[64,2304]{1,0:T(8,128)(2,1)S(1)} collective-permute-done((bf16[64,2304]{1,0:T(8,128)(2,1)S(1)}, bf16[64,2304]{1,0:T(8,128)(2,1)S(1)}, u32[]{:S(2)}, u32[]{:S(2)}) %collective-permute-start.6) | collective-permute-done | bytes 294944 | tf_op jit(solution)/shard_map/ppermute | solution.py:46
  44.2 0.4 collective-permute-start.8
  44.6 0.0 collective-permute-done.13
  44.6 4.5 %collective-permute-start.14 = (bf16[32,2304]{1,0:T(8,128)(2,1)S(1)}, bf16[32,2304]{1,0:T(8,128)(2,1)S(1)}, u32[]{:S(2)}, u32[]{:S(2)}) collective-permute-start(bf16[32,2304]{1,0:T(8,128)(2,1)S(1)} %get-tuple-element.24), channel_id=1, source_target_pairs={{0,31},{1,30},{2,29},{3,28},{4,27},{5,26},{6,25},{7,24},{8,23},{9,... | collective-permute-start | bytes 442376 | tf_op jit(solution)/shard_map/ppermute | solution.py:55
  49.1 0.0 collective-permute-done.4.other_ref
  49.2 2.3 %shard_map.62 = (bf16[512,512]{1,0:T(8,128)(2,1)S(1)}, bf16[256,512]{1,0:T(8,128)(2,1)S(1)}) custom-call(s32[1]{0:T(128)} %bitcast.device_ref, bf16[1024,2304]{1,0:T(8,128)(2,1)S(1)} %get-tuple-element.16.windows_ref, bf16[128,2304]{1,0:T(8,128)(2,1)S(1)} %pad_maximum_fusion.own_ref, bf16[128,2304]{1,0:T(8,128)(2,1)S(1)} %collective-permute-done.4.other_ref), custom_call_target="tpu_custom_call" | custom-call | flops 1207959552 | bytes 6684672 | tf_op jit(solution)/shard_map/pallas_call | solution.py:254
  51.4 0.0 collective-permute-done.7.refs_2_
  51.5 0.0 collective-permute-done.8.refs_3_
  51.5 2.9 %shard_map.63 = bf16[512,512]{1,0:T(8,128)(2,1)} custom-call(bf16[1024,2304]{1,0:T(8,128)(2,1)S(1)} %get-tuple-element.16.windows_ref, bf16[512,512]{1,0:T(8,128)(2,1)S(1)} %get-tuple-element.17.early_ref, bf16[256,512]{1,0:T(8,128)(2,1)S(1)} %get-tuple-element.18.chosen_ref, bf16[64,2304]{1,0:T(8,128)(2,1)S(1)} %collective-permute-done.5.refs_0_, ...), custom_call_target="tpu_custom_call" | custom-call | flops 1207959552 | bytes 7208960 | tf_op jit(solution)/shard_map/pallas_call | solution.py:254
  54.4 2.6 %collective-permute-done.14.got_ref = bf16[32,2304]{1,0:T(8,128)(2,1)S(1)} collective-permute-done((bf16[32,2304]{1,0:T(8,128)(2,1)S(1)}, bf16[32,2304]{1,0:T(8,128)(2,1)S(1)}, u32[]{:S(2)}, u32[]{:S(2)}) %collective-permute-start.14) | collective-permute-done | bytes 147488 | tf_op jit(solution)/shard_map/ppermute | solution.py:55
  56.9 1.2 %shard_map.65 = f32[9,16,512]{2,1,0:T(8,128)} custom-call(f32[32,2304]{1,0:T(8,128)S(1)} %get-tuple-element.25.own_ref, bf16[32,2304]{1,0:T(8,128)(2,1)S(1)} %collective-permute-done.14.got_ref), custom_call_target="tpu_custom_call" | custom-call | flops 37748736 | bytes 737280 | tf_op jit(solution)/shard_map/pallas_call | solution.py:254
  (6 shorter events, 0.1 us)
Async XLA Ops:
  1.5 7.7 %collective-permute-start = (bf16[2,4,512]{2,1,0:T(4,128)(2,1)S(1)}, bf16[2,4,512]{2,1,0:T(4,128)(2,1)S(1)}, u32[]{:S(2)}, u32[]{:S(2)}) collective-permute-start(bf16[2,4,512]{2,1,0:T(4,128)(2,1)S(1)} %fusion.18), channel_id=1, source_target_pairs={{0,1},{1,0},{2,3},{3,2},{4,5},{5,4},{6,7},{7,6},{8,9},{9,8},{10,11... | collective-permute-start | bytes 24584 | tf_op jit(solution)/shard_map/ppermute | solution.py:277
  1.8 11.7 %collective-permute-start.1 = (bf16[9,16,512]{2,1,0:T(8,128)(2,1)}, bf16[9,16,512]{2,1,0:T(8,128)(2,1)S(1)}, u32[]{:S(2)}, u32[]{:S(2)}) collective-permute-start(bf16[9,16,512]{2,1,0:T(8,128)(2,1)} %bitcast.5), channel_id=1, source_target_pairs={{0,31},{1,30},{2,29},{3,28},{4,27},{5,26},{6,25},{7,24},{8,23},{9,... | collective-permute-start | bytes 442376 | tf_op jit(solution)/shard_map/ppermute | solution.py:55
  9.2 4.2 %copy-start = (bf16[16,9,512]{2,0,1:T(8,128)(2,1)S(1)}, bf16[16,9,512]{2,0,1:T(8,128)(2,1)}, u32[]{:S(2)}) copy-start(bf16[16,9,512]{2,0,1:T(8,128)(2,1)} %param.7) | copy-start | bytes 442372
  10.8 9.0 %collective-permute-start.10 = (bf16[128,2304]{1,0:T(8,128)(2,1)S(1)}, bf16[128,2304]{1,0:T(8,128)(2,1)S(1)}, u32[]{:S(2)}, u32[]{:S(2)}) collective-permute-start(bf16[128,2304]{1,0:T(8,128)(2,1)S(1)} %get-tuple-element.23), channel_id=1, source_target_pairs={{0,2},{1,3},{2,0},{3,1},{4,6},{5,7},{6,4},{7,5},{8,10},{9,11},{10,... | collective-permute-start | bytes 1769480 | tf_op jit(solution)/shard_map/ppermute | solution.py:46
  14.0 5.1 %collective-permute-start.2 = (bf16[32,2304]{1,0:T(8,128)(2,1)S(1)}, bf16[32,2304]{1,0:T(8,128)(2,1)S(1)}, u32[]{:S(2)}, u32[]{:S(2)}) collective-permute-start(bf16[32,2304]{1,0:T(8,128)(2,1)S(1)} %shard_map.61), channel_id=1, source_target_pairs={{0,8},{1,9},{2,10},{3,11},{4,12},{5,13},{6,14},{7,15},{8,0},{9,1},... | collective-permute-start | bytes 442376 | tf_op jit(solution)/shard_map/ppermute | solution.py:55
  15.5 5.7 %collective-permute-start.9 = (bf16[128,2304]{1,0:T(8,128)(2,1)S(1)}, bf16[128,2304]{1,0:T(8,128)(2,1)S(1)}, u32[]{:S(2)}, u32[]{:S(2)}) collective-permute-start(bf16[128,2304]{1,0:T(8,128)(2,1)S(1)} %get-tuple-element.21), channel_id=1, source_target_pairs={{0,2},{1,3},{2,0},{3,1},{4,6},{5,7},{6,4},{7,5},{8,10},{9,11},{10,... | collective-permute-start | bytes 1769480 | tf_op jit(solution)/shard_map/ppermute | solution.py:46
  19.1 14.3 %collective-permute-start.3 = (bf16[64,2304]{1,0:T(8,128)(2,1)S(1)}, bf16[64,2304]{1,0:T(8,128)(2,1)S(1)}, u32[]{:S(2)}, u32[]{:S(2)}) collective-permute-start(bf16[64,2304]{1,0:T(8,128)(2,1)S(1)} %pad_maximum_fusion.1), channel_id=1, source_target_pairs={{0,1},{1,0},{2,6},{3,7},{4,5},{5,4},{6,2},{7,3},{8,9},{9,8},{10,14... | collective-permute-start | bytes 884744 | tf_op jit(solution)/shard_map/ppermute | solution.py:46
  19.9 12.0 %collective-permute-start.11 = (bf16[128,2304]{1,0:T(8,128)(2,1)S(1)}, bf16[128,2304]{1,0:T(8,128)(2,1)S(1)}, u32[]{:S(2)}, u32[]{:S(2)}) collective-permute-start(bf16[128,2304]{1,0:T(8,128)(2,1)S(1)} %add_convert_fusion), channel_id=1, source_target_pairs={{0,4},{1,5},{2,3},{3,2},{4,0},{5,1},{6,7},{7,6},{8,12},{9,13},{10,... | collective-permute-start | bytes 1769480 | tf_op jit(solution)/shard_map/ppermute | solution.py:46
  31.9 7.9 %collective-permute-start.12 = (bf16[64,2304]{1,0:T(8,128)(2,1)S(1)}, bf16[64,2304]{1,0:T(8,128)(2,1)S(1)}, u32[]{:S(2)}, u32[]{:S(2)}) collective-permute-start(bf16[64,2304]{1,0:T(8,128)(2,1)S(1)} %fusion), channel_id=1, source_target_pairs={{0,1},{1,0},{2,6},{3,7},{4,5},{5,4},{6,2},{7,3},{8,9},{9,8},{10,14... | collective-permute-start | bytes 884744 | tf_op jit(solution)/shard_map/ppermute | solution.py:46
  32.8 9.3 %collective-permute-start.5 = (bf16[64,2304]{1,0:T(8,128)(2,1)S(1)}, bf16[64,2304]{1,0:T(8,128)(2,1)S(1)}, u32[]{:S(2)}, u32[]{:S(2)}) collective-permute-start(bf16[64,2304]{1,0:T(8,128)(2,1)S(1)} %pad_maximum_fusion.1), channel_id=1, source_target_pairs={{0,4},{1,5},{2,3},{3,2},{4,0},{5,1},{6,7},{7,6},{8,12},{9,13},{10,... | collective-permute-start | bytes 884744 | tf_op jit(solution)/shard_map/ppermute | solution.py:46
  33.4 10.8 %collective-permute-start.6 = (bf16[64,2304]{1,0:T(8,128)(2,1)S(1)}, bf16[64,2304]{1,0:T(8,128)(2,1)S(1)}, u32[]{:S(2)}, u32[]{:S(2)}) collective-permute-start(bf16[64,2304]{1,0:T(8,128)(2,1)S(1)} %collective-permute-done.3), channel_id=1, source_target_pairs={{0,4},{1,5},{2,3},{3,2},{4,0},{5,1},{6,7},{7,6},{8,12},{9,13},{10,... | collective-permute-start | bytes 884744 | tf_op jit(solution)/shard_map/ppermute | solution.py:46
  39.9 4.7 %collective-permute-start.13 = (bf16[32,2304]{1,0:T(8,128)(2,1)S(1)}, bf16[32,2304]{1,0:T(8,128)(2,1)S(1)}, u32[]{:S(2)}, u32[]{:S(2)}) collective-permute-start(bf16[32,2304]{1,0:T(8,128)(2,1)S(1)} %slice.61), channel_id=1, source_target_pairs={{0,8},{1,9},{2,10},{3,11},{4,12},{5,13},{6,14},{7,15},{8,0},{9,1},... | collective-permute-start | bytes 442376 | tf_op jit(solution)/shard_map/ppermute | solution.py:55
  40.3 8.9 %collective-permute-start.4 = (bf16[128,2304]{1,0:T(8,128)(2,1)S(1)}, bf16[128,2304]{1,0:T(8,128)(2,1)S(1)}, u32[]{:S(2)}, u32[]{:S(2)}) collective-permute-start(bf16[128,2304]{1,0:T(8,128)(2,1)S(1)} %pad_maximum_fusion.own_ref), channel_id=1, source_target_pairs={{0,2},{1,3},{2,0},{3,1},{4,6},{5,7},{6,4},{7,5},{8,10},{9,11},{10,... | collective-permute-start | bytes 1769480 | tf_op jit(solution)/shard_map/ppermute | solution.py:46
  42.1 9.3 %collective-permute-start.7 = (bf16[64,2304]{1,0:T(8,128)(2,1)S(1)}, bf16[64,2304]{1,0:T(8,128)(2,1)S(1)}, u32[]{:S(2)}, u32[]{:S(2)}) collective-permute-start(bf16[64,2304]{1,0:T(8,128)(2,1)S(1)} %collective-permute-done.5.refs_0_), channel_id=1, source_target_pairs={{0,2},{1,3},{2,0},{3,1},{4,6},{5,7},{6,4},{7,5},{8,10},{9,11},{10,... | collective-permute-start | bytes 884744 | tf_op jit(solution)/shard_map/ppermute | solution.py:46
  44.2 7.2 %collective-permute-start.8 = (bf16[64,2304]{1,0:T(8,128)(2,1)S(1)}, bf16[64,2304]{1,0:T(8,128)(2,1)S(1)}, u32[]{:S(2)}, u32[]{:S(2)}) collective-permute-start(bf16[64,2304]{1,0:T(8,128)(2,1)S(1)} %collective-permute-done.6.refs_1_), channel_id=1, source_target_pairs={{0,2},{1,3},{2,0},{3,1},{4,6},{5,7},{6,4},{7,5},{8,10},{9,11},{10,... | collective-permute-start | bytes 884744 | tf_op jit(solution)/shard_map/ppermute | solution.py:46
  44.6 12.3 %collective-permute-start.14 = (bf16[32,2304]{1,0:T(8,128)(2,1)S(1)}, bf16[32,2304]{1,0:T(8,128)(2,1)S(1)}, u32[]{:S(2)}, u32[]{:S(2)}) collective-permute-start(bf16[32,2304]{1,0:T(8,128)(2,1)S(1)} %get-tuple-element.24), channel_id=1, source_target_pairs={{0,31},{1,30},{2,29},{3,28},{4,27},{5,26},{6,25},{7,24},{8,23},{9,... | collective-permute-start | bytes 442376 | tf_op jit(solution)/shard_map/ppermute | solution.py:55

commit v6 on v5

--- a/solution.py
+++ b/solution.py
@@ -57,24 +57,30 @@
     def complement(self, block):
         return self.shift(block, self.count - 1)
 
-    def source(self, position, device, rows):
+    def source(self, position, device, rows, turns):
         shift = rows.bit_length() - 1
         slot, low = position >> shift, position & (rows - 1)
         bit = self.count.bit_length() - 2
-        flag = (slot >> bit) & 1
-        owner = device ^ (flag * self.core)
-        parity = jnp.where((owner & self.core) != 0, 1, 0)
-        first = parity * self.cross[1] + (1 - parity) * self.cross[0]
-        second = parity * self.cross[0] + (1 - parity) * self.cross[1]
-        owner = owner ^ (((slot >> (bit - 1)) & 1) * first)
-        owner = owner ^ (((slot >> (bit - 2)) & 1) * second)
-        bit -= 3
-        for group in self.groups:
-            for mask in reversed(group):
+        owner = device
+        for turn in turns:
+            if turn == "rest":
+                masks = [mask for group in self.groups for mask in reversed(group)]
+            elif turn == "core":
+                masks = [self.core]
+            elif turn == "mirror":
+                masks = [self.count - 1]
+            else:
+                odd = jnp.where((owner & self.core) != 0, 1, 0)
+                odd = odd if turn == "a" else 1 - odd
+                masks = [odd * self.cross[1] + (1 - odd) * self.cross[0]]
+            for mask in masks:
                 owner = owner ^ (((slot >> bit) & 1) * mask)
                 bit -= 1
-        owner = owner ^ ((slot & 1) * (self.count - 1))
         return (owner << shift) + low
+
+
+SUM_TURNS = ("core", "a", "b", "rest", "mirror")
+GET_TURNS = ("core", "a", "rest", "b", "mirror")
 
 
 def anti_identity(size):
@@ -83,10 +89,10 @@
     return jnp.where(row + col == size - 1, 1.0, 0.0).astype(BF16)
 
 
-def selection(plan, device, rows, width):
+def selection(plan, device, rows, width, turns):
     position = lax.broadcasted_iota(jnp.int32, (width, 128), 0)
     lane = lax.broadcasted_iota(jnp.int32, (width, 128), 1)
-    source = plan.source(position, device, rows)
+    source = plan.source(position, device, rows, turns)
 
     def one_hot(index):
         return jnp.concatenate(
@@ -120,7 +126,7 @@
     copies = [pltpu.make_async_copy(far, near, arrived.at[i]) for i, (far, near) in enumerate(pairs)]
     for copy in copies:
         copy.start()
-    direct, mirror = selection(plan, device_ref[0], rows, width)
+    direct, mirror = selection(plan, device_ref[0], rows, width, SUM_TURNS)
     for copy in copies:
         copy.wait()
     values = values_ref[...]
@@ -192,11 +198,12 @@
 
 def early_input_kernel(plan, rows, begins, late_begins, device_ref, windows_ref, own_ref, other_ref, out_ref, late_ref):
     refs = (own_ref, other_ref)
-    direct, _ = selection(plan, device_ref[0], rows, out_ref.shape[1])
+    direct, _ = selection(plan, device_ref[0], rows, out_ref.shape[1], GET_TURNS)
     out_ref[...] = dot(rounded_sums(2 * rows, windows_ref, refs), chosen_rows(direct, refs, begins)).astype(BF16)
-    size = late_ref.shape[0] // len(late_begins)
-    for place, begin in enumerate(late_begins):
-        late_ref[place * size : (place + 1) * size, :] = direct[begin : begin + size, :]
+    place = 0
+    for begin, size in late_begins:
+        late_ref[place : place + size, :] = direct[begin : begin + size, :]
+        place += size
 
 
 def late_input_kernel(group, windows_ref, early_ref, chosen_ref, *refs):
@@ -351,19 +358,24 @@
         tied_kernel, [((2 * rows, depth), BF16, True)], (by_tap, far_weight),
         flops=4 * rows * depth * half, given=(1,),
     )
-    for place, group in reversed(list(enumerate(plan.groups))):
-        gathered = jnp.concatenate([gathered] + [plan.shift(gathered, m) for m in plan.group_masks(group)[1:]], axis=0)
+    gathered = jnp.concatenate([gathered, plan.swap(gathered, "b")], axis=0)
+    for place in range(len(plan.groups) - 1, -1, -1):
+        pieces = [plan.shift(gathered, mask) for mask in plan.group_masks(plan.groups[place])[1:]]
+        if place:
+            gathered = jnp.concatenate([gathered] + pieces, axis=0)
+        else:
+            relayed = jnp.concatenate(pieces, axis=0)
     size = gathered.shape[0]
-    relayed = plan.swap(gathered, "b")
     late = [plan.swap(gathered, "a")]
     late.append(plan.swap(relayed, "a"))
     gathered = jnp.concatenate([gathered, relayed], axis=0)
+    span = gathered.shape[0]
     other = plan.swap(gathered, "core")
     for place in range(2):
         late.append(plan.swap(late[place], "core"))
-    begins = (2 * size, 3 * size, 6 * size, 7 * size)
+    late_begins = [(begin, n) for core in (span, 3 * span) for begin, n in ((core, size), (core + size, span - size))]
     early, chosen = call(
-        functools.partial(early_input_kernel, plan, rows, (0, 4 * size), begins),
+        functools.partial(early_input_kernel, plan, rows, (0, 2 * span), late_begins),
         [((count, width), BF16, True), ((half, width), BF16, True)], (device, windows, gathered, other),
         scalars=1, flops=work, given=(1, 2, 3),
     )

time: 59.2 us -> 58.2 us (0.983)
  the two profiles are of different devices: /device:TPU:11 before, /device:TPU:1 now
where the time goes in v6:
time: 58.2 us; the launch traced here: 58 us
  starting transfers between devices  30 us (52%)
  Pallas kernels  13.3 us (23%)
  waiting for transfers between devices  12.6 us (22%)
  other arithmetic  1.28 us (2%)
  between operations  0.8 us (1%)
    ppermute x4, starting transfers between devices, shift(): return lax.ppermute(block, AXES, [(d, d ^ mask) for d in range(self.count)])  15.3 us
    pallas_call x7, Pallas kernels, call(): pl.pallas_call(kernel, out_shape=[(ON_CHIP if stays else jax.ShapeDtypeSt...  13.3 us
    ppermute x10, starting transfers between devices, swap(): return lax.ppermute(block, AXES, route)  12.6 us
    ppermute x10, waiting for transfers between devices, swap(): return lax.ppermute(block, AXES, route)  12.6 us
    ppermute x1, starting transfers between devices, edges(): lax.ppermute(jnp.where(where == 0, top, bottom), 'pos', [(0, 1), (1, 0)])  2.09 us
  transfers between devices with their start and end apart: 15, of which 4 were waited for; matrix products, arithmetic and copies ran while one was open for 1% of the time, Pallas kernels for 21%

profile of v6, /device:TPU:1, one launch (start us, length us, event | category | flops | bytes accessed | tf_op | source)
XLA Modules:
  0.0 58.0 jit_solution(2310240851823805757)
XLA Ops:
  0.6 0.8 %fusion.18 = bf16[2,4,512]{2,1,0:T(4,128)(2,1)S(1)} fusion(bf16[2,256,512]{2,1,0:T(8,128)(2,1)} %pre_hbm.1, bf16[2,256,512]{2,1,0:T(8,128)(2,1)} %out_grad_hbm.1, pred[]{:T(512)S(6)} %eq.2), kind=kLoop, calls=%fused_computation.35 | loop fusion | flops 102400 | bytes 40961 | tf_op jit(solution)/shard_map/jit(_where)/select_n | solution.py:284
  1.5 2.1 %collective-permute-start = (bf16[2,4,512]{2,1,0:T(4,128)(2,1)S(1)}, bf16[2,4,512]{2,1,0:T(4,128)(2,1)S(1)}, u32[]{:S(2)}, u32[]{:S(2)}) collective-permute-start(bf16[2,4,512]{2,1,0:T(4,128)(2,1)S(1)} %fusion.18), channel_id=1, source_target_pairs={{0,1},{1,0},{2,3},{3,2},{4,5},{5,4},{6,7},{7,6},{8,9},{9,8},{10,11... | collective-permute-start | bytes 24584 | tf_op jit(solution)/shard_map/ppermute | solution.py:284
  3.5 5.1 %collective-permute-start.1 = (bf16[9,16,512]{2,1,0:T(8,128)(2,1)}, bf16[9,16,512]{2,1,0:T(8,128)(2,1)S(1)}, u32[]{:S(2)}, u32[]{:S(2)}) collective-permute-start(bf16[9,16,512]{2,1,0:T(8,128)(2,1)} %bitcast.5), channel_id=1, source_target_pairs={{0,31},{1,30},{2,29},{3,28},{4,27},{5,26},{6,25},{7,24},{8,23},{9,... | collective-permute-start | bytes 442376 | tf_op jit(solution)/shard_map/ppermute | solution.py:55
  8.6 3.3 %shard_map.59 = (bf16[256,1024]{1,0:T(8,128)(2,1)S(1)}, bf16[256,1024]{1,0:T(8,128)(2,1)S(1)}, f32[4,272,256]{2,1,0:T(8,128)S(1)}, bf16[1024,2304]{1,0:T(8,128)(2,1)S(1)}) custom-call(s32[1]{0:T(128)} %bitcast.device_ref, bf16[512,512]{1,0:T(8,128)(2,1)} %bitcast.9, bf16[2,256,512]{2,1,0:T(8,128)(2,1)} %pre_hbm.1, bf16[2,256,512]{2,1,0:T(8,128)(2,1)} %out_grad_hbm.1), custom_call_target="tpu_custom_call" | custom-call | flops 536870912 | bytes 8454144 | tf_op jit(solution)/shard_map/pallas_call | solution.py:261
  12.0 0.0 collective-permute-done
  12.0 0.0 copy-start
  12.1 1.6 %shard_map.60 = (bf16[128,2304]{1,0:T(8,128)(2,1)S(1)}, f32[128,2304]{1,0:T(8,128)S(1)}, f32[4,272,256]{2,1,0:T(8,128)S(1)}, bf16[1024,2304]{1,0:T(8,128)(2,1)S(1)}) custom-call(bf16[256,1024]{1,0:T(8,128)(2,1)S(1)} %get-tuple-element.13.order_ref, bf16[2,8,512]{2,1,0:T(8,128)(2,1)S(1)} %pad_maximum_fusion.2.halo_ref, ...), custom_call_target="tpu_custom_call", output_to_operand_aliasing={{2}: (2, {}), {3}: (3, {})} | custom-call | flops 1207959552 | bytes 13975552 | tf_op jit(solution)/shard_map/pallas_call | solution.py:261
  13.6 0.1 collective-permute-start.10
  13.7 0.0 collective-permute-done.1.far_ref
  13.7 0.0 copy-done
  13.7 0.5 shard_map.61
  14.3 1.2 %collective-permute-start.2 = (bf16[32,2304]{1,0:T(8,128)(2,1)S(1)}, bf16[32,2304]{1,0:T(8,128)(2,1)S(1)}, u32[]{:S(2)}, u32[]{:S(2)}) collective-permute-start(bf16[32,2304]{1,0:T(8,128)(2,1)S(1)} %shard_map.61), channel_id=1, source_target_pairs={{0,1},{1,0},{2,6},{3,7},{4,5},{5,4},{6,2},{7,3},{8,9},{9,8},{10,14... | collective-permute-start | bytes 442376 | tf_op jit(solution)/shard_map/ppermute | solution.py:46
  15.4 1.4 %shard_map.64 = (bf16[128,2304]{1,0:T(8,128)(2,1)S(1)}, f32[128,2304]{1,0:T(8,128)S(1)}) custom-call(bf16[256,1024]{1,0:T(8,128)(2,1)S(1)} %get-tuple-element.19.order_ref, bf16[1024,2304]{1,0:T(8,128)(2,1)S(1)} %get-tuple-element.16.windows_ref), custom_call_target="tpu_custom_call" | custom-call | flops 1207959552 | bytes 7012352 | tf_op jit(solution)/shard_map/pallas_call | solution.py:261
  16.8 0.9 %collective-permute-start.9 = (bf16[128,2304]{1,0:T(8,128)(2,1)S(1)}, bf16[128,2304]{1,0:T(8,128)(2,1)S(1)}, u32[]{:S(2)}, u32[]{:S(2)}) collective-permute-start(bf16[128,2304]{1,0:T(8,128)(2,1)S(1)} %get-tuple-element.21), channel_id=1, source_target_pairs={{0,2},{1,3},{2,0},{3,1},{4,6},{5,7},{6,4},{7,5},{8,10},{9,11},{10,... | collective-permute-start | bytes 1769480 | tf_op jit(solution)/shard_map/ppermute | solution.py:46
  17.7 0.9 %collective-permute-done.2 = bf16[32,2304]{1,0:T(8,128)(2,1)S(1)} collective-permute-done((bf16[32,2304]{1,0:T(8,128)(2,1)S(1)}, bf16[32,2304]{1,0:T(8,128)(2,1)S(1)}, u32[]{:S(2)}, u32[]{:S(2)}) %collective-permute-start.2) | collective-permute-done | bytes 147488 | tf_op jit(solution)/shard_map/ppermute | solution.py:46
  18.6 2.5 %collective-permute-start.3 = (bf16[64,2304]{1,0:T(8,128)(2,1)S(1)}, bf16[64,2304]{1,0:T(8,128)(2,1)S(1)}, u32[]{:S(2)}, u32[]{:S(2)}) collective-permute-start(bf16[64,2304]{1,0:T(8,128)(2,1)S(1)} %pad_maximum_fusion.1), channel_id=1, source_target_pairs={{0,8},{1,9},{2,10},{3,11},{4,12},{5,13},{6,14},{7,15},{8,0},{9,1},... | collective-permute-start | bytes 884744 | tf_op jit(solution)/shard_map/ppermute | solution.py:55
  21.2 0.0 collective-permute-done.10
  21.2 0.1 add_convert_fusion
  21.3 0.6 %collective-permute-start.11 = (bf16[128,2304]{1,0:T(8,128)(2,1)S(1)}, bf16[128,2304]{1,0:T(8,128)(2,1)S(1)}, u32[]{:S(2)}, u32[]{:S(2)}) collective-permute-start(bf16[128,2304]{1,0:T(8,128)(2,1)S(1)} %add_convert_fusion), channel_id=1, source_target_pairs={{0,4},{1,5},{2,3},{3,2},{4,0},{5,1},{6,7},{7,6},{8,12},{9,13},{10,... | collective-permute-start | bytes 1769480 | tf_op jit(solution)/shard_map/ppermute | solution.py:46
  21.9 0.0 collective-permute-done.9
  21.9 0.1 convert_add_fusion
  22.0 8.3 %collective-permute-done.11 = bf16[128,2304]{1,0:T(8,128)(2,1)S(1)} collective-permute-done((bf16[128,2304]{1,0:T(8,128)(2,1)S(1)}, bf16[128,2304]{1,0:T(8,128)(2,1)S(1)}, u32[]{:S(2)}, u32[]{:S(2)}) %collective-permute-start.11) | collective-permute-done | bytes 589856 | tf_op jit(solution)/shard_map/ppermute | solution.py:46
  30.4 0.1 fusion
  30.4 1.3 %collective-permute-start.12 = (bf16[64,2304]{1,0:T(8,128)(2,1)S(1)}, bf16[64,2304]{1,0:T(8,128)(2,1)S(1)}, u32[]{:S(2)}, u32[]{:S(2)}) collective-permute-start(bf16[64,2304]{1,0:T(8,128)(2,1)S(1)} %fusion), channel_id=1, source_target_pairs={{0,1},{1,0},{2,6},{3,7},{4,5},{5,4},{6,2},{7,3},{8,9},{9,8},{10,14... | collective-permute-start | bytes 884744 | tf_op jit(solution)/shard_map/ppermute | solution.py:46
  31.7 0.3 collective-permute-start.5
  32.0 0.0 collective-permute-done.3
  32.0 1.2 %collective-permute-start.6 = (bf16[64,2304]{1,0:T(8,128)(2,1)S(1)}, bf16[64,2304]{1,0:T(8,128)(2,1)S(1)}, u32[]{:S(2)}, u32[]{:S(2)}) collective-permute-start(bf16[64,2304]{1,0:T(8,128)(2,1)S(1)} %collective-permute-done.3), channel_id=1, source_target_pairs={{0,4},{1,5},{2,3},{3,2},{4,0},{5,1},{6,7},{7,6},{8,12},{9,13},{10,... | collective-permute-start | bytes 884744 | tf_op jit(solution)/shard_map/ppermute | solution.py:46
  33.2 3.2 %collective-permute-done.12 = bf16[64,2304]{1,0:T(8,128)(2,1)S(1)} collective-permute-done((bf16[64,2304]{1,0:T(8,128)(2,1)S(1)}, bf16[64,2304]{1,0:T(8,128)(2,1)S(1)}, u32[]{:S(2)}, u32[]{:S(2)}) %collective-permute-start.12) | collective-permute-done | bytes 294944 | tf_op jit(solution)/shard_map/ppermute | solution.py:46
  36.4 0.1 fusion.1
  36.5 0.1 collective-permute-start.13
  36.6 6.7 %collective-permute-start.4 = (bf16[128,2304]{1,0:T(8,128)(2,1)S(1)}, bf16[128,2304]{1,0:T(8,128)(2,1)S(1)}, u32[]{:S(2)}, u32[]{:S(2)}) collective-permute-start(bf16[128,2304]{1,0:T(8,128)(2,1)S(1)} %pad_maximum_fusion.own_ref), channel_id=1, source_target_pairs={{0,2},{1,3},{2,0},{3,1},{4,6},{5,7},{6,4},{7,5},{8,10},{9,11},{10,... | collective-permute-start | bytes 1769480 | tf_op jit(solution)/shard_map/ppermute | solution.py:46
  43.4 0.0 collective-permute-done.5.refs_0_
  43.4 0.1 collective-permute-start.7
  43.4 0.2 collective-permute-done.6.refs_1_
  43.6 0.2 collective-permute-start.8
  43.9 0.0 collective-permute-done.13
  43.9 7.6 %collective-permute-start.14 = (bf16[32,2304]{1,0:T(8,128)(2,1)S(1)}, bf16[32,2304]{1,0:T(8,128)(2,1)S(1)}, u32[]{:S(2)}, u32[]{:S(2)}) collective-permute-start(bf16[32,2304]{1,0:T(8,128)(2,1)S(1)} %get-tuple-element.24), channel_id=1, source_target_pairs={{0,31},{1,30},{2,29},{3,28},{4,27},{5,26},{6,25},{7,24},{8,23},{9,... | collective-permute-start | bytes 442376 | tf_op jit(solution)/shard_map/ppermute | solution.py:55
  51.5 0.0 collective-permute-done.4.other_ref
  51.5 2.3 %shard_map.62 = (bf16[512,512]{1,0:T(8,128)(2,1)S(1)}, bf16[256,512]{1,0:T(8,128)(2,1)S(1)}) custom-call(s32[1]{0:T(128)} %bitcast.device_ref, bf16[1024,2304]{1,0:T(8,128)(2,1)S(1)} %get-tuple-element.16.windows_ref, bf16[128,2304]{1,0:T(8,128)(2,1)S(1)} %pad_maximum_fusion.own_ref, bf16[128,2304]{1,0:T(8,128)(2,1)S(1)} %collective-permute-done.4.other_ref), custom_call_target="tpu_custom_call" | custom-call | flops 1207959552 | bytes 6684672 | tf_op jit(solution)/shard_map/pallas_call | solution.py:261
  53.8 0.0 collective-permute-done.7.refs_2_
  53.8 0.0 collective-permute-done.8.refs_3_
  53.8 2.9 %shard_map.63 = bf16[512,512]{1,0:T(8,128)(2,1)} custom-call(bf16[1024,2304]{1,0:T(8,128)(2,1)S(1)} %get-tuple-element.16.windows_ref, bf16[512,512]{1,0:T(8,128)(2,1)S(1)} %get-tuple-element.17.early_ref, bf16[256,512]{1,0:T(8,128)(2,1)S(1)} %get-tuple-element.18.chosen_ref, bf16[64,2304]{1,0:T(8,128)(2,1)S(1)} %collective-permute-done.5.refs_0_, ...), custom_call_target="tpu_custom_call" | custom-call | flops 1207959552 | bytes 7208960 | tf_op jit(solution)/shard_map/pallas_call | solution.py:261
  56.7 0.0 collective-permute-done.14.got_ref
  56.7 1.3 %shard_map.65 = f32[9,16,512]{2,1,0:T(8,128)} custom-call(f32[32,2304]{1,0:T(8,128)S(1)} %get-tuple-element.25.own_ref, bf16[32,2304]{1,0:T(8,128)(2,1)S(1)} %collective-permute-done.14.got_ref), custom_call_target="tpu_custom_call" | custom-call | flops 37748736 | bytes 737280 | tf_op jit(solution)/shard_map/pallas_call | solution.py:261
  (6 shorter events, 0.1 us)
Async XLA Ops:
  1.5 10.5 %collective-permute-start = (bf16[2,4,512]{2,1,0:T(4,128)(2,1)S(1)}, bf16[2,4,512]{2,1,0:T(4,128)(2,1)S(1)}, u32[]{:S(2)}, u32[]{:S(2)}) collective-permute-start(bf16[2,4,512]{2,1,0:T(4,128)(2,1)S(1)} %fusion.18), channel_id=1, source_target_pairs={{0,1},{1,0},{2,3},{3,2},{4,5},{5,4},{6,7},{7,6},{8,9},{9,8},{10,11... | collective-permute-start | bytes 24584 | tf_op jit(solution)/shard_map/ppermute | solution.py:284
  3.5 10.1 %collective-permute-start.1 = (bf16[9,16,512]{2,1,0:T(8,128)(2,1)}, bf16[9,16,512]{2,1,0:T(8,128)(2,1)S(1)}, u32[]{:S(2)}, u32[]{:S(2)}) collective-permute-start(bf16[9,16,512]{2,1,0:T(8,128)(2,1)} %bitcast.5), channel_id=1, source_target_pairs={{0,31},{1,30},{2,29},{3,28},{4,27},{5,26},{6,25},{7,24},{8,23},{9,... | collective-permute-start | bytes 442376 | tf_op jit(solution)/shard_map/ppermute | solution.py:55
  12.0 1.7 %copy-start = (bf16[16,9,512]{2,0,1:T(8,128)(2,1)S(1)}, bf16[16,9,512]{2,0,1:T(8,128)(2,1)}, u32[]{:S(2)}) copy-start(bf16[16,9,512]{2,0,1:T(8,128)(2,1)} %param.7) | copy-start | bytes 442372
  13.6 7.6 %collective-permute-start.10 = (bf16[128,2304]{1,0:T(8,128)(2,1)S(1)}, bf16[128,2304]{1,0:T(8,128)(2,1)S(1)}, u32[]{:S(2)}, u32[]{:S(2)}) collective-permute-start(bf16[128,2304]{1,0:T(8,128)(2,1)S(1)} %get-tuple-element.23), channel_id=1, source_target_pairs={{0,2},{1,3},{2,0},{3,1},{4,6},{5,7},{6,4},{7,5},{8,10},{9,11},{10,... | collective-permute-start | bytes 1769480 | tf_op jit(solution)/shard_map/ppermute | solution.py:46
  14.3 4.4 %collective-permute-start.2 = (bf16[32,2304]{1,0:T(8,128)(2,1)S(1)}, bf16[32,2304]{1,0:T(8,128)(2,1)S(1)}, u32[]{:S(2)}, u32[]{:S(2)}) collective-permute-start(bf16[32,2304]{1,0:T(8,128)(2,1)S(1)} %shard_map.61), channel_id=1, source_target_pairs={{0,1},{1,0},{2,6},{3,7},{4,5},{5,4},{6,2},{7,3},{8,9},{9,8},{10,14... | collective-permute-start | bytes 442376 | tf_op jit(solution)/shard_map/ppermute | solution.py:46
  16.8 5.1 %collective-permute-start.9 = (bf16[128,2304]{1,0:T(8,128)(2,1)S(1)}, bf16[128,2304]{1,0:T(8,128)(2,1)S(1)}, u32[]{:S(2)}, u32[]{:S(2)}) collective-permute-start(bf16[128,2304]{1,0:T(8,128)(2,1)S(1)} %get-tuple-element.21), channel_id=1, source_target_pairs={{0,2},{1,3},{2,0},{3,1},{4,6},{5,7},{6,4},{7,5},{8,10},{9,11},{10,... | collective-permute-start | bytes 1769480 | tf_op jit(solution)/shard_map/ppermute | solution.py:46
  18.6 13.4 %collective-permute-start.3 = (bf16[64,2304]{1,0:T(8,128)(2,1)S(1)}, bf16[64,2304]{1,0:T(8,128)(2,1)S(1)}, u32[]{:S(2)}, u32[]{:S(2)}) collective-permute-start(bf16[64,2304]{1,0:T(8,128)(2,1)S(1)} %pad_maximum_fusion.1), channel_id=1, source_target_pairs={{0,8},{1,9},{2,10},{3,11},{4,12},{5,13},{6,14},{7,15},{8,0},{9,1},... | collective-permute-start | bytes 884744 | tf_op jit(solution)/shard_map/ppermute | solution.py:55
  21.3 9.1 %collective-permute-start.11 = (bf16[128,2304]{1,0:T(8,128)(2,1)S(1)}, bf16[128,2304]{1,0:T(8,128)(2,1)S(1)}, u32[]{:S(2)}, u32[]{:S(2)}) collective-permute-start(bf16[128,2304]{1,0:T(8,128)(2,1)S(1)} %add_convert_fusion), channel_id=1, source_target_pairs={{0,4},{1,5},{2,3},{3,2},{4,0},{5,1},{6,7},{7,6},{8,12},{9,13},{10,... | collective-permute-start | bytes 1769480 | tf_op jit(solution)/shard_map/ppermute | solution.py:46
  30.4 5.9 %collective-permute-start.12 = (bf16[64,2304]{1,0:T(8,128)(2,1)S(1)}, bf16[64,2304]{1,0:T(8,128)(2,1)S(1)}, u32[]{:S(2)}, u32[]{:S(2)}) collective-permute-start(bf16[64,2304]{1,0:T(8,128)(2,1)S(1)} %fusion), channel_id=1, source_target_pairs={{0,1},{1,0},{2,6},{3,7},{4,5},{5,4},{6,2},{7,3},{8,9},{9,8},{10,14... | collective-permute-start | bytes 884744 | tf_op jit(solution)/shard_map/ppermute | solution.py:46
  31.7 11.6 %collective-permute-start.5 = (bf16[64,2304]{1,0:T(8,128)(2,1)S(1)}, bf16[64,2304]{1,0:T(8,128)(2,1)S(1)}, u32[]{:S(2)}, u32[]{:S(2)}) collective-permute-start(bf16[64,2304]{1,0:T(8,128)(2,1)S(1)} %pad_maximum_fusion.1), channel_id=1, source_target_pairs={{0,4},{1,5},{2,3},{3,2},{4,0},{5,1},{6,7},{7,6},{8,12},{9,13},{10,... | collective-permute-start | bytes 884744 | tf_op jit(solution)/shard_map/ppermute | solution.py:46
  32.0 11.6 %collective-permute-start.6 = (bf16[64,2304]{1,0:T(8,128)(2,1)S(1)}, bf16[64,2304]{1,0:T(8,128)(2,1)S(1)}, u32[]{:S(2)}, u32[]{:S(2)}) collective-permute-start(bf16[64,2304]{1,0:T(8,128)(2,1)S(1)} %collective-permute-done.3), channel_id=1, source_target_pairs={{0,4},{1,5},{2,3},{3,2},{4,0},{5,1},{6,7},{7,6},{8,12},{9,13},{10,... | collective-permute-start | bytes 884744 | tf_op jit(solution)/shard_map/ppermute | solution.py:46
  36.5 7.4 %collective-permute-start.13 = (bf16[32,2304]{1,0:T(8,128)(2,1)S(1)}, bf16[32,2304]{1,0:T(8,128)(2,1)S(1)}, u32[]{:S(2)}, u32[]{:S(2)}) collective-permute-start(bf16[32,2304]{1,0:T(8,128)(2,1)S(1)} %slice.61), channel_id=1, source_target_pairs={{0,8},{1,9},{2,10},{3,11},{4,12},{5,13},{6,14},{7,15},{8,0},{9,1},... | collective-permute-start | bytes 442376 | tf_op jit(solution)/shard_map/ppermute | solution.py:55
  36.6 14.9 %collective-permute-start.4 = (bf16[128,2304]{1,0:T(8,128)(2,1)S(1)}, bf16[128,2304]{1,0:T(8,128)(2,1)S(1)}, u32[]{:S(2)}, u32[]{:S(2)}) collective-permute-start(bf16[128,2304]{1,0:T(8,128)(2,1)S(1)} %pad_maximum_fusion.own_ref), channel_id=1, source_target_pairs={{0,2},{1,3},{2,0},{3,1},{4,6},{5,7},{6,4},{7,5},{8,10},{9,11},{10,... | collective-permute-start | bytes 1769480 | tf_op jit(solution)/shard_map/ppermute | solution.py:46
  43.4 10.4 %collective-permute-start.7 = (bf16[64,2304]{1,0:T(8,128)(2,1)S(1)}, bf16[64,2304]{1,0:T(8,128)(2,1)S(1)}, u32[]{:S(2)}, u32[]{:S(2)}) collective-permute-start(bf16[64,2304]{1,0:T(8,128)(2,1)S(1)} %collective-permute-done.5.refs_0_), channel_id=1, source_target_pairs={{0,2},{1,3},{2,0},{3,1},{4,6},{5,7},{6,4},{7,5},{8,10},{9,11},{10,... | collective-permute-start | bytes 884744 | tf_op jit(solution)/shard_map/ppermute | solution.py:46
  43.6 10.2 %collective-permute-start.8 = (bf16[64,2304]{1,0:T(8,128)(2,1)S(1)}, bf16[64,2304]{1,0:T(8,128)(2,1)S(1)}, u32[]{:S(2)}, u32[]{:S(2)}) collective-permute-start(bf16[64,2304]{1,0:T(8,128)(2,1)S(1)} %collective-permute-done.6.refs_1_), channel_id=1, source_target_pairs={{0,2},{1,3},{2,0},{3,1},{4,6},{5,7},{6,4},{7,5},{8,10},{9,11},{10,... | collective-permute-start | bytes 884744 | tf_op jit(solution)/shard_map/ppermute | solution.py:46
  43.9 12.8 %collective-permute-start.14 = (bf16[32,2304]{1,0:T(8,128)(2,1)S(1)}, bf16[32,2304]{1,0:T(8,128)(2,1)S(1)}, u32[]{:S(2)}, u32[]{:S(2)}) collective-permute-start(bf16[32,2304]{1,0:T(8,128)(2,1)S(1)} %get-tuple-element.24), channel_id=1, source_target_pairs={{0,31},{1,30},{2,29},{3,28},{4,27},{5,26},{6,25},{7,24},{8,23},{9,... | collective-permute-start | bytes 442376 | tf_op jit(solution)/shard_map/ppermute | solution.py:55

commit v7 on v6

--- a/solution.py
+++ b/solution.py
@@ -237,15 +237,17 @@
             ).astype(BF16)
 
 
-def finish_kernel(own_ref, got_ref, out_ref):
+def finish_kernel(*refs):
+    out_ref = refs[-1]
     taps, rows, width = out_ref.shape
     half = width // 2
     cuts = [slice(k * half, (k + 1) * half) for k in range(taps)]
-    far = own_ref[rows:, :] + got_ref[:rows, :].astype(F32)
+    own = jnp.concatenate([ref[...] for ref in refs[:-1:2]], axis=1)
+    got = jnp.concatenate([ref[...] for ref in refs[1:-1:2]], axis=1).astype(F32)
+    far, near = own[rows:] + got[:rows], own[:rows] + got[rows:]
     high = far.astype(BF16)
     low = (far - high.astype(F32)).astype(BF16)
     high, low = (reversed_taps([part[:, cut] for cut in cuts]) for part in (high, low))
-    near = own_ref[:rows, :] + got_ref[rows:, :].astype(F32)
     for k, cut in enumerate(cuts):
         out_ref[k, :, :half] = near[:, cut]
         out_ref[k, :, half:] = high[k] + low[k]
@@ -329,27 +331,38 @@
     )
     received = plan.swap(sent, "core")
     second_sent, second_kept = call(sums_kernel, sums, (second_order, windows), flops=work, given=(0, 1))
-    received = plan.swap((kept + received.astype(F32)).astype(BF16), "a")
-    kept = second_kept + plan.swap(second_sent, "core").astype(F32)
-    middle = kept.shape[0] // 2
-    sent = (kept[middle:] + received[middle:].astype(F32)).astype(BF16)
-    kept = kept[:middle] + received[:middle].astype(F32)
-    received = plan.swap(sent, "b")
-    for place, group in enumerate(plan.groups):
-        if place == 0:
-            kept = kept + received.astype(F32)
-        masks = plan.group_masks(group)
-        size = kept.shape[0] // len(masks)
-        pieces = [
-            plan.shift(kept[j * size : (j + 1) * size].astype(BF16), masks[j]).astype(F32)
-            for j in range(1, len(masks))
-        ]
-        kept = functools.reduce(jnp.add, pieces, kept[:size])
-    got = plan.complement(kept.astype(BF16))
+    cut = (taps + 1) // 2 * half
+    chunks = (slice(0, cut), slice(cut, depth))
+    for place, chunk in enumerate(chunks):
+        arrived = plan.swap((kept[:, chunk] + received[:, chunk].astype(F32)).astype(BF16), "a")
+        late_sums = [arrived] if place == 0 else late_sums + [arrived]
+    second_got = plan.swap(second_sent, "core")
+    pairs = []
+    for place, chunk in enumerate(chunks):
+        arrived = late_sums[place]
+        middle = second_kept.shape[0] // 2
+
+        def part(rows_of):
+            own = second_kept[rows_of, chunk] + second_got[rows_of, chunk].astype(F32)
+            return own + arrived[rows_of].astype(F32)
+
+        sums = part(slice(0, middle))
+        arrived = plan.swap(part(slice(middle, None)).astype(BF16), "b")
+        for number, group in enumerate(plan.groups):
+            if number == 0:
+                sums = sums + arrived.astype(F32)
+            masks = plan.group_masks(group)
+            size = sums.shape[0] // len(masks)
+            pieces = [
+                plan.shift(sums[j * size : (j + 1) * size].astype(BF16), masks[j]).astype(F32)
+                for j in range(1, len(masks))
+            ]
+            sums = functools.reduce(jnp.add, pieces, sums[:size])
+        pairs += [sums, plan.complement(sums.astype(BF16))]
     grad_weight = jnp.transpose(
         call(
-            finish_kernel, [((taps, rows, width), F32, False)], (kept, got),
-            flops=4 * rows * depth * half, given=(0, 1),
+            finish_kernel, [((taps, rows, width), F32, False)], pairs,
+            flops=4 * rows * depth * half, given=range(4),
         ),
         (1, 0, 2),
     )

time: 58.2 us -> 63.9 us (1.098)
  the two profiles are of different devices: /device:TPU:1 before, /device:TPU:11 now
where the time goes in v7:
time: 63.9 us; the launch traced here: 63.2 us
  starting transfers between devices  33.4 us (52%)
  waiting for transfers between devices  14.3 us (22%)
  Pallas kernels  13.3 us (21%)
  other arithmetic  1.31 us (2%)
  between operations  0.83 us (1%)
    ppermute x6, starting transfers between devices, shift(): return lax.ppermute(block, AXES, [(d, d ^ mask) for d in range(self.count)])  17.5 us
    ppermute x12, starting transfers between devices, swap(): return lax.ppermute(block, AXES, route)  15.6 us
    pallas_call x7, Pallas kernels, call(): pl.pallas_call(kernel, out_shape=[(ON_CHIP if stays else jax.ShapeDtypeSt...  13.3 us
    ppermute x6, waiting for transfers between devices, shift(): return lax.ppermute(block, AXES, [(d, d ^ mask) for d in range(self.count)])  7.71 us
    ppermute x12, waiting for transfers between devices, swap(): return lax.ppermute(block, AXES, route)  6.62 us
  transfers between devices with their start and end apart: 19, of which 5 were waited for; matrix products, arithmetic and copies ran while one was open for 1% of the time, Pallas kernels for 18%

profile of v7, /device:TPU:11, one launch (start us, length us, event | category | flops | bytes accessed | tf_op | source)
XLA Modules:
  0.0 63.2 jit_solution(12828082749093514396)
XLA Ops:
  0.6 0.0 copy-start
  0.6 0.8 %fusion.16 = bf16[2,4,512]{2,1,0:T(4,128)(2,1)S(1)} fusion(bf16[2,256,512]{2,1,0:T(8,128)(2,1)} %pre_hbm.1, bf16[2,256,512]{2,1,0:T(8,128)(2,1)} %out_grad_hbm.1, pred[]{:T(512)S(6)} %eq.2), kind=kLoop, calls=%fused_computation.37 | loop fusion | flops 102400 | bytes 40961 | tf_op jit(solution)/shard_map/jit(_where)/select_n | solution.py:286
  1.5 0.3 collective-permute-start
  1.8 4.0 %collective-permute-start.1 = (bf16[9,16,512]{2,1,0:T(8,128)(2,1)}, bf16[9,16,512]{2,1,0:T(8,128)(2,1)S(1)}, u32[]{:S(2)}, u32[]{:S(2)}) collective-permute-start(bf16[9,16,512]{2,1,0:T(8,128)(2,1)} %bitcast.5), channel_id=1, source_target_pairs={{0,31},{1,30},{2,29},{3,28},{4,27},{5,26},{6,25},{7,24},{8,23},{9,... | collective-permute-start | bytes 442376 | tf_op jit(solution)/shard_map/ppermute | solution.py:55
  5.8 3.3 %shard_map.59 = (bf16[256,1024]{1,0:T(8,128)(2,1)S(1)}, bf16[256,1024]{1,0:T(8,128)(2,1)S(1)}, f32[4,272,256]{2,1,0:T(8,128)S(1)}, bf16[1024,2304]{1,0:T(8,128)(2,1)S(1)}) custom-call(s32[1]{0:T(128)} %bitcast.device_ref, bf16[512,512]{1,0:T(8,128)(2,1)} %bitcast.9, bf16[2,256,512]{2,1,0:T(8,128)(2,1)} %pre_hbm.1, bf16[2,256,512]{2,1,0:T(8,128)(2,1)} %out_grad_hbm.1), custom_call_target="tpu_custom_call" | custom-call | flops 536870912 | bytes 8454144 | tf_op jit(solution)/shard_map/pallas_call | solution.py:263
  9.2 0.0 collective-permute-done
  9.2 4.3 %collective-permute-done.1.far_ref = bf16[9,16,512]{2,1,0:T(8,128)(2,1)S(1)} collective-permute-done((bf16[9,16,512]{2,1,0:T(8,128)(2,1)}, bf16[9,16,512]{2,1,0:T(8,128)(2,1)S(1)}, u32[]{:S(2)}, u32[]{:S(2)}) %collective-permute-start.1) | collective-permute-done | bytes 147488 | tf_op jit(solution)/shard_map/ppermute | solution.py:55
  13.5 0.5 shard_map.61
  14.0 1.0 %collective-permute-start.2 = (bf16[32,2304]{1,0:T(8,128)(2,1)S(1)}, bf16[32,2304]{1,0:T(8,128)(2,1)S(1)}, u32[]{:S(2)}, u32[]{:S(2)}) collective-permute-start(bf16[32,2304]{1,0:T(8,128)(2,1)S(1)} %shard_map.61), channel_id=1, source_target_pairs={{0,1},{1,0},{2,6},{3,7},{4,5},{5,4},{6,2},{7,3},{8,9},{9,8},{10,14... | collective-permute-start | bytes 442376 | tf_op jit(solution)/shard_map/ppermute | solution.py:46
  15.0 1.5 %shard_map.60 = (bf16[128,2304]{1,0:T(8,128)(2,1)S(1)}, f32[128,2304]{1,0:T(8,128)S(1)}, f32[4,272,256]{2,1,0:T(8,128)S(1)}, bf16[1024,2304]{1,0:T(8,128)(2,1)S(1)}) custom-call(bf16[256,1024]{1,0:T(8,128)(2,1)S(1)} %get-tuple-element.13.order_ref, bf16[2,8,512]{2,1,0:T(8,128)(2,1)S(1)} %pad_maximum_fusion.2.halo_ref, ...), custom_call_target="tpu_custom_call", output_to_operand_aliasing={{2}: (2, {}), {3}: (3, {})} | custom-call | flops 1207959552 | bytes 13975552 | tf_op jit(solution)/shard_map/pallas_call | solution.py:263
  16.6 1.0 %collective-permute-start.10 = (bf16[128,2304]{1,0:T(8,128)(2,1)S(1)}, bf16[128,2304]{1,0:T(8,128)(2,1)S(1)}, u32[]{:S(2)}, u32[]{:S(2)}) collective-permute-start(bf16[128,2304]{1,0:T(8,128)(2,1)S(1)} %get-tuple-element.23), channel_id=1, source_target_pairs={{0,2},{1,3},{2,0},{3,1},{4,6},{5,7},{6,4},{7,5},{8,10},{9,11},{10,... | collective-permute-start | bytes 1769480 | tf_op jit(solution)/shard_map/ppermute | solution.py:46
  17.5 0.8 %collective-permute-done.2 = bf16[32,2304]{1,0:T(8,128)(2,1)S(1)} collective-permute-done((bf16[32,2304]{1,0:T(8,128)(2,1)S(1)}, bf16[32,2304]{1,0:T(8,128)(2,1)S(1)}, u32[]{:S(2)}, u32[]{:S(2)}) %collective-permute-start.2) | collective-permute-done | bytes 147488 | tf_op jit(solution)/shard_map/ppermute | solution.py:46
  18.4 0.1 collective-permute-start.3
  18.5 1.4 %shard_map.64 = (bf16[128,2304]{1,0:T(8,128)(2,1)S(1)}, f32[128,2304]{1,0:T(8,128)S(1)}) custom-call(bf16[256,1024]{1,0:T(8,128)(2,1)S(1)} %get-tuple-element.19.order_ref, bf16[1024,2304]{1,0:T(8,128)(2,1)S(1)} %get-tuple-element.16.windows_ref), custom_call_target="tpu_custom_call" | custom-call | flops 1207959552 | bytes 7012352 | tf_op jit(solution)/shard_map/pallas_call | solution.py:263
  19.9 1.3 %collective-permute-start.9 = (bf16[128,2304]{1,0:T(8,128)(2,1)S(1)}, bf16[128,2304]{1,0:T(8,128)(2,1)S(1)}, u32[]{:S(2)}, u32[]{:S(2)}) collective-permute-start(bf16[128,2304]{1,0:T(8,128)(2,1)S(1)} %get-tuple-element.21), channel_id=1, source_target_pairs={{0,2},{1,3},{2,0},{3,1},{4,6},{5,7},{6,4},{7,5},{8,10},{9,11},{10,... | collective-permute-start | bytes 1769480 | tf_op jit(solution)/shard_map/ppermute | solution.py:46
  21.2 1.2 %collective-permute-start.5 = (bf16[64,2304]{1,0:T(8,128)(2,1)S(1)}, bf16[64,2304]{1,0:T(8,128)(2,1)S(1)}, u32[]{:S(2)}, u32[]{:S(2)}) collective-permute-start(bf16[64,2304]{1,0:T(8,128)(2,1)S(1)} %pad_maximum_fusion.1), channel_id=1, source_target_pairs={{0,4},{1,5},{2,3},{3,2},{4,0},{5,1},{6,7},{7,6},{8,12},{9,13},{10,... | collective-permute-start | bytes 884744 | tf_op jit(solution)/shard_map/ppermute | solution.py:46
  22.3 3.4 %collective-permute-done.3 = bf16[64,2304]{1,0:T(8,128)(2,1)S(1)} collective-permute-done((bf16[64,2304]{1,0:T(8,128)(2,1)S(1)}, bf16[64,2304]{1,0:T(8,128)(2,1)S(1)}, u32[]{:S(2)}, u32[]{:S(2)}) %collective-permute-start.3) | collective-permute-done | bytes 294944 | tf_op jit(solution)/shard_map/ppermute | solution.py:55
  25.8 0.6 %collective-permute-start.6 = (bf16[64,2304]{1,0:T(8,128)(2,1)S(1)}, bf16[64,2304]{1,0:T(8,128)(2,1)S(1)}, u32[]{:S(2)}, u32[]{:S(2)}) collective-permute-start(bf16[64,2304]{1,0:T(8,128)(2,1)S(1)} %collective-permute-done.3), channel_id=1, source_target_pairs={{0,4},{1,5},{2,3},{3,2},{4,0},{5,1},{6,7},{7,6},{8,12},{9,13},{10,... | collective-permute-start | bytes 884744 | tf_op jit(solution)/shard_map/ppermute | solution.py:46
  26.4 0.0 collective-permute-done.10
  26.5 0.9 %collective-permute-start.15 = (bf16[128,1024]{1,0:T(8,128)(2,1)S(1)}, bf16[128,1024]{1,0:T(8,128)(2,1)S(1)}, u32[]{:S(2)}, u32[]{:S(2)}) collective-permute-start(bf16[128,1024]{1,0:T(8,128)(2,1)S(1)} %add_convert_fusion.1), channel_id=1, source_target_pairs={{0,4},{1,5},{2,3},{3,2},{4,0},{5,1},{6,7},{7,6},{8,12},{9,13},{10,... | collective-permute-start | bytes 786440 | tf_op jit(solution)/shard_map/ppermute | solution.py:46
  27.4 0.1 add_convert_fusion
  27.4 0.7 %collective-permute-start.11 = (bf16[128,1280]{1,0:T(8,128)(2,1)S(1)}, bf16[128,1280]{1,0:T(8,128)(2,1)S(1)}, u32[]{:S(2)}, u32[]{:S(2)}) collective-permute-start(bf16[128,1280]{1,0:T(8,128)(2,1)S(1)} %add_convert_fusion), channel_id=1, source_target_pairs={{0,4},{1,5},{2,3},{3,2},{4,0},{5,1},{6,7},{7,6},{8,12},{9,13},{10,... | collective-permute-start | bytes 983048 | tf_op jit(solution)/shard_map/ppermute | solution.py:46
  28.2 0.0 collective-permute-done.5.refs_0_
  28.2 3.3 %collective-permute-start.4 = (bf16[128,2304]{1,0:T(8,128)(2,1)S(1)}, bf16[128,2304]{1,0:T(8,128)(2,1)S(1)}, u32[]{:S(2)}, u32[]{:S(2)}) collective-permute-start(bf16[128,2304]{1,0:T(8,128)(2,1)S(1)} %pad_maximum_fusion.own_ref), channel_id=1, source_target_pairs={{0,2},{1,3},{2,0},{3,1},{4,6},{5,7},{6,4},{7,5},{8,10},{9,11},{10,... | collective-permute-start | bytes 1769480 | tf_op jit(solution)/shard_map/ppermute | solution.py:46
  31.5 0.0 collective-permute-done.9
  31.5 0.1 collective-permute-start.7
  31.6 2.9 %collective-permute-done.15 = bf16[128,1024]{1,0:T(8,128)(2,1)S(1)} collective-permute-done((bf16[128,1024]{1,0:T(8,128)(2,1)S(1)}, bf16[128,1024]{1,0:T(8,128)(2,1)S(1)}, u32[]{:S(2)}, u32[]{:S(2)}) %collective-permute-start.15) | collective-permute-done | bytes 262176 | tf_op jit(solution)/shard_map/ppermute | solution.py:46
  34.5 0.7 %collective-permute-start.16 = (bf16[64,1024]{1,0:T(8,128)(2,1)S(1)}, bf16[64,1024]{1,0:T(8,128)(2,1)S(1)}, u32[]{:S(2)}, u32[]{:S(2)}) collective-permute-start(bf16[64,1024]{1,0:T(8,128)(2,1)S(1)} %add_convert_fusion.3), channel_id=1, source_target_pairs={{0,1},{1,0},{2,6},{3,7},{4,5},{5,4},{6,2},{7,3},{8,9},{9,8},{10,14... | collective-permute-start | bytes 393224 | tf_op jit(solution)/shard_map/ppermute | solution.py:46
  35.2 0.0 collective-permute-done.6.refs_1_
  35.2 3.5 %collective-permute-start.8 = (bf16[64,2304]{1,0:T(8,128)(2,1)S(1)}, bf16[64,2304]{1,0:T(8,128)(2,1)S(1)}, u32[]{:S(2)}, u32[]{:S(2)}) collective-permute-start(bf16[64,2304]{1,0:T(8,128)(2,1)S(1)} %collective-permute-done.6.refs_1_), channel_id=1, source_target_pairs={{0,2},{1,3},{2,0},{3,1},{4,6},{5,7},{6,4},{7,5},{8,10},{9,11},{10,... | collective-permute-start | bytes 884744 | tf_op jit(solution)/shard_map/ppermute | solution.py:46
  38.7 0.0 collective-permute-done.11
  38.7 0.1 add_convert_fusion.2
  38.8 1.3 %collective-permute-start.12 = (bf16[64,1280]{1,0:T(8,128)(2,1)S(1)}, bf16[64,1280]{1,0:T(8,128)(2,1)S(1)}, u32[]{:S(2)}, u32[]{:S(2)}) collective-permute-start(bf16[64,1280]{1,0:T(8,128)(2,1)S(1)} %add_convert_fusion.2), channel_id=1, source_target_pairs={{0,1},{1,0},{2,6},{3,7},{4,5},{5,4},{6,2},{7,3},{8,9},{9,8},{10,14... | collective-permute-start | bytes 491528 | tf_op jit(solution)/shard_map/ppermute | solution.py:46
  40.1 0.0 collective-permute-done.16
  40.1 0.1 convert_add_fusion.1
  40.2 0.4 collective-permute-start.17
  40.5 2.9 %collective-permute-done.12 = bf16[64,1280]{1,0:T(8,128)(2,1)S(1)} collective-permute-done((bf16[64,1280]{1,0:T(8,128)(2,1)S(1)}, bf16[64,1280]{1,0:T(8,128)(2,1)S(1)}, u32[]{:S(2)}, u32[]{:S(2)}) %collective-permute-start.12) | collective-permute-done | bytes 163872 | tf_op jit(solution)/shard_map/ppermute | solution.py:46
  43.4 0.1 convert_add_fusion
  43.5 0.1 collective-permute-start.13
  43.6 0.0 collective-permute-done.17
  43.6 8.2 %collective-permute-start.18 = (bf16[32,1024]{1,0:T(8,128)(2,1)S(1)}, bf16[32,1024]{1,0:T(8,128)(2,1)S(1)}, u32[]{:S(2)}, u32[]{:S(2)}) collective-permute-start(bf16[32,1024]{1,0:T(8,128)(2,1)S(1)} %get-tuple-element.24), channel_id=1, source_target_pairs={{0,31},{1,30},{2,29},{3,28},{4,27},{5,26},{6,25},{7,24},{8,23},{9,... | collective-permute-start | bytes 196616 | tf_op jit(solution)/shard_map/ppermute | solution.py:55
  51.8 0.0 collective-permute-done.13
  51.9 4.8 %collective-permute-start.14 = (bf16[32,1280]{1,0:T(8,128)(2,1)S(1)}, bf16[32,1280]{1,0:T(8,128)(2,1)S(1)}, u32[]{:S(2)}, u32[]{:S(2)}) collective-permute-start(bf16[32,1280]{1,0:T(8,128)(2,1)S(1)} %get-tuple-element.26), channel_id=1, source_target_pairs={{0,31},{1,30},{2,29},{3,28},{4,27},{5,26},{6,25},{7,24},{8,23},{9,... | collective-permute-start | bytes 245768 | tf_op jit(solution)/shard_map/ppermute | solution.py:55
  56.7 2.3 %shard_map.62 = (bf16[512,512]{1,0:T(8,128)(2,1)S(1)}, bf16[256,512]{1,0:T(8,128)(2,1)S(1)}) custom-call(s32[1]{0:T(128)} %bitcast.device_ref, bf16[1024,2304]{1,0:T(8,128)(2,1)S(1)} %get-tuple-element.16.windows_ref, bf16[128,2304]{1,0:T(8,128)(2,1)S(1)} %pad_maximum_fusion.own_ref, bf16[128,2304]{1,0:T(8,128)(2,1)S(1)} %collective-permute-done.4.other_ref), custom_call_target="tpu_custom_call" | custom-call | flops 1207959552 | bytes 6684672 | tf_op jit(solution)/shard_map/pallas_call | solution.py:263
  59.0 0.0 collective-permute-done.8.refs_3_
  59.0 2.9 %shard_map.63 = bf16[512,512]{1,0:T(8,128)(2,1)} custom-call(bf16[1024,2304]{1,0:T(8,128)(2,1)S(1)} %get-tuple-element.16.windows_ref, bf16[512,512]{1,0:T(8,128)(2,1)S(1)} %get-tuple-element.17.early_ref, bf16[256,512]{1,0:T(8,128)(2,1)S(1)} %get-tuple-element.18.chosen_ref, bf16[64,2304]{1,0:T(8,128)(2,1)S(1)} %collective-permute-done.5.refs_0_, ...), custom_call_target="tpu_custom_call" | custom-call | flops 1207959552 | bytes 7208960 | tf_op jit(solution)/shard_map/pallas_call | solution.py:263
  61.9 0.0 collective-permute-done.18.refs_3_
  62.0 1.3 %shard_map.65 = f32[9,16,512]{2,1,0:T(8,128)} custom-call(f32[32,1280]{1,0:T(8,128)S(1)} %get-tuple-element.27.refs_0_, bf16[32,1280]{1,0:T(8,128)(2,1)S(1)} %collective-permute-done.14.refs_1_, f32[32,1024]{1,0:T(8,128)S(1)} %get-tuple-element.25.refs_2_, bf16[32,1024]{1,0:T(8,128)(2,1)S(1)} %collective-permute-done.18.refs_3_), custom_call_target="tpu_custom_call" | custom-call | flops 37748736 | bytes 737280 | tf_op jit(solution)/shard_map/pallas_call | solution.py:263
  (14 shorter events, 0.2 us)
Async XLA Ops:
  0.6 12.9 %copy-start = (bf16[16,9,512]{2,0,1:T(8,128)(2,1)S(1)}, bf16[16,9,512]{2,0,1:T(8,128)(2,1)}, u32[]{:S(2)}) copy-start(bf16[16,9,512]{2,0,1:T(8,128)(2,1)} %param.7) | copy-start | bytes 442372
  1.5 7.7 %collective-permute-start = (bf16[2,4,512]{2,1,0:T(4,128)(2,1)S(1)}, bf16[2,4,512]{2,1,0:T(4,128)(2,1)S(1)}, u32[]{:S(2)}, u32[]{:S(2)}) collective-permute-start(bf16[2,4,512]{2,1,0:T(4,128)(2,1)S(1)} %fusion.16), channel_id=1, source_target_pairs={{0,1},{1,0},{2,3},{3,2},{4,5},{5,4},{6,7},{7,6},{8,9},{9,8},{10,11... | collective-permute-start | bytes 24584 | tf_op jit(solution)/shard_map/ppermute | solution.py:286
  1.8 11.7 %collective-permute-start.1 = (bf16[9,16,512]{2,1,0:T(8,128)(2,1)}, bf16[9,16,512]{2,1,0:T(8,128)(2,1)S(1)}, u32[]{:S(2)}, u32[]{:S(2)}) collective-permute-start(bf16[9,16,512]{2,1,0:T(8,128)(2,1)} %bitcast.5), channel_id=1, source_target_pairs={{0,31},{1,30},{2,29},{3,28},{4,27},{5,26},{6,25},{7,24},{8,23},{9,... | collective-permute-start | bytes 442376 | tf_op jit(solution)/shard_map/ppermute | solution.py:55
  14.0 4.4 %collective-permute-start.2 = (bf16[32,2304]{1,0:T(8,128)(2,1)S(1)}, bf16[32,2304]{1,0:T(8,128)(2,1)S(1)}, u32[]{:S(2)}, u32[]{:S(2)}) collective-permute-start(bf16[32,2304]{1,0:T(8,128)(2,1)S(1)} %shard_map.61), channel_id=1, source_target_pairs={{0,1},{1,0},{2,6},{3,7},{4,5},{5,4},{6,2},{7,3},{8,9},{9,8},{10,14... | collective-permute-start | bytes 442376 | tf_op jit(solution)/shard_map/ppermute | solution.py:46
  16.6 9.9 %collective-permute-start.10 = (bf16[128,2304]{1,0:T(8,128)(2,1)S(1)}, bf16[128,2304]{1,0:T(8,128)(2,1)S(1)}, u32[]{:S(2)}, u32[]{:S(2)}) collective-permute-start(bf16[128,2304]{1,0:T(8,128)(2,1)S(1)} %get-tuple-element.23), channel_id=1, source_target_pairs={{0,2},{1,3},{2,0},{3,1},{4,6},{5,7},{6,4},{7,5},{8,10},{9,11},{10,... | collective-permute-start | bytes 1769480 | tf_op jit(solution)/shard_map/ppermute | solution.py:46
  18.4 7.4 %collective-permute-start.3 = (bf16[64,2304]{1,0:T(8,128)(2,1)S(1)}, bf16[64,2304]{1,0:T(8,128)(2,1)S(1)}, u32[]{:S(2)}, u32[]{:S(2)}) collective-permute-start(bf16[64,2304]{1,0:T(8,128)(2,1)S(1)} %pad_maximum_fusion.1), channel_id=1, source_target_pairs={{0,8},{1,9},{2,10},{3,11},{4,12},{5,13},{6,14},{7,15},{8,0},{9,1},... | collective-permute-start | bytes 884744 | tf_op jit(solution)/shard_map/ppermute | solution.py:55
  19.9 11.6 %collective-permute-start.9 = (bf16[128,2304]{1,0:T(8,128)(2,1)S(1)}, bf16[128,2304]{1,0:T(8,128)(2,1)S(1)}, u32[]{:S(2)}, u32[]{:S(2)}) collective-permute-start(bf16[128,2304]{1,0:T(8,128)(2,1)S(1)} %get-tuple-element.21), channel_id=1, source_target_pairs={{0,2},{1,3},{2,0},{3,1},{4,6},{5,7},{6,4},{7,5},{8,10},{9,11},{10,... | collective-permute-start | bytes 1769480 | tf_op jit(solution)/shard_map/ppermute | solution.py:46
  21.2 7.0 %collective-permute-start.5 = (bf16[64,2304]{1,0:T(8,128)(2,1)S(1)}, bf16[64,2304]{1,0:T(8,128)(2,1)S(1)}, u32[]{:S(2)}, u32[]{:S(2)}) collective-permute-start(bf16[64,2304]{1,0:T(8,128)(2,1)S(1)} %pad_maximum_fusion.1), channel_id=1, source_target_pairs={{0,4},{1,5},{2,3},{3,2},{4,0},{5,1},{6,7},{7,6},{8,12},{9,13},{10,... | collective-permute-start | bytes 884744 | tf_op jit(solution)/shard_map/ppermute | solution.py:46
  25.8 9.4 %collective-permute-start.6 = (bf16[64,2304]{1,0:T(8,128)(2,1)S(1)}, bf16[64,2304]{1,0:T(8,128)(2,1)S(1)}, u32[]{:S(2)}, u32[]{:S(2)}) collective-permute-start(bf16[64,2304]{1,0:T(8,128)(2,1)S(1)} %collective-permute-done.3), channel_id=1, source_target_pairs={{0,4},{1,5},{2,3},{3,2},{4,0},{5,1},{6,7},{7,6},{8,12},{9,13},{10,... | collective-permute-start | bytes 884744 | tf_op jit(solution)/shard_map/ppermute | solution.py:46
  26.5 8.0 %collective-permute-start.15 = (bf16[128,1024]{1,0:T(8,128)(2,1)S(1)}, bf16[128,1024]{1,0:T(8,128)(2,1)S(1)}, u32[]{:S(2)}, u32[]{:S(2)}) collective-permute-start(bf16[128,1024]{1,0:T(8,128)(2,1)S(1)} %add_convert_fusion.1), channel_id=1, source_target_pairs={{0,4},{1,5},{2,3},{3,2},{4,0},{5,1},{6,7},{7,6},{8,12},{9,13},{10,... | collective-permute-start | bytes 786440 | tf_op jit(solution)/shard_map/ppermute | solution.py:46
  27.4 11.3 %collective-permute-start.11 = (bf16[128,1280]{1,0:T(8,128)(2,1)S(1)}, bf16[128,1280]{1,0:T(8,128)(2,1)S(1)}, u32[]{:S(2)}, u32[]{:S(2)}) collective-permute-start(bf16[128,1280]{1,0:T(8,128)(2,1)S(1)} %add_convert_fusion), channel_id=1, source_target_pairs={{0,4},{1,5},{2,3},{3,2},{4,0},{5,1},{6,7},{7,6},{8,12},{9,13},{10,... | collective-permute-start | bytes 983048 | tf_op jit(solution)/shard_map/ppermute | solution.py:46
  28.2 28.5 %collective-permute-start.4 = (bf16[128,2304]{1,0:T(8,128)(2,1)S(1)}, bf16[128,2304]{1,0:T(8,128)(2,1)S(1)}, u32[]{:S(2)}, u32[]{:S(2)}) collective-permute-start(bf16[128,2304]{1,0:T(8,128)(2,1)S(1)} %pad_maximum_fusion.own_ref), channel_id=1, source_target_pairs={{0,2},{1,3},{2,0},{3,1},{4,6},{5,7},{6,4},{7,5},{8,10},{9,11},{10,... | collective-permute-start | bytes 1769480 | tf_op jit(solution)/shard_map/ppermute | solution.py:46
  31.5 27.5 %collective-permute-start.7 = (bf16[64,2304]{1,0:T(8,128)(2,1)S(1)}, bf16[64,2304]{1,0:T(8,128)(2,1)S(1)}, u32[]{:S(2)}, u32[]{:S(2)}) collective-permute-start(bf16[64,2304]{1,0:T(8,128)(2,1)S(1)} %collective-permute-done.5.refs_0_), channel_id=1, source_target_pairs={{0,2},{1,3},{2,0},{3,1},{4,6},{5,7},{6,4},{7,5},{8,10},{9,11},{10,... | collective-permute-start | bytes 884744 | tf_op jit(solution)/shard_map/ppermute | solution.py:46
  34.5 5.6 %collective-permute-start.16 = (bf16[64,1024]{1,0:T(8,128)(2,1)S(1)}, bf16[64,1024]{1,0:T(8,128)(2,1)S(1)}, u32[]{:S(2)}, u32[]{:S(2)}) collective-permute-start(bf16[64,1024]{1,0:T(8,128)(2,1)S(1)} %add_convert_fusion.3), channel_id=1, source_target_pairs={{0,1},{1,0},{2,6},{3,7},{4,5},{5,4},{6,2},{7,3},{8,9},{9,8},{10,14... | collective-permute-start | bytes 393224 | tf_op jit(solution)/shard_map/ppermute | solution.py:46
  35.2 23.8 %collective-permute-start.8 = (bf16[64,2304]{1,0:T(8,128)(2,1)S(1)}, bf16[64,2304]{1,0:T(8,128)(2,1)S(1)}, u32[]{:S(2)}, u32[]{:S(2)}) collective-permute-start(bf16[64,2304]{1,0:T(8,128)(2,1)S(1)} %collective-permute-done.6.refs_1_), channel_id=1, source_target_pairs={{0,2},{1,3},{2,0},{3,1},{4,6},{5,7},{6,4},{7,5},{8,10},{9,11},{10,... | collective-permute-start | bytes 884744 | tf_op jit(solution)/shard_map/ppermute | solution.py:46
  38.8 4.6 %collective-permute-start.12 = (bf16[64,1280]{1,0:T(8,128)(2,1)S(1)}, bf16[64,1280]{1,0:T(8,128)(2,1)S(1)}, u32[]{:S(2)}, u32[]{:S(2)}) collective-permute-start(bf16[64,1280]{1,0:T(8,128)(2,1)S(1)} %add_convert_fusion.2), channel_id=1, source_target_pairs={{0,1},{1,0},{2,6},{3,7},{4,5},{5,4},{6,2},{7,3},{8,9},{9,8},{10,14... | collective-permute-start | bytes 491528 | tf_op jit(solution)/shard_map/ppermute | solution.py:46
  40.2 3.4 %collective-permute-start.17 = (bf16[32,1024]{1,0:T(8,128)(2,1)S(1)}, bf16[32,1024]{1,0:T(8,128)(2,1)S(1)}, u32[]{:S(2)}, u32[]{:S(2)}) collective-permute-start(bf16[32,1024]{1,0:T(8,128)(2,1)S(1)} %slice.137), channel_id=1, source_target_pairs={{0,8},{1,9},{2,10},{3,11},{4,12},{5,13},{6,14},{7,15},{8,0},{9,1},... | collective-permute-start | bytes 196616 | tf_op jit(solution)/shard_map/ppermute | solution.py:55
  43.5 8.3 %collective-permute-start.13 = (bf16[32,1280]{1,0:T(8,128)(2,1)S(1)}, bf16[32,1280]{1,0:T(8,128)(2,1)S(1)}, u32[]{:S(2)}, u32[]{:S(2)}) collective-permute-start(bf16[32,1280]{1,0:T(8,128)(2,1)S(1)} %slice.136), channel_id=1, source_target_pairs={{0,8},{1,9},{2,10},{3,11},{4,12},{5,13},{6,14},{7,15},{8,0},{9,1},... | collective-permute-start | bytes 245768 | tf_op jit(solution)/shard_map/ppermute | solution.py:55
  43.6 18.3 %collective-permute-start.18 = (bf16[32,1024]{1,0:T(8,128)(2,1)S(1)}, bf16[32,1024]{1,0:T(8,128)(2,1)S(1)}, u32[]{:S(2)}, u32[]{:S(2)}) collective-permute-start(bf16[32,1024]{1,0:T(8,128)(2,1)S(1)} %get-tuple-element.24), channel_id=1, source_target_pairs={{0,31},{1,30},{2,29},{3,28},{4,27},{5,26},{6,25},{7,24},{8,23},{9,... | collective-permute-start | bytes 196616 | tf_op jit(solution)/shard_map/ppermute | solution.py:55
  51.9 10.1 %collective-permute-start.14 = (bf16[32,1280]{1,0:T(8,128)(2,1)S(1)}, bf16[32,1280]{1,0:T(8,128)(2,1)S(1)}, u32[]{:S(2)}, u32[]{:S(2)}) collective-permute-start(bf16[32,1280]{1,0:T(8,128)(2,1)S(1)} %get-tuple-element.26), channel_id=1, source_target_pairs={{0,31},{1,30},{2,29},{3,28},{4,27},{5,26},{6,25},{7,24},{8,23},{9,... | collective-permute-start | bytes 245768 | tf_op jit(solution)/shard_map/ppermute | solution.py:55

commit v8 on v7

--- a/solution.py
+++ b/solution.py
@@ -57,12 +57,12 @@
     def complement(self, block):
         return self.shift(block, self.count - 1)
 
-    def source(self, position, device, rows, turns):
+    def source(self, position, device, rows):
         shift = rows.bit_length() - 1
         slot, low = position >> shift, position & (rows - 1)
         bit = self.count.bit_length() - 2
         owner = device
-        for turn in turns:
+        for turn in ("core", "a", "b", "rest", "mirror"):
             if turn == "rest":
                 masks = [mask for group in self.groups for mask in reversed(group)]
             elif turn == "core":
@@ -79,20 +79,16 @@
         return (owner << shift) + low
 
 
-SUM_TURNS = ("core", "a", "b", "rest", "mirror")
-GET_TURNS = ("core", "a", "rest", "b", "mirror")
-
-
 def anti_identity(size):
     row = lax.broadcasted_iota(jnp.int32, (size, size), 0)
     col = lax.broadcasted_iota(jnp.int32, (size, size), 1)
     return jnp.where(row + col == size - 1, 1.0, 0.0).astype(BF16)
 
 
-def selection(plan, device, rows, width, turns):
+def selection(plan, device, rows, width):
     position = lax.broadcasted_iota(jnp.int32, (width, 128), 0)
     lane = lax.broadcasted_iota(jnp.int32, (width, 128), 1)
-    source = plan.source(position, device, rows, turns)
+    source = plan.source(position, device, rows)
 
     def one_hot(index):
         return jnp.concatenate(
@@ -126,7 +122,7 @@
     copies = [pltpu.make_async_copy(far, near, arrived.at[i]) for i, (far, near) in enumerate(pairs)]
     for copy in copies:
         copy.start()
-    direct, mirror = selection(plan, device_ref[0], rows, width, SUM_TURNS)
+    direct, mirror = selection(plan, device_ref[0], rows, width)
     for copy in copies:
         copy.wait()
     values = values_ref[...]
@@ -192,18 +188,15 @@
     return (dot(windows_ref[:count, :], weights, NT) + dot(windows_ref[count:, :], mirrored, NT)).astype(BF16)
 
 
-def chosen_rows(direct, weight_refs, begins):
-    return jnp.concatenate([direct[a : a + ref.shape[0], :] for ref, a in zip(weight_refs, begins)], axis=0)
-
-
-def early_input_kernel(plan, rows, begins, late_begins, device_ref, windows_ref, own_ref, other_ref, out_ref, late_ref):
-    refs = (own_ref, other_ref)
-    direct, _ = selection(plan, device_ref[0], rows, out_ref.shape[1], GET_TURNS)
-    out_ref[...] = dot(rounded_sums(2 * rows, windows_ref, refs), chosen_rows(direct, refs, begins)).astype(BF16)
-    place = 0
-    for begin, size in late_begins:
-        late_ref[place : place + size, :] = direct[begin : begin + size, :]
-        place += size
+def chosen_rows(direct, places):
+    return jnp.concatenate([direct[begin : begin + size, :] for begin, size in places], axis=0)
+
+
+def early_input_kernel(plan, rows, places, late_places, device_ref, windows_ref, own_ref, other_ref, out_ref, late_ref):
+    direct, _ = selection(plan, device_ref[0], rows, out_ref.shape[1])
+    sums = rounded_sums(2 * rows, windows_ref, (own_ref, other_ref))
+    out_ref[...] = dot(sums, chosen_rows(direct, places)).astype(BF16)
+    late_ref[...] = chosen_rows(direct, late_places)
 
 
 def late_input_kernel(group, windows_ref, early_ref, chosen_ref, *refs):
@@ -371,24 +364,31 @@
         tied_kernel, [((2 * rows, depth), BF16, True)], (by_tap, far_weight),
         flops=4 * rows * depth * half, given=(1,),
     )
-    gathered = jnp.concatenate([gathered, plan.swap(gathered, "b")], axis=0)
-    for place in range(len(plan.groups) - 1, -1, -1):
-        pieces = [plan.shift(gathered, mask) for mask in plan.group_masks(plan.groups[place])[1:]]
-        if place:
-            gathered = jnp.concatenate([gathered] + pieces, axis=0)
-        else:
-            relayed = jnp.concatenate(pieces, axis=0)
-    size = gathered.shape[0]
-    late = [plan.swap(gathered, "a")]
-    late.append(plan.swap(relayed, "a"))
-    gathered = jnp.concatenate([gathered, relayed], axis=0)
-    span = gathered.shape[0]
+    parts = [gathered, plan.swap(gathered, "b")]
+    for place in range(len(plan.groups) - 1, 0, -1):
+        masks = plan.group_masks(plan.groups[place])[1:]
+        parts = [jnp.concatenate([part] + [plan.shift(part, mask) for mask in masks], axis=0) for part in parts]
+    masks = plan.group_masks(plan.groups[0])
+    relayed = []
+    for place in range(2):
+        relayed.append(jnp.concatenate([plan.shift(parts[place], mask) for mask in masks[1:]], axis=0))
+    late = [plan.swap(jnp.concatenate(parts, axis=0), "a")]
+    late.append(plan.swap(jnp.concatenate(relayed, axis=0), "a"))
+    gathered = jnp.concatenate(parts + relayed, axis=0)
+    span, size = gathered.shape[0], parts[0].shape[0]
+
+    def places(base):
+        return [
+            (base + side * span // 2 + begin, n)
+            for begin, n in ((0, size), (size, span // 2 - size)) for side in range(2)
+        ]
+
     other = plan.swap(gathered, "core")
     for place in range(2):
         late.append(plan.swap(late[place], "core"))
-    late_begins = [(begin, n) for core in (span, 3 * span) for begin, n in ((core, size), (core + size, span - size))]
+    early_places, late_places = places(0) + places(2 * span), places(span) + places(3 * span)
     early, chosen = call(
-        functools.partial(early_input_kernel, plan, rows, (0, 2 * span), late_begins),
+        functools.partial(early_input_kernel, plan, rows, early_places, late_places),
         [((count, width), BF16, True), ((half, width), BF16, True)], (device, windows, gathered, other),
         scalars=1, flops=work, given=(1, 2, 3),
     )

time: 63.9 us -> 64.5 us (level)
  the two profiles are of different devices: /device:TPU:11 before, /device:TPU:1 now
where the time goes in v8:
time: 64.5 us; the launch traced here: 64.3 us
  starting transfers between devices  31.4 us (49%)
  waiting for transfers between devices  17.5 us (27%)
  Pallas kernels  13.3 us (21%)
  other arithmetic  1.31 us (2%)
  between operations  0.82 us (1%)
    ppermute x7, starting transfers between devices, shift(): return lax.ppermute(block, AXES, [(d, d ^ mask) for d in range(self.count)])  19.9 us
    pallas_call x7, Pallas kernels, call(): pl.pallas_call(kernel, out_shape=[(ON_CHIP if stays else jax.ShapeDtypeSt...  13.3 us
    ppermute x7, waiting for transfers between devices, shift(): return lax.ppermute(block, AXES, [(d, d ^ mask) for d in range(self.count)])  9.91 us
    ppermute x12, starting transfers between devices, swap(): return lax.ppermute(block, AXES, route)  9.36 us
    ppermute x12, waiting for transfers between devices, swap(): return lax.ppermute(block, AXES, route)  7.55 us
    ppermute x1, starting transfers between devices, edges(): lax.ppermute(jnp.where(where == 0, top, bottom), 'pos', [(0, 1), (1, 0)])  2.09 us
  transfers between devices with their start and end apart: 20, of which 8 were waited for; matrix products, arithmetic and copies ran while one was open for 1% of the time, Pallas kernels for 18%

profile of v8, /device:TPU:1, one launch (start us, length us, event | category | flops | bytes accessed | tf_op | source)
XLA Modules:
  0.0 64.3 jit_solution(11208800356013087940)
XLA Ops:
  0.6 0.0 copy-start
  0.6 0.8 %fusion.16 = bf16[2,4,512]{2,1,0:T(4,128)(2,1)S(1)} fusion(bf16[2,256,512]{2,1,0:T(8,128)(2,1)} %pre_hbm.1, bf16[2,256,512]{2,1,0:T(8,128)(2,1)} %out_grad_hbm.1, pred[]{:T(512)S(6)} %eq.2), kind=kLoop, calls=%fused_computation.38 | loop fusion | flops 102400 | bytes 40961 | tf_op jit(solution)/shard_map/jit(_where)/select_n | solution.py:279
  1.5 2.1 %collective-permute-start = (bf16[2,4,512]{2,1,0:T(4,128)(2,1)S(1)}, bf16[2,4,512]{2,1,0:T(4,128)(2,1)S(1)}, u32[]{:S(2)}, u32[]{:S(2)}) collective-permute-start(bf16[2,4,512]{2,1,0:T(4,128)(2,1)S(1)} %fusion.16), channel_id=1, source_target_pairs={{0,1},{1,0},{2,3},{3,2},{4,5},{5,4},{6,7},{7,6},{8,9},{9,8},{10,11... | collective-permute-start | bytes 24584 | tf_op jit(solution)/shard_map/ppermute | solution.py:279
  3.6 5.1 %collective-permute-start.1 = (bf16[9,16,512]{2,1,0:T(8,128)(2,1)}, bf16[9,16,512]{2,1,0:T(8,128)(2,1)S(1)}, u32[]{:S(2)}, u32[]{:S(2)}) collective-permute-start(bf16[9,16,512]{2,1,0:T(8,128)(2,1)} %bitcast.5), channel_id=1, source_target_pairs={{0,31},{1,30},{2,29},{3,28},{4,27},{5,26},{6,25},{7,24},{8,23},{9,... | collective-permute-start | bytes 442376 | tf_op jit(solution)/shard_map/ppermute | solution.py:55
  8.7 3.3 %shard_map.59 = (bf16[256,1024]{1,0:T(8,128)(2,1)S(1)}, bf16[256,1024]{1,0:T(8,128)(2,1)S(1)}, f32[4,272,256]{2,1,0:T(8,128)S(1)}, bf16[1024,2304]{1,0:T(8,128)(2,1)S(1)}) custom-call(s32[1]{0:T(128)} %bitcast.device_ref, bf16[512,512]{1,0:T(8,128)(2,1)} %bitcast.9, bf16[2,256,512]{2,1,0:T(8,128)(2,1)} %pre_hbm.1, bf16[2,256,512]{2,1,0:T(8,128)(2,1)} %out_grad_hbm.1), custom_call_target="tpu_custom_call" | custom-call | flops 536870912 | bytes 8454144 | tf_op jit(solution)/shard_map/pallas_call | solution.py:256
  12.0 0.0 collective-permute-done
  12.1 1.5 %collective-permute-done.1.far_ref = bf16[9,16,512]{2,1,0:T(8,128)(2,1)S(1)} collective-permute-done((bf16[9,16,512]{2,1,0:T(8,128)(2,1)}, bf16[9,16,512]{2,1,0:T(8,128)(2,1)S(1)}, u32[]{:S(2)}, u32[]{:S(2)}) %collective-permute-start.1) | collective-permute-done | bytes 147488 | tf_op jit(solution)/shard_map/ppermute | solution.py:55
  13.6 0.5 shard_map.61
  14.2 1.3 %collective-permute-start.2 = (bf16[32,2304]{1,0:T(8,128)(2,1)S(1)}, bf16[32,2304]{1,0:T(8,128)(2,1)S(1)}, u32[]{:S(2)}, u32[]{:S(2)}) collective-permute-start(bf16[32,2304]{1,0:T(8,128)(2,1)S(1)} %shard_map.61), channel_id=1, source_target_pairs={{0,1},{1,0},{2,6},{3,7},{4,5},{5,4},{6,2},{7,3},{8,9},{9,8},{10,14... | collective-permute-start | bytes 442376 | tf_op jit(solution)/shard_map/ppermute | solution.py:46
  15.5 1.5 %shard_map.60 = (bf16[128,2304]{1,0:T(8,128)(2,1)S(1)}, f32[128,2304]{1,0:T(8,128)S(1)}, f32[4,272,256]{2,1,0:T(8,128)S(1)}, bf16[1024,2304]{1,0:T(8,128)(2,1)S(1)}) custom-call(bf16[256,1024]{1,0:T(8,128)(2,1)S(1)} %get-tuple-element.13.order_ref, bf16[2,8,512]{2,1,0:T(8,128)(2,1)S(1)} %pad_maximum_fusion.3.halo_ref, ...), custom_call_target="tpu_custom_call", output_to_operand_aliasing={{2}: (2, {}), {3}: (3, {})} | custom-call | flops 1207959552 | bytes 13975552 | tf_op jit(solution)/shard_map/pallas_call | solution.py:256
  17.0 0.1 collective-permute-start.11
  17.1 1.4 %shard_map.64 = (bf16[128,2304]{1,0:T(8,128)(2,1)S(1)}, f32[128,2304]{1,0:T(8,128)S(1)}) custom-call(bf16[256,1024]{1,0:T(8,128)(2,1)S(1)} %get-tuple-element.19.order_ref, bf16[1024,2304]{1,0:T(8,128)(2,1)S(1)} %get-tuple-element.16.windows_ref), custom_call_target="tpu_custom_call" | custom-call | flops 1207959552 | bytes 7012352 | tf_op jit(solution)/shard_map/pallas_call | solution.py:256
  18.5 0.6 collective-permute-start.10
  19.0 2.6 %collective-permute-start.3 = (bf16[32,2304]{1,0:T(8,128)(2,1)S(1)}, bf16[32,2304]{1,0:T(8,128)(2,1)S(1)}, u32[]{:S(2)}, u32[]{:S(2)}) collective-permute-start(bf16[32,2304]{1,0:T(8,128)(2,1)S(1)} %shard_map.61), channel_id=1, source_target_pairs={{0,8},{1,9},{2,10},{3,11},{4,12},{5,13},{6,14},{7,15},{8,0},{9,1},... | collective-permute-start | bytes 442376 | tf_op jit(solution)/shard_map/ppermute | solution.py:55
  21.7 0.0 collective-permute-done.2
  21.7 0.0 collective-permute-start.4
  21.7 0.9 %collective-permute-start.6 = (bf16[64,2304]{1,0:T(8,128)(2,1)S(1)}, bf16[64,2304]{1,0:T(8,128)(2,1)S(1)}, u32[]{:S(2)}, u32[]{:S(2)}) collective-permute-start(bf16[64,2304]{1,0:T(8,128)(2,1)S(1)} %pad_maximum_fusion.1), channel_id=1, source_target_pairs={{0,4},{1,5},{2,3},{3,2},{4,0},{5,1},{6,7},{7,6},{8,12},{9,13},{10,... | collective-permute-start | bytes 884744 | tf_op jit(solution)/shard_map/ppermute | solution.py:46
  22.6 3.2 %collective-permute-done.3 = bf16[32,2304]{1,0:T(8,128)(2,1)S(1)} collective-permute-done((bf16[32,2304]{1,0:T(8,128)(2,1)S(1)}, bf16[32,2304]{1,0:T(8,128)(2,1)S(1)}, u32[]{:S(2)}, u32[]{:S(2)}) %collective-permute-start.3) | collective-permute-done | bytes 147488 | tf_op jit(solution)/shard_map/ppermute | solution.py:55
  25.8 3.2 %collective-permute-done.4 = bf16[32,2304]{1,0:T(8,128)(2,1)S(1)} collective-permute-done((bf16[32,2304]{1,0:T(8,128)(2,1)S(1)}, bf16[32,2304]{1,0:T(8,128)(2,1)S(1)}, u32[]{:S(2)}, u32[]{:S(2)}) %collective-permute-start.4) | collective-permute-done | bytes 147488 | tf_op jit(solution)/shard_map/ppermute | solution.py:55
  29.0 0.5 collective-permute-start.7
  29.5 1.1 %collective-permute-start.16 = (bf16[128,1024]{1,0:T(8,128)(2,1)S(1)}, bf16[128,1024]{1,0:T(8,128)(2,1)S(1)}, u32[]{:S(2)}, u32[]{:S(2)}) collective-permute-start(bf16[128,1024]{1,0:T(8,128)(2,1)S(1)} %add_convert_fusion.1), channel_id=1, source_target_pairs={{0,4},{1,5},{2,3},{3,2},{4,0},{5,1},{6,7},{7,6},{8,12},{9,13},{10,... | collective-permute-start | bytes 786440 | tf_op jit(solution)/shard_map/ppermute | solution.py:46
  30.6 0.1 add_convert_fusion
  30.7 0.5 collective-permute-start.12
  31.2 0.0 collective-permute-done.6.refs_0_
  31.2 1.9 %collective-permute-start.5 = (bf16[128,2304]{1,0:T(8,128)(2,1)S(1)}, bf16[128,2304]{1,0:T(8,128)(2,1)S(1)}, u32[]{:S(2)}, u32[]{:S(2)}) collective-permute-start(bf16[128,2304]{1,0:T(8,128)(2,1)S(1)} %pad_maximum_fusion.own_ref), channel_id=1, source_target_pairs={{0,2},{1,3},{2,0},{3,1},{4,6},{5,7},{6,4},{7,5},{8,10},{9,11},{10,... | collective-permute-start | bytes 1769480 | tf_op jit(solution)/shard_map/ppermute | solution.py:46
  33.1 0.1 collective-permute-start.8
  33.2 1.7 %collective-permute-done.7.refs_1_ = bf16[64,2304]{1,0:T(8,128)(2,1)S(1)} collective-permute-done((bf16[64,2304]{1,0:T(8,128)(2,1)S(1)}, bf16[64,2304]{1,0:T(8,128)(2,1)S(1)}, u32[]{:S(2)}, u32[]{:S(2)}) %collective-permute-start.7) | collective-permute-done | bytes 294944 | tf_op jit(solution)/shard_map/ppermute | solution.py:46
  34.9 1.5 %collective-permute-start.9 = (bf16[64,2304]{1,0:T(8,128)(2,1)S(1)}, bf16[64,2304]{1,0:T(8,128)(2,1)S(1)}, u32[]{:S(2)}, u32[]{:S(2)}) collective-permute-start(bf16[64,2304]{1,0:T(8,128)(2,1)S(1)} %collective-permute-done.7.refs_1_), channel_id=1, source_target_pairs={{0,2},{1,3},{2,0},{3,1},{4,6},{5,7},{6,4},{7,5},{8,10},{9,11},{10,... | collective-permute-start | bytes 884744 | tf_op jit(solution)/shard_map/ppermute | solution.py:46
  36.4 1.3 %collective-permute-done.16 = bf16[128,1024]{1,0:T(8,128)(2,1)S(1)} collective-permute-done((bf16[128,1024]{1,0:T(8,128)(2,1)S(1)}, bf16[128,1024]{1,0:T(8,128)(2,1)S(1)}, u32[]{:S(2)}, u32[]{:S(2)}) %collective-permute-start.16) | collective-permute-done | bytes 262176 | tf_op jit(solution)/shard_map/ppermute | solution.py:46
  37.8 0.5 collective-permute-start.17
  38.3 3.0 %collective-permute-done.12 = bf16[128,1280]{1,0:T(8,128)(2,1)S(1)} collective-permute-done((bf16[128,1280]{1,0:T(8,128)(2,1)S(1)}, bf16[128,1280]{1,0:T(8,128)(2,1)S(1)}, u32[]{:S(2)}, u32[]{:S(2)}) %collective-permute-start.12) | collective-permute-done | bytes 327712 | tf_op jit(solution)/shard_map/ppermute | solution.py:46
  41.2 0.1 add_convert_fusion.2
  41.3 0.5 collective-permute-start.13
  41.8 1.6 %collective-permute-done.17 = bf16[64,1024]{1,0:T(8,128)(2,1)S(1)} collective-permute-done((bf16[64,1024]{1,0:T(8,128)(2,1)S(1)}, bf16[64,1024]{1,0:T(8,128)(2,1)S(1)}, u32[]{:S(2)}, u32[]{:S(2)}) %collective-permute-start.17) | collective-permute-done | bytes 131104 | tf_op jit(solution)/shard_map/ppermute | solution.py:46
  43.4 0.1 convert_add_fusion.1
  43.4 1.2 %collective-permute-start.18 = (bf16[32,1024]{1,0:T(8,128)(2,1)S(1)}, bf16[32,1024]{1,0:T(8,128)(2,1)S(1)}, u32[]{:S(2)}, u32[]{:S(2)}) collective-permute-start(bf16[32,1024]{1,0:T(8,128)(2,1)S(1)} %slice.137), channel_id=1, source_target_pairs={{0,8},{1,9},{2,10},{3,11},{4,12},{5,13},{6,14},{7,15},{8,0},{9,1},... | collective-permute-start | bytes 196616 | tf_op jit(solution)/shard_map/ppermute | solution.py:55
  44.7 0.0 collective-permute-done.5.other_ref
  44.7 2.3 %shard_map.62 = (bf16[512,512]{1,0:T(8,128)(2,1)S(1)}, bf16[256,512]{1,0:T(8,128)(2,1)S(1)}) custom-call(s32[1]{0:T(128)} %bitcast.device_ref, bf16[1024,2304]{1,0:T(8,128)(2,1)S(1)} %get-tuple-element.16.windows_ref, bf16[128,2304]{1,0:T(8,128)(2,1)S(1)} %pad_maximum_fusion.own_ref, bf16[128,2304]{1,0:T(8,128)(2,1)S(1)} %collective-permute-done.5.other_ref), custom_call_target="tpu_custom_call" | custom-call | flops 1207959552 | bytes 6684672 | tf_op jit(solution)/shard_map/pallas_call | solution.py:256
  47.0 0.0 collective-permute-done.13
  47.0 0.1 convert_add_fusion
  47.1 0.3 collective-permute-start.14
  47.5 0.0 collective-permute-done.18
  47.5 7.9 %collective-permute-start.19 = (bf16[32,1024]{1,0:T(8,128)(2,1)S(1)}, bf16[32,1024]{1,0:T(8,128)(2,1)S(1)}, u32[]{:S(2)}, u32[]{:S(2)}) collective-permute-start(bf16[32,1024]{1,0:T(8,128)(2,1)S(1)} %get-tuple-element.24), channel_id=1, source_target_pairs={{0,31},{1,30},{2,29},{3,28},{4,27},{5,26},{6,25},{7,24},{8,23},{9,... | collective-permute-start | bytes 196616 | tf_op jit(solution)/shard_map/ppermute | solution.py:55
  55.4 2.7 %collective-permute-start.15 = (bf16[32,1280]{1,0:T(8,128)(2,1)S(1)}, bf16[32,1280]{1,0:T(8,128)(2,1)S(1)}, u32[]{:S(2)}, u32[]{:S(2)}) collective-permute-start(bf16[32,1280]{1,0:T(8,128)(2,1)S(1)} %get-tuple-element.26), channel_id=1, source_target_pairs={{0,31},{1,30},{2,29},{3,28},{4,27},{5,26},{6,25},{7,24},{8,23},{9,... | collective-permute-start | bytes 245768 | tf_op jit(solution)/shard_map/ppermute | solution.py:55
  58.1 2.9 %shard_map.63 = bf16[512,512]{1,0:T(8,128)(2,1)} custom-call(bf16[1024,2304]{1,0:T(8,128)(2,1)S(1)} %get-tuple-element.16.windows_ref, bf16[512,512]{1,0:T(8,128)(2,1)S(1)} %get-tuple-element.17.early_ref, bf16[256,512]{1,0:T(8,128)(2,1)S(1)} %get-tuple-element.18.chosen_ref, bf16[64,2304]{1,0:T(8,128)(2,1)S(1)} %collective-permute-done.6.refs_0_, ...), custom_call_target="tpu_custom_call" | custom-call | flops 1207959552 | bytes 7208960 | tf_op jit(solution)/shard_map/pallas_call | solution.py:256
  61.1 0.0 collective-permute-done.19.refs_3_
  61.1 2.0 %collective-permute-done.15.refs_1_ = bf16[32,1280]{1,0:T(8,128)(2,1)S(1)} collective-permute-done((bf16[32,1280]{1,0:T(8,128)(2,1)S(1)}, bf16[32,1280]{1,0:T(8,128)(2,1)S(1)}, u32[]{:S(2)}, u32[]{:S(2)}) %collective-permute-start.15) | collective-permute-done | bytes 81952 | tf_op jit(solution)/shard_map/ppermute | solution.py:55
  63.0 1.2 %shard_map.65 = f32[9,16,512]{2,1,0:T(8,128)} custom-call(f32[32,1280]{1,0:T(8,128)S(1)} %get-tuple-element.27.refs_0_, bf16[32,1280]{1,0:T(8,128)(2,1)S(1)} %collective-permute-done.15.refs_1_, f32[32,1024]{1,0:T(8,128)S(1)} %get-tuple-element.25.refs_2_, bf16[32,1024]{1,0:T(8,128)(2,1)S(1)} %collective-permute-done.19.refs_3_), custom_call_target="tpu_custom_call" | custom-call | flops 37748736 | bytes 737280 | tf_op jit(solution)/shard_map/pallas_call | solution.py:256
  (17 shorter events, 0.3 us)
Async XLA Ops:
  0.6 13.0 %copy-start = (bf16[16,9,512]{2,0,1:T(8,128)(2,1)S(1)}, bf16[16,9,512]{2,0,1:T(8,128)(2,1)}, u32[]{:S(2)}) copy-start(bf16[16,9,512]{2,0,1:T(8,128)(2,1)} %param.7) | copy-start | bytes 442372
  1.5 10.5 %collective-permute-start = (bf16[2,4,512]{2,1,0:T(4,128)(2,1)S(1)}, bf16[2,4,512]{2,1,0:T(4,128)(2,1)S(1)}, u32[]{:S(2)}, u32[]{:S(2)}) collective-permute-start(bf16[2,4,512]{2,1,0:T(4,128)(2,1)S(1)} %fusion.16), channel_id=1, source_target_pairs={{0,1},{1,0},{2,3},{3,2},{4,5},{5,4},{6,7},{7,6},{8,9},{9,8},{10,11... | collective-permute-start | bytes 24584 | tf_op jit(solution)/shard_map/ppermute | solution.py:279
  3.6 10.0 %collective-permute-start.1 = (bf16[9,16,512]{2,1,0:T(8,128)(2,1)}, bf16[9,16,512]{2,1,0:T(8,128)(2,1)S(1)}, u32[]{:S(2)}, u32[]{:S(2)}) collective-permute-start(bf16[9,16,512]{2,1,0:T(8,128)(2,1)} %bitcast.5), channel_id=1, source_target_pairs={{0,31},{1,30},{2,29},{3,28},{4,27},{5,26},{6,25},{7,24},{8,23},{9,... | collective-permute-start | bytes 442376 | tf_op jit(solution)/shard_map/ppermute | solution.py:55
  14.2 7.5 %collective-permute-start.2 = (bf16[32,2304]{1,0:T(8,128)(2,1)S(1)}, bf16[32,2304]{1,0:T(8,128)(2,1)S(1)}, u32[]{:S(2)}, u32[]{:S(2)}) collective-permute-start(bf16[32,2304]{1,0:T(8,128)(2,1)S(1)} %shard_map.61), channel_id=1, source_target_pairs={{0,1},{1,0},{2,6},{3,7},{4,5},{5,4},{6,2},{7,3},{8,9},{9,8},{10,14... | collective-permute-start | bytes 442376 | tf_op jit(solution)/shard_map/ppermute | solution.py:46
  17.0 12.4 %collective-permute-start.11 = (bf16[128,2304]{1,0:T(8,128)(2,1)S(1)}, bf16[128,2304]{1,0:T(8,128)(2,1)S(1)}, u32[]{:S(2)}, u32[]{:S(2)}) collective-permute-start(bf16[128,2304]{1,0:T(8,128)(2,1)S(1)} %get-tuple-element.23), channel_id=1, source_target_pairs={{0,2},{1,3},{2,0},{3,1},{4,6},{5,7},{6,4},{7,5},{8,10},{9,11},{10,... | collective-permute-start | bytes 1769480 | tf_op jit(solution)/shard_map/ppermute | solution.py:46
  18.5 14.7 %collective-permute-start.10 = (bf16[128,2304]{1,0:T(8,128)(2,1)S(1)}, bf16[128,2304]{1,0:T(8,128)(2,1)S(1)}, u32[]{:S(2)}, u32[]{:S(2)}) collective-permute-start(bf16[128,2304]{1,0:T(8,128)(2,1)S(1)} %get-tuple-element.21), channel_id=1, source_target_pairs={{0,2},{1,3},{2,0},{3,1},{4,6},{5,7},{6,4},{7,5},{8,10},{9,11},{10,... | collective-permute-start | bytes 1769480 | tf_op jit(solution)/shard_map/ppermute | solution.py:46
  19.0 6.8 %collective-permute-start.3 = (bf16[32,2304]{1,0:T(8,128)(2,1)S(1)}, bf16[32,2304]{1,0:T(8,128)(2,1)S(1)}, u32[]{:S(2)}, u32[]{:S(2)}) collective-permute-start(bf16[32,2304]{1,0:T(8,128)(2,1)S(1)} %shard_map.61), channel_id=1, source_target_pairs={{0,8},{1,9},{2,10},{3,11},{4,12},{5,13},{6,14},{7,15},{8,0},{9,1},... | collective-permute-start | bytes 442376 | tf_op jit(solution)/shard_map/ppermute | solution.py:55
  21.7 7.3 %collective-permute-start.4 = (bf16[32,2304]{1,0:T(8,128)(2,1)S(1)}, bf16[32,2304]{1,0:T(8,128)(2,1)S(1)}, u32[]{:S(2)}, u32[]{:S(2)}) collective-permute-start(bf16[32,2304]{1,0:T(8,128)(2,1)S(1)} %collective-permute-done.2), channel_id=1, source_target_pairs={{0,8},{1,9},{2,10},{3,11},{4,12},{5,13},{6,14},{7,15},{8,0},{9,1},... | collective-permute-start | bytes 442376 | tf_op jit(solution)/shard_map/ppermute | solution.py:55
  21.7 9.5 %collective-permute-start.6 = (bf16[64,2304]{1,0:T(8,128)(2,1)S(1)}, bf16[64,2304]{1,0:T(8,128)(2,1)S(1)}, u32[]{:S(2)}, u32[]{:S(2)}) collective-permute-start(bf16[64,2304]{1,0:T(8,128)(2,1)S(1)} %pad_maximum_fusion.1), channel_id=1, source_target_pairs={{0,4},{1,5},{2,3},{3,2},{4,0},{5,1},{6,7},{7,6},{8,12},{9,13},{10,... | collective-permute-start | bytes 884744 | tf_op jit(solution)/shard_map/ppermute | solution.py:46
  29.0 5.9 %collective-permute-start.7 = (bf16[64,2304]{1,0:T(8,128)(2,1)S(1)}, bf16[64,2304]{1,0:T(8,128)(2,1)S(1)}, u32[]{:S(2)}, u32[]{:S(2)}) collective-permute-start(bf16[64,2304]{1,0:T(8,128)(2,1)S(1)} %pad_maximum_fusion.2), channel_id=1, source_target_pairs={{0,4},{1,5},{2,3},{3,2},{4,0},{5,1},{6,7},{7,6},{8,12},{9,13},{10,... | collective-permute-start | bytes 884744 | tf_op jit(solution)/shard_map/ppermute | solution.py:46
  29.5 8.2 %collective-permute-start.16 = (bf16[128,1024]{1,0:T(8,128)(2,1)S(1)}, bf16[128,1024]{1,0:T(8,128)(2,1)S(1)}, u32[]{:S(2)}, u32[]{:S(2)}) collective-permute-start(bf16[128,1024]{1,0:T(8,128)(2,1)S(1)} %add_convert_fusion.1), channel_id=1, source_target_pairs={{0,4},{1,5},{2,3},{3,2},{4,0},{5,1},{6,7},{7,6},{8,12},{9,13},{10,... | collective-permute-start | bytes 786440 | tf_op jit(solution)/shard_map/ppermute | solution.py:46
  30.7 10.5 %collective-permute-start.12 = (bf16[128,1280]{1,0:T(8,128)(2,1)S(1)}, bf16[128,1280]{1,0:T(8,128)(2,1)S(1)}, u32[]{:S(2)}, u32[]{:S(2)}) collective-permute-start(bf16[128,1280]{1,0:T(8,128)(2,1)S(1)} %add_convert_fusion), channel_id=1, source_target_pairs={{0,4},{1,5},{2,3},{3,2},{4,0},{5,1},{6,7},{7,6},{8,12},{9,13},{10,... | collective-permute-start | bytes 983048 | tf_op jit(solution)/shard_map/ppermute | solution.py:46
  31.2 13.5 %collective-permute-start.5 = (bf16[128,2304]{1,0:T(8,128)(2,1)S(1)}, bf16[128,2304]{1,0:T(8,128)(2,1)S(1)}, u32[]{:S(2)}, u32[]{:S(2)}) collective-permute-start(bf16[128,2304]{1,0:T(8,128)(2,1)S(1)} %pad_maximum_fusion.own_ref), channel_id=1, source_target_pairs={{0,2},{1,3},{2,0},{3,1},{4,6},{5,7},{6,4},{7,5},{8,10},{9,11},{10,... | collective-permute-start | bytes 1769480 | tf_op jit(solution)/shard_map/ppermute | solution.py:46
  33.1 25.0 %collective-permute-start.8 = (bf16[64,2304]{1,0:T(8,128)(2,1)S(1)}, bf16[64,2304]{1,0:T(8,128)(2,1)S(1)}, u32[]{:S(2)}, u32[]{:S(2)}) collective-permute-start(bf16[64,2304]{1,0:T(8,128)(2,1)S(1)} %collective-permute-done.6.refs_0_), channel_id=1, source_target_pairs={{0,2},{1,3},{2,0},{3,1},{4,6},{5,7},{6,4},{7,5},{8,10},{9,11},{10,... | collective-permute-start | bytes 884744 | tf_op jit(solution)/shard_map/ppermute | solution.py:46
  34.9 23.2 %collective-permute-start.9 = (bf16[64,2304]{1,0:T(8,128)(2,1)S(1)}, bf16[64,2304]{1,0:T(8,128)(2,1)S(1)}, u32[]{:S(2)}, u32[]{:S(2)}) collective-permute-start(bf16[64,2304]{1,0:T(8,128)(2,1)S(1)} %collective-permute-done.7.refs_1_), channel_id=1, source_target_pairs={{0,2},{1,3},{2,0},{3,1},{4,6},{5,7},{6,4},{7,5},{8,10},{9,11},{10,... | collective-permute-start | bytes 884744 | tf_op jit(solution)/shard_map/ppermute | solution.py:46
  37.8 5.6 %collective-permute-start.17 = (bf16[64,1024]{1,0:T(8,128)(2,1)S(1)}, bf16[64,1024]{1,0:T(8,128)(2,1)S(1)}, u32[]{:S(2)}, u32[]{:S(2)}) collective-permute-start(bf16[64,1024]{1,0:T(8,128)(2,1)S(1)} %add_convert_fusion.3), channel_id=1, source_target_pairs={{0,1},{1,0},{2,6},{3,7},{4,5},{5,4},{6,2},{7,3},{8,9},{9,8},{10,14... | collective-permute-start | bytes 393224 | tf_op jit(solution)/shard_map/ppermute | solution.py:46
  41.3 5.7 %collective-permute-start.13 = (bf16[64,1280]{1,0:T(8,128)(2,1)S(1)}, bf16[64,1280]{1,0:T(8,128)(2,1)S(1)}, u32[]{:S(2)}, u32[]{:S(2)}) collective-permute-start(bf16[64,1280]{1,0:T(8,128)(2,1)S(1)} %add_convert_fusion.2), channel_id=1, source_target_pairs={{0,1},{1,0},{2,6},{3,7},{4,5},{5,4},{6,2},{7,3},{8,9},{9,8},{10,14... | collective-permute-start | bytes 491528 | tf_op jit(solution)/shard_map/ppermute | solution.py:46
  43.4 4.0 %collective-permute-start.18 = (bf16[32,1024]{1,0:T(8,128)(2,1)S(1)}, bf16[32,1024]{1,0:T(8,128)(2,1)S(1)}, u32[]{:S(2)}, u32[]{:S(2)}) collective-permute-start(bf16[32,1024]{1,0:T(8,128)(2,1)S(1)} %slice.137), channel_id=1, source_target_pairs={{0,8},{1,9},{2,10},{3,11},{4,12},{5,13},{6,14},{7,15},{8,0},{9,1},... | collective-permute-start | bytes 196616 | tf_op jit(solution)/shard_map/ppermute | solution.py:55
  47.1 8.3 %collective-permute-start.14 = (bf16[32,1280]{1,0:T(8,128)(2,1)S(1)}, bf16[32,1280]{1,0:T(8,128)(2,1)S(1)}, u32[]{:S(2)}, u32[]{:S(2)}) collective-permute-start(bf16[32,1280]{1,0:T(8,128)(2,1)S(1)} %slice.136), channel_id=1, source_target_pairs={{0,8},{1,9},{2,10},{3,11},{4,12},{5,13},{6,14},{7,15},{8,0},{9,1},... | collective-permute-start | bytes 245768 | tf_op jit(solution)/shard_map/ppermute | solution.py:55
  47.5 13.6 %collective-permute-start.19 = (bf16[32,1024]{1,0:T(8,128)(2,1)S(1)}, bf16[32,1024]{1,0:T(8,128)(2,1)S(1)}, u32[]{:S(2)}, u32[]{:S(2)}) collective-permute-start(bf16[32,1024]{1,0:T(8,128)(2,1)S(1)} %get-tuple-element.24), channel_id=1, source_target_pairs={{0,31},{1,30},{2,29},{3,28},{4,27},{5,26},{6,25},{7,24},{8,23},{9,... | collective-permute-start | bytes 196616 | tf_op jit(solution)/shard_map/ppermute | solution.py:55
  55.4 7.6 %collective-permute-start.15 = (bf16[32,1280]{1,0:T(8,128)(2,1)S(1)}, bf16[32,1280]{1,0:T(8,128)(2,1)S(1)}, u32[]{:S(2)}, u32[]{:S(2)}) collective-permute-start(bf16[32,1280]{1,0:T(8,128)(2,1)S(1)} %get-tuple-element.26), channel_id=1, source_target_pairs={{0,31},{1,30},{2,29},{3,28},{4,27},{5,26},{6,25},{7,24},{8,23},{9,... | collective-permute-start | bytes 245768 | tf_op jit(solution)/shard_map/ppermute | solution.py:55

commit v9 on v8

--- a/solution.py
+++ b/solution.py
@@ -230,13 +230,12 @@
             ).astype(BF16)
 
 
-def finish_kernel(*refs):
+def finish_kernel(got_ref, *refs):
     out_ref = refs[-1]
     taps, rows, width = out_ref.shape
     half = width // 2
     cuts = [slice(k * half, (k + 1) * half) for k in range(taps)]
-    own = jnp.concatenate([ref[...] for ref in refs[:-1:2]], axis=1)
-    got = jnp.concatenate([ref[...] for ref in refs[1:-1:2]], axis=1).astype(F32)
+    own, got = jnp.concatenate([ref[...] for ref in refs[:-1]], axis=1), got_ref[...].astype(F32)
     far, near = own[rows:] + got[:rows], own[:rows] + got[rows:]
     high = far.astype(BF16)
     low = (far - high.astype(F32)).astype(BF16)
@@ -324,13 +323,13 @@
     )
     received = plan.swap(sent, "core")
     second_sent, second_kept = call(sums_kernel, sums, (second_order, windows), flops=work, given=(0, 1))
-    cut = (taps + 1) // 2 * half
+    cut = 4 * taps // 5 * half
     chunks = (slice(0, cut), slice(cut, depth))
     for place, chunk in enumerate(chunks):
         arrived = plan.swap((kept[:, chunk] + received[:, chunk].astype(F32)).astype(BF16), "a")
         late_sums = [arrived] if place == 0 else late_sums + [arrived]
     second_got = plan.swap(second_sent, "core")
-    pairs = []
+    done = []
     for place, chunk in enumerate(chunks):
         arrived = late_sums[place]
         middle = second_kept.shape[0] // 2
@@ -351,11 +350,12 @@
                 for j in range(1, len(masks))
             ]
             sums = functools.reduce(jnp.add, pieces, sums[:size])
-        pairs += [sums, plan.complement(sums.astype(BF16))]
+        done.append(sums)
+    got = plan.complement(jnp.concatenate([sums.astype(BF16) for sums in done], axis=1))
     grad_weight = jnp.transpose(
         call(
-            finish_kernel, [((taps, rows, width), F32, False)], pairs,
-            flops=4 * rows * depth * half, given=range(4),
+            finish_kernel, [((taps, rows, width), F32, False)], (got, *done),
+            flops=4 * rows * depth * half, given=range(3),
         ),
         (1, 0, 2),
     )

time: 64.5 us -> 65.7 us (1.019)
  the two profiles are of different devices: /device:TPU:1 before, /device:TPU:11 now
where the time goes in v9:
time: 65.7 us; the launch traced here: 65.4 us
  waiting for transfers between devices  27.2 us (41%)
  starting transfers between devices  22.7 us (35%)
  Pallas kernels  13.3 us (20%)
  other arithmetic  1.33 us (2%)
  between operations  0.85 us (1%)
    ppermute x6, waiting for transfers between devices, shift(): return lax.ppermute(block, AXES, [(d, d ^ mask) for d in range(self.count)])  16 us
    pallas_call x7, Pallas kernels, call(): pl.pallas_call(kernel, out_shape=[(ON_CHIP if stays else jax.ShapeDtypeSt...  13.3 us
    ppermute x12, starting transfers between devices, swap(): return lax.ppermute(block, AXES, route)  12.1 us
    ppermute x12, waiting for transfers between devices, swap(): return lax.ppermute(block, AXES, route)  11.2 us
    ppermute x6, starting transfers between devices, shift(): return lax.ppermute(block, AXES, [(d, d ^ mask) for d in range(self.count)])  10.3 us
  transfers between devices with their start and end apart: 19, of which 7 were waited for; matrix products, arithmetic and copies ran while one was open for 1% of the time, Pallas kernels for 18%

profile of v9, /device:TPU:11, one launch (start us, length us, event | category | flops | bytes accessed | tf_op | source)
XLA Modules:
  0.0 65.4 jit_solution(15636129158777121868)
XLA Ops:
  0.6 0.0 copy-start
  0.6 0.8 %fusion.16 = bf16[2,4,512]{2,1,0:T(4,128)(2,1)S(1)} fusion(bf16[2,256,512]{2,1,0:T(8,128)(2,1)} %pre_hbm.1, bf16[2,256,512]{2,1,0:T(8,128)(2,1)} %out_grad_hbm.1, pred[]{:T(512)S(6)} %eq.2), kind=kLoop, calls=%fused_computation.39 | loop fusion | flops 102400 | bytes 40961 | tf_op jit(solution)/shard_map/jit(_where)/select_n | solution.py:278
  1.5 0.3 collective-permute-start
  1.8 4.0 %collective-permute-start.1 = (bf16[9,16,512]{2,1,0:T(8,128)(2,1)}, bf16[9,16,512]{2,1,0:T(8,128)(2,1)S(1)}, u32[]{:S(2)}, u32[]{:S(2)}) collective-permute-start(bf16[9,16,512]{2,1,0:T(8,128)(2,1)} %bitcast.5), channel_id=1, source_target_pairs={{0,31},{1,30},{2,29},{3,28},{4,27},{5,26},{6,25},{7,24},{8,23},{9,... | collective-permute-start | bytes 442376 | tf_op jit(solution)/shard_map/ppermute | solution.py:55
  5.8 3.3 %shard_map.59 = (bf16[256,1024]{1,0:T(8,128)(2,1)S(1)}, bf16[256,1024]{1,0:T(8,128)(2,1)S(1)}, f32[4,272,256]{2,1,0:T(8,128)S(1)}, bf16[1024,2304]{1,0:T(8,128)(2,1)S(1)}) custom-call(s32[1]{0:T(128)} %bitcast.device_ref, bf16[512,512]{1,0:T(8,128)(2,1)} %bitcast.9, bf16[2,256,512]{2,1,0:T(8,128)(2,1)} %pre_hbm.1, bf16[2,256,512]{2,1,0:T(8,128)(2,1)} %out_grad_hbm.1), custom_call_target="tpu_custom_call" | custom-call | flops 536870912 | bytes 8454144 | tf_op jit(solution)/shard_map/pallas_call | solution.py:255
  9.2 0.0 collective-permute-done
  9.2 4.2 %collective-permute-done.1.far_ref = bf16[9,16,512]{2,1,0:T(8,128)(2,1)S(1)} collective-permute-done((bf16[9,16,512]{2,1,0:T(8,128)(2,1)}, bf16[9,16,512]{2,1,0:T(8,128)(2,1)S(1)}, u32[]{:S(2)}, u32[]{:S(2)}) %collective-permute-start.1) | collective-permute-done | bytes 147488 | tf_op jit(solution)/shard_map/ppermute | solution.py:55
  13.5 0.5 shard_map.61
  14.0 1.0 %collective-permute-start.2 = (bf16[32,2304]{1,0:T(8,128)(2,1)S(1)}, bf16[32,2304]{1,0:T(8,128)(2,1)S(1)}, u32[]{:S(2)}, u32[]{:S(2)}) collective-permute-start(bf16[32,2304]{1,0:T(8,128)(2,1)S(1)} %shard_map.61), channel_id=1, source_target_pairs={{0,1},{1,0},{2,6},{3,7},{4,5},{5,4},{6,2},{7,3},{8,9},{9,8},{10,14... | collective-permute-start | bytes 442376 | tf_op jit(solution)/shard_map/ppermute | solution.py:46
  15.0 1.5 %shard_map.60 = (bf16[128,2304]{1,0:T(8,128)(2,1)S(1)}, f32[128,2304]{1,0:T(8,128)S(1)}, f32[4,272,256]{2,1,0:T(8,128)S(1)}, bf16[1024,2304]{1,0:T(8,128)(2,1)S(1)}) custom-call(bf16[256,1024]{1,0:T(8,128)(2,1)S(1)} %get-tuple-element.13.order_ref, bf16[2,8,512]{2,1,0:T(8,128)(2,1)S(1)} %pad_maximum_fusion.4.halo_ref, ...), custom_call_target="tpu_custom_call", output_to_operand_aliasing={{2}: (2, {}), {3}: (3, {})} | custom-call | flops 1207959552 | bytes 13975552 | tf_op jit(solution)/shard_map/pallas_call | solution.py:255
  16.5 1.0 %collective-permute-start.11 = (bf16[128,2304]{1,0:T(8,128)(2,1)S(1)}, bf16[128,2304]{1,0:T(8,128)(2,1)S(1)}, u32[]{:S(2)}, u32[]{:S(2)}) collective-permute-start(bf16[128,2304]{1,0:T(8,128)(2,1)S(1)} %get-tuple-element.23), channel_id=1, source_target_pairs={{0,2},{1,3},{2,0},{3,1},{4,6},{5,7},{6,4},{7,5},{8,10},{9,11},{10,... | collective-permute-start | bytes 1769480 | tf_op jit(solution)/shard_map/ppermute | solution.py:46
  17.5 1.4 %shard_map.64 = (bf16[128,2304]{1,0:T(8,128)(2,1)S(1)}, f32[128,2304]{1,0:T(8,128)S(1)}) custom-call(bf16[256,1024]{1,0:T(8,128)(2,1)S(1)} %get-tuple-element.19.order_ref, bf16[1024,2304]{1,0:T(8,128)(2,1)S(1)} %get-tuple-element.16.windows_ref), custom_call_target="tpu_custom_call" | custom-call | flops 1207959552 | bytes 7012352 | tf_op jit(solution)/shard_map/pallas_call | solution.py:255
  18.9 0.1 collective-permute-start.10
  19.0 0.1 collective-permute-start.3
  19.1 0.0 collective-permute-done.2
  19.1 1.4 %collective-permute-start.4 = (bf16[32,2304]{1,0:T(8,128)(2,1)S(1)}, bf16[32,2304]{1,0:T(8,128)(2,1)S(1)}, u32[]{:S(2)}, u32[]{:S(2)}) collective-permute-start(bf16[32,2304]{1,0:T(8,128)(2,1)S(1)} %collective-permute-done.2), channel_id=1, source_target_pairs={{0,8},{1,9},{2,10},{3,11},{4,12},{5,13},{6,14},{7,15},{8,0},{9,1},... | collective-permute-start | bytes 442376 | tf_op jit(solution)/shard_map/ppermute | solution.py:55
  20.6 0.8 %collective-permute-start.6 = (bf16[64,2304]{1,0:T(8,128)(2,1)S(1)}, bf16[64,2304]{1,0:T(8,128)(2,1)S(1)}, u32[]{:S(2)}, u32[]{:S(2)}) collective-permute-start(bf16[64,2304]{1,0:T(8,128)(2,1)S(1)} %pad_maximum_fusion.1), channel_id=1, source_target_pairs={{0,4},{1,5},{2,3},{3,2},{4,0},{5,1},{6,7},{7,6},{8,12},{9,13},{10,... | collective-permute-start | bytes 884744 | tf_op jit(solution)/shard_map/ppermute | solution.py:46
  21.4 2.7 %collective-permute-done.3 = bf16[32,2304]{1,0:T(8,128)(2,1)S(1)} collective-permute-done((bf16[32,2304]{1,0:T(8,128)(2,1)S(1)}, bf16[32,2304]{1,0:T(8,128)(2,1)S(1)}, u32[]{:S(2)}, u32[]{:S(2)}) %collective-permute-start.3) | collective-permute-done | bytes 147488 | tf_op jit(solution)/shard_map/ppermute | solution.py:55
  24.0 3.2 %collective-permute-done.4 = bf16[32,2304]{1,0:T(8,128)(2,1)S(1)} collective-permute-done((bf16[32,2304]{1,0:T(8,128)(2,1)S(1)}, bf16[32,2304]{1,0:T(8,128)(2,1)S(1)}, u32[]{:S(2)}, u32[]{:S(2)}) %collective-permute-start.4) | collective-permute-done | bytes 147488 | tf_op jit(solution)/shard_map/ppermute | solution.py:55
  27.2 1.1 %collective-permute-start.7 = (bf16[64,2304]{1,0:T(8,128)(2,1)S(1)}, bf16[64,2304]{1,0:T(8,128)(2,1)S(1)}, u32[]{:S(2)}, u32[]{:S(2)}) collective-permute-start(bf16[64,2304]{1,0:T(8,128)(2,1)S(1)} %pad_maximum_fusion.2), channel_id=1, source_target_pairs={{0,4},{1,5},{2,3},{3,2},{4,0},{5,1},{6,7},{7,6},{8,12},{9,13},{10,... | collective-permute-start | bytes 884744 | tf_op jit(solution)/shard_map/ppermute | solution.py:46
  28.4 0.0 collective-permute-done.11
  28.4 0.1 add_convert_fusion
  28.5 0.4 collective-permute-start.12
  28.9 1.1 %collective-permute-start.15 = (bf16[128,512]{1,0:T(8,128)(2,1)S(1)}, bf16[128,512]{1,0:T(8,128)(2,1)S(1)}, u32[]{:S(2)}, u32[]{:S(2)}) collective-permute-start(bf16[128,512]{1,0:T(8,128)(2,1)S(1)} %add_convert_fusion.2), channel_id=1, source_target_pairs={{0,4},{1,5},{2,3},{3,2},{4,0},{5,1},{6,7},{7,6},{8,12},{9,13},{10,... | collective-permute-start | bytes 393224 | tf_op jit(solution)/shard_map/ppermute | solution.py:46
  30.1 0.0 collective-permute-done.6.refs_0_
  30.1 2.4 %collective-permute-start.5 = (bf16[128,2304]{1,0:T(8,128)(2,1)S(1)}, bf16[128,2304]{1,0:T(8,128)(2,1)S(1)}, u32[]{:S(2)}, u32[]{:S(2)}) collective-permute-start(bf16[128,2304]{1,0:T(8,128)(2,1)S(1)} %pad_maximum_fusion.own_ref), channel_id=1, source_target_pairs={{0,2},{1,3},{2,0},{3,1},{4,6},{5,7},{6,4},{7,5},{8,10},{9,11},{10,... | collective-permute-start | bytes 1769480 | tf_op jit(solution)/shard_map/ppermute | solution.py:46
  32.5 0.0 collective-permute-done.10
  32.5 0.1 collective-permute-start.8
  32.6 6.9 %collective-permute-done.15 = bf16[128,512]{1,0:T(8,128)(2,1)S(1)} collective-permute-done((bf16[128,512]{1,0:T(8,128)(2,1)S(1)}, bf16[128,512]{1,0:T(8,128)(2,1)S(1)}, u32[]{:S(2)}, u32[]{:S(2)}) %collective-permute-start.15) | collective-permute-done | bytes 131104 | tf_op jit(solution)/shard_map/ppermute | solution.py:46
  39.5 1.3 %collective-permute-start.16 = (bf16[64,512]{1,0:T(8,128)(2,1)S(1)}, bf16[64,512]{1,0:T(8,128)(2,1)S(1)}, u32[]{:S(2)}, u32[]{:S(2)}) collective-permute-start(bf16[64,512]{1,0:T(8,128)(2,1)S(1)} %add_convert_fusion.3), channel_id=1, source_target_pairs={{0,1},{1,0},{2,6},{3,7},{4,5},{5,4},{6,2},{7,3},{8,9},{9,8},{10,14... | collective-permute-start | bytes 196616 | tf_op jit(solution)/shard_map/ppermute | solution.py:46
  40.8 0.0 collective-permute-done.7.refs_1_
  40.8 1.9 %collective-permute-start.9 = (bf16[64,2304]{1,0:T(8,128)(2,1)S(1)}, bf16[64,2304]{1,0:T(8,128)(2,1)S(1)}, u32[]{:S(2)}, u32[]{:S(2)}) collective-permute-start(bf16[64,2304]{1,0:T(8,128)(2,1)S(1)} %collective-permute-done.7.refs_1_), channel_id=1, source_target_pairs={{0,2},{1,3},{2,0},{3,1},{4,6},{5,7},{6,4},{7,5},{8,10},{9,11},{10,... | collective-permute-start | bytes 884744 | tf_op jit(solution)/shard_map/ppermute | solution.py:46
  42.7 0.0 collective-permute-done.12
  42.7 0.1 add_convert_fusion.1
  42.8 0.8 %collective-permute-start.13 = (bf16[64,1792]{1,0:T(8,128)(2,1)S(1)}, bf16[64,1792]{1,0:T(8,128)(2,1)S(1)}, u32[]{:S(2)}, u32[]{:S(2)}) collective-permute-start(bf16[64,1792]{1,0:T(8,128)(2,1)S(1)} %add_convert_fusion.1), channel_id=1, source_target_pairs={{0,1},{1,0},{2,6},{3,7},{4,5},{5,4},{6,2},{7,3},{8,9},{9,8},{10,14... | collective-permute-start | bytes 688136 | tf_op jit(solution)/shard_map/ppermute | solution.py:46
  43.6 0.0 collective-permute-done.16
  43.7 0.1 collective-permute-start.17
  43.8 4.3 %collective-permute-done.13 = bf16[64,1792]{1,0:T(8,128)(2,1)S(1)} collective-permute-done((bf16[64,1792]{1,0:T(8,128)(2,1)S(1)}, bf16[64,1792]{1,0:T(8,128)(2,1)S(1)}, u32[]{:S(2)}, u32[]{:S(2)}) %collective-permute-start.13) | collective-permute-done | bytes 229408 | tf_op jit(solution)/shard_map/ppermute | solution.py:46
  48.0 0.1 convert_add_fusion
  48.2 0.1 collective-permute-start.14
  48.2 0.0 collective-permute-done.17
  48.3 3.6 %collective-permute-done.14 = bf16[32,1792]{1,0:T(8,128)(2,1)S(1)} collective-permute-done((bf16[32,1792]{1,0:T(8,128)(2,1)S(1)}, bf16[32,1792]{1,0:T(8,128)(2,1)S(1)}, u32[]{:S(2)}, u32[]{:S(2)}) %collective-permute-start.14) | collective-permute-done | bytes 114720 | tf_op jit(solution)/shard_map/ppermute | solution.py:55
  51.9 4.7 %collective-permute-start.18 = (bf16[32,2304]{1,0:T(8,128)(2,1)S(1)}, bf16[32,2304]{1,0:T(8,128)(2,1)S(1)}, u32[]{:S(2)}, u32[]{:S(2)}) collective-permute-start(bf16[32,2304]{1,0:T(8,128)(2,1)S(1)} %pad_maximum_fusion.3), channel_id=1, source_target_pairs={{0,31},{1,30},{2,29},{3,28},{4,27},{5,26},{6,25},{7,24},{8,23},{9,... | collective-permute-start | bytes 442376 | tf_op jit(solution)/shard_map/ppermute | solution.py:55
  56.6 0.0 collective-permute-done.5.other_ref
  56.6 2.3 %shard_map.62 = (bf16[512,512]{1,0:T(8,128)(2,1)S(1)}, bf16[256,512]{1,0:T(8,128)(2,1)S(1)}) custom-call(s32[1]{0:T(128)} %bitcast.device_ref, bf16[1024,2304]{1,0:T(8,128)(2,1)S(1)} %get-tuple-element.16.windows_ref, bf16[128,2304]{1,0:T(8,128)(2,1)S(1)} %pad_maximum_fusion.own_ref, bf16[128,2304]{1,0:T(8,128)(2,1)S(1)} %collective-permute-done.5.other_ref), custom_call_target="tpu_custom_call" | custom-call | flops 1207959552 | bytes 6684672 | tf_op jit(solution)/shard_map/pallas_call | solution.py:255
  58.9 2.9 %shard_map.63 = bf16[512,512]{1,0:T(8,128)(2,1)} custom-call(bf16[1024,2304]{1,0:T(8,128)(2,1)S(1)} %get-tuple-element.16.windows_ref, bf16[512,512]{1,0:T(8,128)(2,1)S(1)} %get-tuple-element.17.early_ref, bf16[256,512]{1,0:T(8,128)(2,1)S(1)} %get-tuple-element.18.chosen_ref, bf16[64,2304]{1,0:T(8,128)(2,1)S(1)} %collective-permute-done.6.refs_0_, ...), custom_call_target="tpu_custom_call" | custom-call | flops 1207959552 | bytes 7208960 | tf_op jit(solution)/shard_map/pallas_call | solution.py:255
  61.9 2.3 %collective-permute-done.18.got_ref = bf16[32,2304]{1,0:T(8,128)(2,1)S(1)} collective-permute-done((bf16[32,2304]{1,0:T(8,128)(2,1)S(1)}, bf16[32,2304]{1,0:T(8,128)(2,1)S(1)}, u32[]{:S(2)}, u32[]{:S(2)}) %collective-permute-start.18) | collective-permute-done | bytes 147488 | tf_op jit(solution)/shard_map/ppermute | solution.py:55
  64.2 1.3 %shard_map.65 = f32[9,16,512]{2,1,0:T(8,128)} custom-call(bf16[32,2304]{1,0:T(8,128)(2,1)S(1)} %collective-permute-done.18.got_ref, f32[32,1792]{1,0:T(8,128)S(1)} %get-tuple-element.25.refs_0_, f32[32,512]{1,0:T(8,128)S(1)} %get-tuple-element.27.refs_1_), custom_call_target="tpu_custom_call" | custom-call | flops 37748736 | bytes 737280 | tf_op jit(solution)/shard_map/pallas_call | solution.py:255
  (16 shorter events, 0.3 us)
Async XLA Ops:
  0.6 12.9 %copy-start = (bf16[16,9,512]{2,0,1:T(8,128)(2,1)S(1)}, bf16[16,9,512]{2,0,1:T(8,128)(2,1)}, u32[]{:S(2)}) copy-start(bf16[16,9,512]{2,0,1:T(8,128)(2,1)} %param.7) | copy-start | bytes 442372
  1.5 7.7 %collective-permute-start = (bf16[2,4,512]{2,1,0:T(4,128)(2,1)S(1)}, bf16[2,4,512]{2,1,0:T(4,128)(2,1)S(1)}, u32[]{:S(2)}, u32[]{:S(2)}) collective-permute-start(bf16[2,4,512]{2,1,0:T(4,128)(2,1)S(1)} %fusion.16), channel_id=1, source_target_pairs={{0,1},{1,0},{2,3},{3,2},{4,5},{5,4},{6,7},{7,6},{8,9},{9,8},{10,11... | collective-permute-start | bytes 24584 | tf_op jit(solution)/shard_map/ppermute | solution.py:278
  1.8 11.7 %collective-permute-start.1 = (bf16[9,16,512]{2,1,0:T(8,128)(2,1)}, bf16[9,16,512]{2,1,0:T(8,128)(2,1)S(1)}, u32[]{:S(2)}, u32[]{:S(2)}) collective-permute-start(bf16[9,16,512]{2,1,0:T(8,128)(2,1)} %bitcast.5), channel_id=1, source_target_pairs={{0,31},{1,30},{2,29},{3,28},{4,27},{5,26},{6,25},{7,24},{8,23},{9,... | collective-permute-start | bytes 442376 | tf_op jit(solution)/shard_map/ppermute | solution.py:55
  14.0 5.1 %collective-permute-start.2 = (bf16[32,2304]{1,0:T(8,128)(2,1)S(1)}, bf16[32,2304]{1,0:T(8,128)(2,1)S(1)}, u32[]{:S(2)}, u32[]{:S(2)}) collective-permute-start(bf16[32,2304]{1,0:T(8,128)(2,1)S(1)} %shard_map.61), channel_id=1, source_target_pairs={{0,1},{1,0},{2,6},{3,7},{4,5},{5,4},{6,2},{7,3},{8,9},{9,8},{10,14... | collective-permute-start | bytes 442376 | tf_op jit(solution)/shard_map/ppermute | solution.py:46
  16.5 11.8 %collective-permute-start.11 = (bf16[128,2304]{1,0:T(8,128)(2,1)S(1)}, bf16[128,2304]{1,0:T(8,128)(2,1)S(1)}, u32[]{:S(2)}, u32[]{:S(2)}) collective-permute-start(bf16[128,2304]{1,0:T(8,128)(2,1)S(1)} %get-tuple-element.23), channel_id=1, source_target_pairs={{0,2},{1,3},{2,0},{3,1},{4,6},{5,7},{6,4},{7,5},{8,10},{9,11},{10,... | collective-permute-start | bytes 1769480 | tf_op jit(solution)/shard_map/ppermute | solution.py:46
  18.9 13.6 %collective-permute-start.10 = (bf16[128,2304]{1,0:T(8,128)(2,1)S(1)}, bf16[128,2304]{1,0:T(8,128)(2,1)S(1)}, u32[]{:S(2)}, u32[]{:S(2)}) collective-permute-start(bf16[128,2304]{1,0:T(8,128)(2,1)S(1)} %get-tuple-element.21), channel_id=1, source_target_pairs={{0,2},{1,3},{2,0},{3,1},{4,6},{5,7},{6,4},{7,5},{8,10},{9,11},{10,... | collective-permute-start | bytes 1769480 | tf_op jit(solution)/shard_map/ppermute | solution.py:46
  19.0 5.0 %collective-permute-start.3 = (bf16[32,2304]{1,0:T(8,128)(2,1)S(1)}, bf16[32,2304]{1,0:T(8,128)(2,1)S(1)}, u32[]{:S(2)}, u32[]{:S(2)}) collective-permute-start(bf16[32,2304]{1,0:T(8,128)(2,1)S(1)} %shard_map.61), channel_id=1, source_target_pairs={{0,8},{1,9},{2,10},{3,11},{4,12},{5,13},{6,14},{7,15},{8,0},{9,1},... | collective-permute-start | bytes 442376 | tf_op jit(solution)/shard_map/ppermute | solution.py:55
  19.1 8.1 %collective-permute-start.4 = (bf16[32,2304]{1,0:T(8,128)(2,1)S(1)}, bf16[32,2304]{1,0:T(8,128)(2,1)S(1)}, u32[]{:S(2)}, u32[]{:S(2)}) collective-permute-start(bf16[32,2304]{1,0:T(8,128)(2,1)S(1)} %collective-permute-done.2), channel_id=1, source_target_pairs={{0,8},{1,9},{2,10},{3,11},{4,12},{5,13},{6,14},{7,15},{8,0},{9,1},... | collective-permute-start | bytes 442376 | tf_op jit(solution)/shard_map/ppermute | solution.py:55
  20.6 9.6 %collective-permute-start.6 = (bf16[64,2304]{1,0:T(8,128)(2,1)S(1)}, bf16[64,2304]{1,0:T(8,128)(2,1)S(1)}, u32[]{:S(2)}, u32[]{:S(2)}) collective-permute-start(bf16[64,2304]{1,0:T(8,128)(2,1)S(1)} %pad_maximum_fusion.1), channel_id=1, source_target_pairs={{0,4},{1,5},{2,3},{3,2},{4,0},{5,1},{6,7},{7,6},{8,12},{9,13},{10,... | collective-permute-start | bytes 884744 | tf_op jit(solution)/shard_map/ppermute | solution.py:46
  27.2 13.6 %collective-permute-start.7 = (bf16[64,2304]{1,0:T(8,128)(2,1)S(1)}, bf16[64,2304]{1,0:T(8,128)(2,1)S(1)}, u32[]{:S(2)}, u32[]{:S(2)}) collective-permute-start(bf16[64,2304]{1,0:T(8,128)(2,1)S(1)} %pad_maximum_fusion.2), channel_id=1, source_target_pairs={{0,4},{1,5},{2,3},{3,2},{4,0},{5,1},{6,7},{7,6},{8,12},{9,13},{10,... | collective-permute-start | bytes 884744 | tf_op jit(solution)/shard_map/ppermute | solution.py:46
  28.5 14.3 %collective-permute-start.12 = (bf16[128,1792]{1,0:T(8,128)(2,1)S(1)}, bf16[128,1792]{1,0:T(8,128)(2,1)S(1)}, u32[]{:S(2)}, u32[]{:S(2)}) collective-permute-start(bf16[128,1792]{1,0:T(8,128)(2,1)S(1)} %add_convert_fusion), channel_id=1, source_target_pairs={{0,4},{1,5},{2,3},{3,2},{4,0},{5,1},{6,7},{7,6},{8,12},{9,13},{10,... | collective-permute-start | bytes 1376264 | tf_op jit(solution)/shard_map/ppermute | solution.py:46
  28.9 10.5 %collective-permute-start.15 = (bf16[128,512]{1,0:T(8,128)(2,1)S(1)}, bf16[128,512]{1,0:T(8,128)(2,1)S(1)}, u32[]{:S(2)}, u32[]{:S(2)}) collective-permute-start(bf16[128,512]{1,0:T(8,128)(2,1)S(1)} %add_convert_fusion.2), channel_id=1, source_target_pairs={{0,4},{1,5},{2,3},{3,2},{4,0},{5,1},{6,7},{7,6},{8,12},{9,13},{10,... | collective-permute-start | bytes 393224 | tf_op jit(solution)/shard_map/ppermute | solution.py:46
  30.1 26.5 %collective-permute-start.5 = (bf16[128,2304]{1,0:T(8,128)(2,1)S(1)}, bf16[128,2304]{1,0:T(8,128)(2,1)S(1)}, u32[]{:S(2)}, u32[]{:S(2)}) collective-permute-start(bf16[128,2304]{1,0:T(8,128)(2,1)S(1)} %pad_maximum_fusion.own_ref), channel_id=1, source_target_pairs={{0,2},{1,3},{2,0},{3,1},{4,6},{5,7},{6,4},{7,5},{8,10},{9,11},{10,... | collective-permute-start | bytes 1769480 | tf_op jit(solution)/shard_map/ppermute | solution.py:46
  32.5 26.4 %collective-permute-start.8 = (bf16[64,2304]{1,0:T(8,128)(2,1)S(1)}, bf16[64,2304]{1,0:T(8,128)(2,1)S(1)}, u32[]{:S(2)}, u32[]{:S(2)}) collective-permute-start(bf16[64,2304]{1,0:T(8,128)(2,1)S(1)} %collective-permute-done.6.refs_0_), channel_id=1, source_target_pairs={{0,2},{1,3},{2,0},{3,1},{4,6},{5,7},{6,4},{7,5},{8,10},{9,11},{10,... | collective-permute-start | bytes 884744 | tf_op jit(solution)/shard_map/ppermute | solution.py:46
  39.5 4.1 %collective-permute-start.16 = (bf16[64,512]{1,0:T(8,128)(2,1)S(1)}, bf16[64,512]{1,0:T(8,128)(2,1)S(1)}, u32[]{:S(2)}, u32[]{:S(2)}) collective-permute-start(bf16[64,512]{1,0:T(8,128)(2,1)S(1)} %add_convert_fusion.3), channel_id=1, source_target_pairs={{0,1},{1,0},{2,6},{3,7},{4,5},{5,4},{6,2},{7,3},{8,9},{9,8},{10,14... | collective-permute-start | bytes 196616 | tf_op jit(solution)/shard_map/ppermute | solution.py:46
  40.8 18.1 %collective-permute-start.9 = (bf16[64,2304]{1,0:T(8,128)(2,1)S(1)}, bf16[64,2304]{1,0:T(8,128)(2,1)S(1)}, u32[]{:S(2)}, u32[]{:S(2)}) collective-permute-start(bf16[64,2304]{1,0:T(8,128)(2,1)S(1)} %collective-permute-done.7.refs_1_), channel_id=1, source_target_pairs={{0,2},{1,3},{2,0},{3,1},{4,6},{5,7},{6,4},{7,5},{8,10},{9,11},{10,... | collective-permute-start | bytes 884744 | tf_op jit(solution)/shard_map/ppermute | solution.py:46
  42.8 5.2 %collective-permute-start.13 = (bf16[64,1792]{1,0:T(8,128)(2,1)S(1)}, bf16[64,1792]{1,0:T(8,128)(2,1)S(1)}, u32[]{:S(2)}, u32[]{:S(2)}) collective-permute-start(bf16[64,1792]{1,0:T(8,128)(2,1)S(1)} %add_convert_fusion.1), channel_id=1, source_target_pairs={{0,1},{1,0},{2,6},{3,7},{4,5},{5,4},{6,2},{7,3},{8,9},{9,8},{10,14... | collective-permute-start | bytes 688136 | tf_op jit(solution)/shard_map/ppermute | solution.py:46
  43.7 4.6 %collective-permute-start.17 = (bf16[32,512]{1,0:T(8,128)(2,1)S(1)}, bf16[32,512]{1,0:T(8,128)(2,1)S(1)}, u32[]{:S(2)}, u32[]{:S(2)}) collective-permute-start(bf16[32,512]{1,0:T(8,128)(2,1)S(1)} %slice.137), channel_id=1, source_target_pairs={{0,8},{1,9},{2,10},{3,11},{4,12},{5,13},{6,14},{7,15},{8,0},{9,1},... | collective-permute-start | bytes 98312 | tf_op jit(solution)/shard_map/ppermute | solution.py:55
  48.2 3.7 %collective-permute-start.14 = (bf16[32,1792]{1,0:T(8,128)(2,1)S(1)}, bf16[32,1792]{1,0:T(8,128)(2,1)S(1)}, u32[]{:S(2)}, u32[]{:S(2)}) collective-permute-start(bf16[32,1792]{1,0:T(8,128)(2,1)S(1)} %slice.136), channel_id=1, source_target_pairs={{0,8},{1,9},{2,10},{3,11},{4,12},{5,13},{6,14},{7,15},{8,0},{9,1},... | collective-permute-start | bytes 344072 | tf_op jit(solution)/shard_map/ppermute | solution.py:55
  51.9 12.3 %collective-permute-start.18 = (bf16[32,2304]{1,0:T(8,128)(2,1)S(1)}, bf16[32,2304]{1,0:T(8,128)(2,1)S(1)}, u32[]{:S(2)}, u32[]{:S(2)}) collective-permute-start(bf16[32,2304]{1,0:T(8,128)(2,1)S(1)} %pad_maximum_fusion.3), channel_id=1, source_target_pairs={{0,31},{1,30},{2,29},{3,28},{4,27},{5,26},{6,25},{7,24},{8,23},{9,... | collective-permute-start | bytes 442376 | tf_op jit(solution)/shard_map/ppermute | solution.py:55
